TPU v7x, 512 devices: a whole 4x4x16 slice. The times are simulated.
512 devices in a mesh: gx: 32 (over z, core), gy: 16 (over y, x).
Axes of the slice: x: 4, y: 4, z: 16, core: 2. Of those that a mesh axis runs over, the one named last changes fastest.
Arguments:
- density: float32 [4096, 32, 4096], P('gx', None, 'gy'), may hold values from -5 to 5
- absorb: float32 [32, 4096], P(None, 'gy'), as said below
Outputs:
- radiance: float32 [3, 32, 4096], P(None, 'gx', 'gy')
- transmit: float32 [32, 4096], P('gx', 'gy')
Inputs may be any that keep to these rules, and one draw needn't show every extreme that they name: `absorb`: each ray's coefficient lies between 0.5 / 4096 and 0.05.
All inputs are finite; a program needn't handle non-finite values.
Results may differ from a plain program's by a relative error of at most 0.0003.
Values sent between devices are 32-bit elements; how exact they have to be, the bound alone decides.
A program may use at most 64 MiB of HBM per device.

v0:
```python
import jax
import jax.numpy as jnp
from jax import lax
from jax.sharding import PartitionSpec as P

SLOPES = (2.0, -1.5, 0.8)
OFFSETS = (0.0, 0.5, -0.3)


def extended(value, sides, width):
    for axis, dim in sides:
        size, length = (lax.axis_size(axis), value.shape[dim])
        up = [(i, (i + 1) % size) for i in range(size - 1)]
        down = [(j, i) for i, j in up]
        last = lax.slice_in_dim(value, length - width, length, axis=dim)
        first = lax.slice_in_dim(value, 0, width, axis=dim)
        before = lax.ppermute(last, axis, up)
        after = lax.ppermute(first, axis, down)
        value = jnp.concatenate([before, value, after], axis=dim)
    return value


def entering(value, axis, combine, identity):
    size, index = (lax.axis_size(axis), lax.axis_index(axis))
    everything = lax.all_gather(value, axis)
    start = jnp.broadcast_to(jnp.asarray(identity, value.dtype), value.shape)

    def step(k, before):
        reached = k < index
        new = combine(before, everything[k])
        return jnp.where(reached, new, before)

    return lax.fori_loop(0, size, step, start)


def add_depth(earlier, later):
    return earlier + later


def local(density, absorb):
    padded = extended(density, (("gx", 0), ("gy", 2)), 1)
    step_depth = (padded[2:, :, 1:-1] - padded[:-2, :, 1:-1]) * 0.5
    step_col = (padded[1:-1, :, 2:] - padded[1:-1, :, :-2]) * 0.5
    row_padded = jnp.pad(density, ((0, 0), (1, 1), (0, 0)))
    step_row = (row_padded[:, 2:] - row_padded[:, :-2]) * 0.5
    facing = 0.48 * step_depth + 0.64 * step_row + 0.6 * step_col
    length = jnp.sqrt(step_depth * step_depth + step_row * step_row + step_col * step_col + 1.0)
    lighting = 0.25 + 0.75 * jnp.maximum(facing, 0.0) / length
    extinct = absorb[None] * jax.nn.softplus(density)
    depth_count = density.shape[0]
    depth_index = jnp.arange(depth_count)
    below_mask = (depth_index[:, None] > depth_index[None, :]).astype(jnp.float32)
    prefix = jnp.dot(
        below_mask, extinct.reshape(depth_count, -1), precision=lax.Precision.HIGHEST
    ).reshape(extinct.shape)
    weight = jnp.exp(-prefix) * (1.0 - jnp.exp(-extinct)) * lighting
    local_colour = jnp.stack(
        [
            jnp.sum(weight * jax.nn.sigmoid(slope * density + offset), 0)
            for slope, offset in zip(SLOPES, OFFSETS)
        ]
    )
    optical = jnp.sum(extinct, 0)
    front = entering(optical, "gx", add_depth, jnp.zeros_like(optical))
    scaled = local_colour * jnp.exp(-front)[None]
    colour, total = (
        lax.psum_scatter(scaled, "gx", scatter_dimension=1, tiled=True),
        lax.psum_scatter(optical, "gx", scatter_dimension=0, tiled=True),
    )
    return (colour, jnp.exp(-total))


def solution(mesh):
    placed = (P("gx", None, "gy"), P(None, "gy"))
    return jax.shard_map(
        local,
        mesh=mesh,
        in_specs=placed,
        out_specs=(P(None, "gx", "gy"), P("gx", "gy")),
        check_vma=False,
    )
```

profile of v0, /device:TPU:7, one launch (start us, length us, event | category | flops | bytes accessed | tf_op | source)
XLA Modules:
  0.0 402.3 jit_solution(17270710376603911423)
XLA Ops:
  7.2 0.8 fusion.13
  8.0 2.6 collective-permute-start
  10.7 3.4 collective-permute-start.1
  14.1 8.1 %fusion.1 = (f32[128,32,256]{2,0,1:T(8,128)}, f32[128,32,256]{2,0,1:T(8,128)S(1)}) fusion(f32[32,256]{1,0:T(8,128)} %param.5, f32[128,32,256]{2,1,0:T(8,128)} %param.4), kind=kLoop, calls=%fused_computation.6 | loop fusion | flops 7340032 | bytes 12615680 | tf_op jit(solution)/shard_map/mul | solution.py:49
  22.6 1.5 copy-done
  24.1 2.1 fusion.12
  26.2 2.8 copy.45
  29.1 2.5 collective-permute-start.2
  31.5 1.2 copy.47
  32.7 5.1 %collective-permute-start.3 = (f32[130,32,1]{0,1,2:T(8,128)S(1)}, f32[130,32,1]{0,1,2:T(8,128)S(1)}, u32[]{:S(2)}, u32[]{:S(2)}) collective-permute-start(f32[130,32,1]{0,1,2:T(8,128)S(1)} %copy.47), channel_id=1, source_target_pairs={{0,1},{1,2},{2,3},{3,4},{4,5},{5,6},{6,7},{7,8},{8,9},{9,10},{10,1... | collective-permute-start | bytes 49928 | tf_op jit(solution)/shard_map/ppermute | solution.py:17
  37.8 5.6 %copy.38 = f32[128,32,256]{0,2,1:T(8,128)} copy(f32[128,32,256]{2,0,1:T(8,128)} %get-tuple-element.113) | data formatting | bytes 8388608 | tf_op jit(solution)/shard_map/mul | solution.py:49
  44.2 2.1 copy.48
  46.3 28.2 %multiply_reduce_fusion.2 = (f32[32,256]{1,0:T(8,128)S(1)}, f32[32,256]{1,0:T(8,128)S(1)}, f32[32,256]{1,0:T(8,128)S(1)}, f32[32,256]{1,0:T(8,128)}) fusion(f32[128,32,256]{2,1,0:T(8,128)} %param.4, f32[32,256]{1,0:T(8,128)S(1)} %copy-done.1, f32[1,32,256]{2,0,1:T(1,128)S(1)} %collective-permute-done, f32[128,32,256]{2,0,1:T(8,128)} %copy-done, ...), kind=kOutput, calls=%fused_computation.21 | convolution fusion | flops 1682948096 | bytes 12845568 | tf_op jit(solution)/shard_map/dot_general | solution.py:53
  74.6 1.3 dynamic-slice
  76.0 95.6 %all-reduce.2 = f32[32,256]{1,0:T(8,128)S(1)} all-reduce(f32[32,256]{1,0:T(8,128)} %get-tuple-element.102), channel_id=4, replica_groups=mesh['gx'=32,'gy'=16] {'gx'}, use_global_device_ids=true, to_apply=%region_7.8.clone | all-reduce | flops 8192 | bytes 65536
  171.6 24.5 %while.14 = (s32[]{:T(128)}, f32[32,256]{1,0:T(8,128)S(1)}, s32[]{:T(128)}, f32[32,32,256]{2,1,0:T(8,128)}, s32[]{:T(128)}, /*index=5*/s32[]{:T(128)}) while((s32[]{:T(128)}, f32[32,256]{1,0:T(8,128)S(1)}, s32[]{:T(128)}, f32[32,32,256]{2,1,0:T(8,128)}, s32[]{:T(128)}, /*index=5*/s32[]{:T(128)}) %tuple.50), condition=%wide.region_5.6_spmd.clone, body=%wide.region_4.5_spmd.clone.sunk | while | flops 24580 | bytes 98397 | solution.py:33
  171.6 0.8 add_select_fusion.2
  172.3 0.8 add_select_fusion.2
  173.1 0.8 add_select_fusion.2
  173.9 0.8 add_select_fusion.2
  176.9 0.8 add_select_fusion.2
  177.7 0.8 add_select_fusion.2
  178.5 0.8 add_select_fusion.2
  179.2 0.8 add_select_fusion.2
  182.3 0.8 add_select_fusion.2
  183.0 0.8 add_select_fusion.2
  183.8 0.8 add_select_fusion.2
  186.9 0.8 add_select_fusion.2
  187.6 0.8 add_select_fusion.2
  196.8 1.3 fusion.11
  198.1 195.4 %all-reduce.5.cloned.1.call-done = f32[3,32,256]{2,0,1:T(4,128)} async-done(((f32[3,32,256]{2,0,1:T(4,128)}), f32[3,32,256]{2,0,1:T(4,128)}) %all-reduce.5.cloned.1.call-update) | async-done | bytes 98320
  393.5 1.4 constant_dynamic-slice_fusion
  (42 shorter events, 17.3 us)
Async XLA Ops:
  7.2 164.4 %all-gather.3.cloned.1.call-start = ((), (), s32[]{:S(2)}) async-start(), calls=%async_computation | async-start | bytes 1081344 | tf_op jit(solution)/shard_map/all_gather | solution.py:25
  8.0 14.2 %collective-permute-start = (f32[1,32,256]{2,0,1:T(1,128)S(1)}, f32[1,32,256]{2,0,1:T(1,128)S(1)}, u32[]{:S(2)}, u32[]{:S(2)}) collective-permute-start(f32[1,32,256]{2,0,1:T(1,128)S(1)} %copy.39), channel_id=1, source_target_pairs={{16,0},{32,16},{48,32},{64,48},{80,64},{96,80},{112,96},{128,112},... | collective-permute-start | bytes 98312 | tf_op jit(solution)/shard_map/ppermute | solution.py:18
  10.7 11.5 %collective-permute-start.1 = (f32[1,32,256]{2,0,1:T(1,128)S(1)}, f32[1,32,256]{2,0,1:T(1,128)S(1)}, u32[]{:S(2)}, u32[]{:S(2)}) collective-permute-start(f32[1,32,256]{2,0,1:T(1,128)S(1)} %copy.41), channel_id=1, source_target_pairs={{0,16},{16,32},{32,48},{48,64},{64,80},{80,96},{96,112},{112,128},... | collective-permute-start | bytes 98312 | tf_op jit(solution)/shard_map/ppermute | solution.py:17
  22.2 1.9 copy-start
  29.1 14.4 %collective-permute-start.2 = (f32[130,32,1]{0,1,2:T(8,128)S(1)}, f32[130,32,1]{0,1,2:T(8,128)S(1)}, u32[]{:S(2)}, u32[]{:S(2)}) collective-permute-start(f32[130,32,1]{0,1,2:T(8,128)S(1)} %copy.45), channel_id=1, source_target_pairs={{1,0},{2,1},{3,2},{4,3},{5,4},{6,5},{7,6},{8,7},{9,8},{10,9},{11,1... | collective-permute-start | bytes 49928 | tf_op jit(solution)/shard_map/ppermute | solution.py:18
  32.7 11.4 %collective-permute-start.3 = (f32[130,32,1]{0,1,2:T(8,128)S(1)}, f32[130,32,1]{0,1,2:T(8,128)S(1)}, u32[]{:S(2)}, u32[]{:S(2)}) collective-permute-start(f32[130,32,1]{0,1,2:T(8,128)S(1)} %copy.47), channel_id=1, source_target_pairs={{0,1},{1,2},{2,3},{3,4},{4,5},{5,6},{6,7},{7,8},{8,9},{9,10},{10,1... | collective-permute-start | bytes 49928 | tf_op jit(solution)/shard_map/ppermute | solution.py:17
  43.4 2.9 copy-start.1
  74.5 319.0 %all-reduce.5.cloned.1.call-start = ((), (), s32[]{:S(2)}) async-start(), calls=%async_computation.1 | async-start | bytes 262144
Sparse Core Ops, SparseCore 0:
  74.6 74.2 all-gather.2
  197.0 196.4 all-reduce.4
where the time goes:
time: 406 us; the launch traced here: 402 us
  waiting for transfers between devices  195 us (48%)
  blocking collectives  95.6 us (24%)
  other arithmetic  35 us (9%)
  matrix products  28.2 us (7%)
  local copies, waits for them, and re-layouts  20.3 us (5%)
  between operations  14.1 us (3%)
  starting transfers between devices  13.7 us (3%)
    unnamed x3, waiting for transfers between devices  195 us
    unnamed x1, blocking collectives  95.6 us
    dot_general x1, matrix products, local(): jnp.dot(below_mask, extinct.reshape(depth_count, -1), precision=lax.Preci...  28.2 us
    select_n x32, other arithmetic, step(): return jnp.where(reached, new, before)  24.5 us
    ppermute x2, starting transfers between devices, extended(): before = lax.ppermute(last, axis, up)  8.56 us
  transfers between devices with their start and end apart: 6, of which 1 were waited for; matrix products, arithmetic and copies ran while one was open for 5% of the time, Pallas kernels for 0%

commit v1 on v0

--- a/solution.py
+++ b/solution.py
@@ -18,23 +18,6 @@
         after = lax.ppermute(first, axis, down)
         value = jnp.concatenate([before, value, after], axis=dim)
     return value
-
-
-def entering(value, axis, combine, identity):
-    size, index = (lax.axis_size(axis), lax.axis_index(axis))
-    everything = lax.all_gather(value, axis)
-    start = jnp.broadcast_to(jnp.asarray(identity, value.dtype), value.shape)
-
-    def step(k, before):
-        reached = k < index
-        new = combine(before, everything[k])
-        return jnp.where(reached, new, before)
-
-    return lax.fori_loop(0, size, step, start)
-
-
-def add_depth(earlier, later):
-    return earlier + later
 
 
 def local(density, absorb):
@@ -61,12 +44,14 @@
         ]
     )
     optical = jnp.sum(extinct, 0)
-    front = entering(optical, "gx", add_depth, jnp.zeros_like(optical))
-    scaled = local_colour * jnp.exp(-front)[None]
-    colour, total = (
-        lax.psum_scatter(scaled, "gx", scatter_dimension=1, tiled=True),
-        lax.psum_scatter(optical, "gx", scatter_dimension=0, tiled=True),
-    )
+    stacked = jnp.concatenate([local_colour, optical[None]], axis=0)
+    gathered = lax.all_to_all(stacked, "gx", 1, 1, tiled=True)
+    bricks = gathered.shape[1]
+    brick_index = jnp.arange(bricks)
+    before_mask = (brick_index[:, None] > brick_index[None, :]).astype(jnp.float32)
+    front = jnp.dot(before_mask, gathered[3], precision=lax.Precision.HIGHEST)
+    colour = jnp.sum(gathered[:3] * jnp.exp(-front)[None], axis=1, keepdims=True)
+    total = jnp.sum(gathered[3], axis=0, keepdims=True)
     return (colour, jnp.exp(-total))
 
 

time: 406 us -> 101 us (0.25)
  waiting for transfers between devices: 195 us -> 0.01 us
  blocking collectives: 95.6 us -> 30.5 us
  other arithmetic: 35 us -> 9.32 us
  between operations: 14.1 us -> 0.76 us
    unnamed x3 -> x0, waiting for transfers between devices: 195 us -> none
    unnamed x1 -> x0, blocking collectives: 95.6 us -> none
    all_to_all x0 -> x1, blocking collectives: none -> 30.5 us  [local(): gathered = lax.all_to_all(stacked, 'gx', 1, 1, tiled=True)]
    select_n x32 -> x0, other arithmetic: 24.5 us -> none  [step(): return jnp.where(reached, new, before)]
  transfers between devices with their start and end apart: 6 -> 4, of which waited for: 1 -> 0; matrix products, arithmetic and copies ran while one was open for 5% -> 16% of each run, Pallas kernels for 0% -> 0%
where the time goes in v1:
time: 101 us; the launch traced here: 99.5 us
  blocking collectives  30.5 us (30%)
  matrix products  27.7 us (27%)
  local copies, waits for them, and re-layouts  17.6 us (17%)
  starting transfers between devices  13.6 us (13%)
  other arithmetic  9.32 us (9%)
    all_to_all x1, blocking collectives, local(): gathered = lax.all_to_all(stacked, 'gx', 1, 1, tiled=True)  30.5 us
    dot_general x1, matrix products, local(): jnp.dot(below_mask, extinct.reshape(depth_count, -1), precision=lax.Preci...  27.6 us
    ppermute x2, starting transfers between devices, extended(): before = lax.ppermute(last, axis, up)  8.56 us
    mul x1, other arithmetic, local(): extinct = absorb[None] * jax.nn.softplus(density)  8.07 us
    mul x1, local copies, waits for them, and re-layouts, local(): extinct = absorb[None] * jax.nn.softplus(density)  5.57 us
    ppermute x2, starting transfers between devices, extended(): after = lax.ppermute(first, axis, down)  5.04 us
    slice x3, local copies, waits for them, and re-layouts, extended(): first = lax.slice_in_dim(value, 0, width, axis=dim)  4.97 us
    ppermute x1, local copies, waits for them, and re-layouts, extended(): before = lax.ppermute(last, axis, up)  2.11 us
  transfers between devices with their start and end apart: 4, of which 0 were waited for; matrix products, arithmetic and copies ran while one was open for 16% of the time, Pallas kernels for 0%

profile of v1, /device:TPU:7, one launch (start us, length us, event | category | flops | bytes accessed | tf_op | source)
XLA Modules:
  0.0 99.5 jit_solution(1654332509225769698)
XLA Ops:
  0.6 0.8 fusion.16
  1.5 2.6 %collective-permute-start = (f32[1,32,256]{2,0,1:T(1,128)S(1)}, f32[1,32,256]{2,0,1:T(1,128)S(1)}, u32[]{:S(2)}, u32[]{:S(2)}) collective-permute-start(f32[1,32,256]{2,0,1:T(1,128)S(1)} %copy.39), channel_id=1, source_target_pairs={{16,0},{32,16},{48,32},{64,48},{80,64},{96,80},{112,96},{128,112},... | collective-permute-start | bytes 98312 | tf_op jit(solution)/shard_map/ppermute | solution.py:18
  4.1 3.4 %collective-permute-start.1 = (f32[1,32,256]{2,0,1:T(1,128)S(1)}, f32[1,32,256]{2,0,1:T(1,128)S(1)}, u32[]{:S(2)}, u32[]{:S(2)}) collective-permute-start(f32[1,32,256]{2,0,1:T(1,128)S(1)} %copy.41), channel_id=1, source_target_pairs={{0,16},{16,32},{32,48},{48,64},{64,80},{80,96},{96,112},{112,128},... | collective-permute-start | bytes 98312 | tf_op jit(solution)/shard_map/ppermute | solution.py:17
  7.5 8.1 %fusion.1 = (f32[128,32,256]{2,0,1:T(8,128)}, f32[128,32,256]{2,0,1:T(8,128)S(1)}) fusion(f32[32,256]{1,0:T(8,128)} %param.3, f32[128,32,256]{2,1,0:T(8,128)} %param.2), kind=kLoop, calls=%fused_computation.5 | loop fusion | flops 7340032 | bytes 12615680 | tf_op jit(solution)/shard_map/mul | solution.py:32
  15.6 0.0 copy-start
  15.6 0.0 collective-permute-done
  15.6 0.0 collective-permute-done.1
  15.6 0.4 pad_maximum_fusion
  16.0 1.5 %copy-done = f32[128,32,256]{2,0,1:T(8,128)} copy-done((f32[128,32,256]{2,0,1:T(8,128)}, f32[128,32,256]{2,0,1:T(8,128)S(1)}, u32[]{:S(2)}) %copy-start) | copy-done | bytes 4194328
  17.5 2.1 %fusion.15 = (f32[130,32,1]{2,0,1:T(8,128)}, f32[130,32,1]{2,0,1:T(8,128)S(1)}) fusion(f32[130,32,256]{2,0,1:T(8,128)S(1)} %pad_maximum_fusion), kind=kLoop, calls=%fused_computation.35 | loop fusion | bytes 66560 | tf_op jit(solution)/shard_map/slice | solution.py:16
  19.7 2.8 %copy.45 = f32[130,32,1]{0,1,2:T(8,128)S(1)} copy(f32[130,32,1]{2,0,1:T(8,128)} %get-tuple-element.6) | data formatting | bytes 33280 | tf_op jit(solution)/shard_map/slice | solution.py:16
  22.5 2.5 %collective-permute-start.2 = (f32[130,32,1]{0,1,2:T(8,128)S(1)}, f32[130,32,1]{0,1,2:T(8,128)S(1)}, u32[]{:S(2)}, u32[]{:S(2)}) collective-permute-start(f32[130,32,1]{0,1,2:T(8,128)S(1)} %copy.45), channel_id=1, source_target_pairs={{1,0},{2,1},{3,2},{4,3},{5,4},{6,5},{7,6},{8,7},{9,8},{10,9},{11,1... | collective-permute-start | bytes 49928 | tf_op jit(solution)/shard_map/ppermute | solution.py:18
  24.9 1.2 %copy.47 = f32[130,32,1]{0,1,2:T(8,128)S(1)} copy(f32[130,32,1]{2,0,1:T(8,128)S(1)} %get-tuple-element.7) | data formatting | bytes 33280 | tf_op jit(solution)/shard_map/slice | solution.py:15
  26.1 5.1 %collective-permute-start.3 = (f32[130,32,1]{0,1,2:T(8,128)S(1)}, f32[130,32,1]{0,1,2:T(8,128)S(1)}, u32[]{:S(2)}, u32[]{:S(2)}) collective-permute-start(f32[130,32,1]{0,1,2:T(8,128)S(1)} %copy.47), channel_id=1, source_target_pairs={{0,1},{1,2},{2,3},{3,4},{4,5},{5,6},{6,7},{7,8},{8,9},{9,10},{10,1... | collective-permute-start | bytes 49928 | tf_op jit(solution)/shard_map/ppermute | solution.py:17
  31.3 5.6 %copy.38 = f32[128,32,256]{0,2,1:T(8,128)} copy(f32[128,32,256]{2,0,1:T(8,128)} %get-tuple-element.8) | data formatting | bytes 8388608 | tf_op jit(solution)/shard_map/mul | solution.py:32
  36.8 0.0 copy-start.1
  36.8 0.0 collective-permute-done.2
  36.8 0.7 copy.46
  37.6 0.0 collective-permute-done.3
  37.6 2.1 %copy.48 = f32[130,32,1]{2,0,1:T(8,128)} copy(f32[130,32,1]{0,1,2:T(8,128)S(1)} %collective-permute-done.3) | data formatting | bytes 33280 | tf_op jit(solution)/shard_map/ppermute | solution.py:17
  39.7 0.0 copy-done.1
  39.7 27.6 %multiply_reduce_fusion.2 = (f32[32,256]{1,0:T(8,128)S(1)}, f32[32,256]{1,0:T(8,128)S(1)}, f32[32,256]{1,0:T(8,128)S(1)}, f32[32,256]{1,0:T(8,128)S(1)}) fusion(f32[128,32,256]{2,1,0:T(8,128)} %param.2, f32[32,256]{1,0:T(8,128)S(1)} %copy-done.1, f32[1,32,256]{2,0,1:T(1,128)S(1)} %collective-permute-done, f32[128,32,256]{2,0,1:T(8,128)} %copy-done, ...), kind=kOutput, calls=%fused_computation.20 | convolution fusion | flops 1682948096 | bytes 12845568 | tf_op jit(solution)/shard_map/dot_general | solution.py:36
  67.4 0.1 pad_maximum_fusion.9
  67.6 30.5 %all_to_all.5 = f32[4,32,256]{2,0,1:T(4,128)S(1)} all-to-all(f32[4,32,256]{2,0,1:T(4,128)S(1)} %pad_maximum_fusion.9), channel_id=1, replica_groups=mesh['gx'=32,'gy'=16] {'gx'}, dimensions={1} | all-to-all | bytes 262144 | tf_op jit(solution)/shard_map/all_to_all | solution.py:48
  98.1 0.1 slice_reduce_fusion
  98.2 0.6 negate_exponential_fusion
  98.8 0.1 fusion.9
  98.9 0.1 fusion.10
  99.0 0.6 broadcast_in_dim.5
  (6 shorter events, 0.2 us)
Async XLA Ops:
  1.5 14.2 %collective-permute-start = (f32[1,32,256]{2,0,1:T(1,128)S(1)}, f32[1,32,256]{2,0,1:T(1,128)S(1)}, u32[]{:S(2)}, u32[]{:S(2)}) collective-permute-start(f32[1,32,256]{2,0,1:T(1,128)S(1)} %copy.39), channel_id=1, source_target_pairs={{16,0},{32,16},{48,32},{64,48},{80,64},{96,80},{112,96},{128,112},... | collective-permute-start | bytes 98312 | tf_op jit(solution)/shard_map/ppermute | solution.py:18
  4.1 11.5 %collective-permute-start.1 = (f32[1,32,256]{2,0,1:T(1,128)S(1)}, f32[1,32,256]{2,0,1:T(1,128)S(1)}, u32[]{:S(2)}, u32[]{:S(2)}) collective-permute-start(f32[1,32,256]{2,0,1:T(1,128)S(1)} %copy.41), channel_id=1, source_target_pairs={{0,16},{16,32},{32,48},{48,64},{64,80},{80,96},{96,112},{112,128},... | collective-permute-start | bytes 98312 | tf_op jit(solution)/shard_map/ppermute | solution.py:17
  15.6 1.9 %copy-start = (f32[128,32,256]{2,0,1:T(8,128)}, f32[128,32,256]{2,0,1:T(8,128)S(1)}, u32[]{:S(2)}) copy-start(f32[128,32,256]{2,0,1:T(8,128)S(1)} %get-tuple-element.9) | copy-start | bytes 12582916
  22.5 14.4 %collective-permute-start.2 = (f32[130,32,1]{0,1,2:T(8,128)S(1)}, f32[130,32,1]{0,1,2:T(8,128)S(1)}, u32[]{:S(2)}, u32[]{:S(2)}) collective-permute-start(f32[130,32,1]{0,1,2:T(8,128)S(1)} %copy.45), channel_id=1, source_target_pairs={{1,0},{2,1},{3,2},{4,3},{5,4},{6,5},{7,6},{8,7},{9,8},{10,9},{11,1... | collective-permute-start | bytes 49928 | tf_op jit(solution)/shard_map/ppermute | solution.py:18
  26.1 11.4 %collective-permute-start.3 = (f32[130,32,1]{0,1,2:T(8,128)S(1)}, f32[130,32,1]{0,1,2:T(8,128)S(1)}, u32[]{:S(2)}, u32[]{:S(2)}) collective-permute-start(f32[130,32,1]{0,1,2:T(8,128)S(1)} %copy.47), channel_id=1, source_target_pairs={{0,1},{1,2},{2,3},{3,4},{4,5},{5,6},{6,7},{7,8},{8,9},{9,10},{10,1... | collective-permute-start | bytes 49928 | tf_op jit(solution)/shard_map/ppermute | solution.py:17
  36.8 2.9 %copy-start.1 = (f32[32,256]{1,0:T(8,128)S(1)}, f32[32,256]{1,0:T(8,128)}, u32[]{:S(2)}) copy-start(f32[32,256]{1,0:T(8,128)} %param.3) | copy-start | bytes 98308

commit v2 on v1

--- a/solution.py
+++ b/solution.py
@@ -1,10 +1,15 @@
+import functools
+
 import jax
 import jax.numpy as jnp
 from jax import lax
+from jax.experimental import pallas as pl
+from jax.experimental.pallas import tpu as pltpu
 from jax.sharding import PartitionSpec as P
 
 SLOPES = (2.0, -1.5, 0.8)
 OFFSETS = (0.0, 0.5, -0.3)
+MESH_ID = pl.DeviceIdType.MESH
 
 
 def extended(value, sides, width):
@@ -18,6 +23,91 @@
         after = lax.ppermute(first, axis, down)
         value = jnp.concatenate([before, value, after], axis=dim)
     return value
+
+
+def combine_kernel(n, rows, stacked_ref, colour_ref, transmit_ref, recv, send_sems, recv_sems, local_sem):
+    me = lax.axis_index("gx")
+    col = lax.axis_index("gy")
+
+    def peer_of(i):
+        return lax.rem(me + i, n)
+
+    def link(peer, slot):
+        return pltpu.make_async_remote_copy(
+            src_ref=stacked_ref.at[peer],
+            dst_ref=recv.at[slot],
+            send_sem=send_sems.at[peer],
+            recv_sem=recv_sems.at[slot],
+            device_id=(peer, col),
+            device_id_type=MESH_ID,
+        )
+
+    barrier = pltpu.get_barrier_semaphore()
+
+    def greet(i, carry):
+        pl.semaphore_signal(barrier, inc=1, device_id=(peer_of(i), col), device_id_type=MESH_ID)
+        return carry
+
+    lax.fori_loop(1, n, greet, 0)
+    pl.semaphore_wait(barrier, n - 1)
+
+    def send(i, carry):
+        link(peer_of(i), me).start()
+        return carry
+
+    lax.fori_loop(1, n, send, 0)
+    own = pltpu.make_async_copy(stacked_ref.at[me], recv.at[me], local_sem)
+    own.start()
+    own.wait()
+
+    def finish(i, carry):
+        peer = peer_of(i)
+        link(peer, peer).wait_send()
+        link(peer, peer).wait_recv()
+        return carry
+
+    lax.fori_loop(1, n, finish, 0)
+
+    cols = recv.shape[-1]
+    zero = jnp.zeros((rows, cols), jnp.float32)
+
+    def accumulate(d, carry):
+        front, c0, c1, c2 = carry
+        block = recv[d]
+        seen = jnp.exp(-front)
+        return (
+            front + block[:, 3, :],
+            c0 + block[:, 0, :] * seen,
+            c1 + block[:, 1, :] * seen,
+            c2 + block[:, 2, :] * seen,
+        )
+
+    front, c0, c1, c2 = lax.fori_loop(0, n, accumulate, (zero, zero, zero, zero))
+    colour_ref[0] = c0
+    colour_ref[1] = c1
+    colour_ref[2] = c2
+    transmit_ref[...] = jnp.exp(-front)
+
+
+def combine(stacked, n):
+    rows, cols = stacked.shape[1], stacked.shape[3]
+    vmem = pltpu.MemorySpace.VMEM
+    return pl.pallas_call(
+        functools.partial(combine_kernel, n, rows),
+        out_shape=(
+            jax.ShapeDtypeStruct((3, rows, cols), jnp.float32),
+            jax.ShapeDtypeStruct((rows, cols), jnp.float32),
+        ),
+        in_specs=[pl.BlockSpec(memory_space=vmem)],
+        out_specs=(pl.BlockSpec(memory_space=vmem), pl.BlockSpec(memory_space=vmem)),
+        scratch_shapes=[
+            pltpu.VMEM(stacked.shape, jnp.float32),
+            pltpu.SemaphoreType.DMA((n,)),
+            pltpu.SemaphoreType.DMA((n,)),
+            pltpu.SemaphoreType.DMA,
+        ],
+        compiler_params=pltpu.CompilerParams(collective_id=0, has_side_effects=True),
+    )(stacked)
 
 
 def local(density, absorb):
@@ -37,22 +127,15 @@
         below_mask, extinct.reshape(depth_count, -1), precision=lax.Precision.HIGHEST
     ).reshape(extinct.shape)
     weight = jnp.exp(-prefix) * (1.0 - jnp.exp(-extinct)) * lighting
-    local_colour = jnp.stack(
-        [
-            jnp.sum(weight * jax.nn.sigmoid(slope * density + offset), 0)
-            for slope, offset in zip(SLOPES, OFFSETS)
-        ]
-    )
-    optical = jnp.sum(extinct, 0)
-    stacked = jnp.concatenate([local_colour, optical[None]], axis=0)
-    gathered = lax.all_to_all(stacked, "gx", 1, 1, tiled=True)
-    bricks = gathered.shape[1]
-    brick_index = jnp.arange(bricks)
-    before_mask = (brick_index[:, None] > brick_index[None, :]).astype(jnp.float32)
-    front = jnp.dot(before_mask, gathered[3], precision=lax.Precision.HIGHEST)
-    colour = jnp.sum(gathered[:3] * jnp.exp(-front)[None], axis=1, keepdims=True)
-    total = jnp.sum(gathered[3], axis=0, keepdims=True)
-    return (colour, jnp.exp(-total))
+    parts = [
+        jnp.sum(weight * jax.nn.sigmoid(slope * density + offset), 0)
+        for slope, offset in zip(SLOPES, OFFSETS)
+    ]
+    parts.append(jnp.sum(extinct, 0))
+    n = lax.axis_size("gx")
+    nz, cols = absorb.shape
+    stacked = jnp.stack(parts, axis=1).reshape(n, nz // n, 4, cols)
+    return combine(stacked, n)
 
 
 def solution(mesh):

time: 101 us -> 96.7 us (0.957)
  blocking collectives: 30.5 us -> 0 us
  Pallas kernels: 0 us -> 25.6 us
  local copies, waits for them, and re-layouts: 17.6 us -> 19.5 us
    all_to_all x1 -> x0, blocking collectives: 30.5 us -> none  [local(): gathered = lax.all_to_all(stacked, 'gx', 1, 1, tiled=True)]
    pallas_call x0 -> x1, Pallas kernels: none -> 25.6 us  [combine(): pl.pallas_call(functools.partial(combine_kernel, n, rows), out_shape=(jax...]
    unnamed x4 -> x6, local copies, waits for them, and re-layouts: 1.5 us -> 3.98 us
where the time goes in v2:
time: 96.7 us; the launch traced here: 96.2 us
  matrix products  27.6 us (29%)
  Pallas kernels  25.6 us (26%)
  local copies, waits for them, and re-layouts  19.5 us (20%)
  starting transfers between devices  13.6 us (14%)
  other arithmetic  9.25 us (10%)
    dot_general x1, matrix products, local(): jnp.dot(below_mask, extinct.reshape(depth_count, -1), precision=lax.Preci...  27.6 us
    pallas_call x1, Pallas kernels, combine(): pl.pallas_call(functools.partial(combine_kernel, n, rows), out_shape=(jax...  25.6 us
    ppermute x2, starting transfers between devices, extended(): before = lax.ppermute(last, axis, up)  8.56 us
    mul x1, other arithmetic, local(): extinct = absorb[None] * jax.nn.softplus(density)  8.07 us
    mul x1, local copies, waits for them, and re-layouts, local(): extinct = absorb[None] * jax.nn.softplus(density)  5.57 us
    ppermute x2, starting transfers between devices, extended(): after = lax.ppermute(first, axis, down)  5.04 us
    slice x3, local copies, waits for them, and re-layouts, extended(): first = lax.slice_in_dim(value, 0, width, axis=dim)  4.97 us
    unnamed x6, local copies, waits for them, and re-layouts  3.98 us
  transfers between devices with their start and end apart: 4, of which 0 were waited for; matrix products, arithmetic and copies ran while one was open for 16% of the time, Pallas kernels for 0%

profile of v2, /device:TPU:7, one launch (start us, length us, event | category | flops | bytes accessed | tf_op | source)
XLA Modules:
  0.0 96.2 jit_solution(17248635959335140242)
XLA Ops:
  0.6 0.8 fusion.12
  1.5 2.6 %collective-permute-start = (f32[1,32,256]{2,0,1:T(1,128)S(1)}, f32[1,32,256]{2,0,1:T(1,128)S(1)}, u32[]{:S(2)}, u32[]{:S(2)}) collective-permute-start(f32[1,32,256]{2,0,1:T(1,128)S(1)} %copy.39), channel_id=1, source_target_pairs={{16,0},{32,16},{48,32},{64,48},{80,64},{96,80},{112,96},{128,112},... | collective-permute-start | bytes 98312 | tf_op jit(solution)/shard_map/ppermute | solution.py:23
  4.1 3.4 %collective-permute-start.1 = (f32[1,32,256]{2,0,1:T(1,128)S(1)}, f32[1,32,256]{2,0,1:T(1,128)S(1)}, u32[]{:S(2)}, u32[]{:S(2)}) collective-permute-start(f32[1,32,256]{2,0,1:T(1,128)S(1)} %copy.41), channel_id=1, source_target_pairs={{0,16},{16,32},{32,48},{48,64},{64,80},{80,96},{96,112},{112,128},... | collective-permute-start | bytes 98312 | tf_op jit(solution)/shard_map/ppermute | solution.py:22
  7.5 8.1 %fusion.1 = (f32[128,32,256]{2,0,1:T(8,128)}, f32[128,32,256]{2,0,1:T(8,128)S(1)}) fusion(f32[32,256]{1,0:T(8,128)} %param.3, f32[128,32,256]{2,1,0:T(8,128)} %param.2), kind=kLoop, calls=%fused_computation.5 | loop fusion | flops 7340032 | bytes 12615680 | tf_op jit(solution)/shard_map/mul | solution.py:122
  15.6 0.0 copy-start
  15.6 0.0 collective-permute-done
  15.6 0.0 collective-permute-done.1
  15.6 0.4 pad_maximum_fusion
  16.0 1.5 %copy-done = f32[128,32,256]{2,0,1:T(8,128)} copy-done((f32[128,32,256]{2,0,1:T(8,128)}, f32[128,32,256]{2,0,1:T(8,128)S(1)}, u32[]{:S(2)}) %copy-start) | copy-done | bytes 4194328
  17.5 2.1 %fusion.11 = (f32[130,32,1]{2,0,1:T(8,128)}, f32[130,32,1]{2,0,1:T(8,128)S(1)}) fusion(f32[130,32,256]{2,0,1:T(8,128)S(1)} %pad_maximum_fusion), kind=kLoop, calls=%fused_computation.26 | loop fusion | bytes 66560 | tf_op jit(solution)/shard_map/slice | solution.py:21
  19.7 2.8 %copy.45 = f32[130,32,1]{0,1,2:T(8,128)S(1)} copy(f32[130,32,1]{2,0,1:T(8,128)} %get-tuple-element.6) | data formatting | bytes 33280 | tf_op jit(solution)/shard_map/slice | solution.py:21
  22.5 2.5 %collective-permute-start.2 = (f32[130,32,1]{0,1,2:T(8,128)S(1)}, f32[130,32,1]{0,1,2:T(8,128)S(1)}, u32[]{:S(2)}, u32[]{:S(2)}) collective-permute-start(f32[130,32,1]{0,1,2:T(8,128)S(1)} %copy.45), channel_id=1, source_target_pairs={{1,0},{2,1},{3,2},{4,3},{5,4},{6,5},{7,6},{8,7},{9,8},{10,9},{11,1... | collective-permute-start | bytes 49928 | tf_op jit(solution)/shard_map/ppermute | solution.py:23
  24.9 1.2 %copy.47 = f32[130,32,1]{0,1,2:T(8,128)S(1)} copy(f32[130,32,1]{2,0,1:T(8,128)S(1)} %get-tuple-element.7) | data formatting | bytes 33280 | tf_op jit(solution)/shard_map/slice | solution.py:20
  26.1 5.1 %collective-permute-start.3 = (f32[130,32,1]{0,1,2:T(8,128)S(1)}, f32[130,32,1]{0,1,2:T(8,128)S(1)}, u32[]{:S(2)}, u32[]{:S(2)}) collective-permute-start(f32[130,32,1]{0,1,2:T(8,128)S(1)} %copy.47), channel_id=1, source_target_pairs={{0,1},{1,2},{2,3},{3,4},{4,5},{5,6},{6,7},{7,8},{8,9},{9,10},{10,1... | collective-permute-start | bytes 49928 | tf_op jit(solution)/shard_map/ppermute | solution.py:22
  31.3 5.6 %copy.38 = f32[128,32,256]{0,2,1:T(8,128)} copy(f32[128,32,256]{2,0,1:T(8,128)} %get-tuple-element.8) | data formatting | bytes 8388608 | tf_op jit(solution)/shard_map/mul | solution.py:122
  36.8 0.0 copy-start.1
  36.8 0.0 collective-permute-done.2
  36.8 0.7 copy.46
  37.6 0.0 collective-permute-done.3
  37.6 2.1 %copy.48 = f32[130,32,1]{2,0,1:T(8,128)} copy(f32[130,32,1]{0,1,2:T(8,128)S(1)} %collective-permute-done.3) | data formatting | bytes 33280 | tf_op jit(solution)/shard_map/ppermute | solution.py:22
  39.7 0.0 copy-done.1
  39.7 27.6 %multiply_reduce_fusion.2 = (f32[32,256]{1,0:T(8,128)S(1)}, f32[32,256]{1,0:T(8,128)S(1)}, f32[32,256]{1,0:T(8,128)S(1)}, f32[32,256]{1,0:T(8,128)S(1)}) fusion(f32[128,32,256]{2,1,0:T(8,128)} %param.2, f32[32,256]{1,0:T(8,128)S(1)} %copy-done.1, f32[1,32,256]{2,0,1:T(1,128)S(1)} %collective-permute-done, f32[128,32,256]{2,0,1:T(8,128)} %copy-done, ...), kind=kOutput, calls=%fused_computation.20 | convolution fusion | flops 1682948096 | bytes 12845568 | tf_op jit(solution)/shard_map/dot_general | solution.py:126
  67.4 0.8 maximum_bitcast_fusion.stacked_ref
  68.2 25.6 %shard_map.41 = (f32[3,1,256]{2,1,0:T(1,128)}, f32[1,256]{1,0:T(1,128)}) custom-call(f32[32,1,4,256]{3,2,1,0:T(4,128)} %maximum_bitcast_fusion.stacked_ref), custom_call_target="tpu_custom_call" | custom-call | tf_op jit(solution)/shard_map/pallas_call | solution.py:95
  93.8 1.3 %copy.60 = f32[3,1,256]{2,1,0:T(1,128)} copy(f32[3,1,256]{2,1,0:T(1,128)} %get-tuple-element.14) | data formatting | bytes 6144
  95.0 1.2 %copy.61 = f32[1,256]{1,0:T(1,128)} copy(f32[1,256]{1,0:T(1,128)} %get-tuple-element.15) | data formatting | bytes 2048
  (6 shorter events, 0.2 us)
Async XLA Ops:
  1.5 14.2 %collective-permute-start = (f32[1,32,256]{2,0,1:T(1,128)S(1)}, f32[1,32,256]{2,0,1:T(1,128)S(1)}, u32[]{:S(2)}, u32[]{:S(2)}) collective-permute-start(f32[1,32,256]{2,0,1:T(1,128)S(1)} %copy.39), channel_id=1, source_target_pairs={{16,0},{32,16},{48,32},{64,48},{80,64},{96,80},{112,96},{128,112},... | collective-permute-start | bytes 98312 | tf_op jit(solution)/shard_map/ppermute | solution.py:23
  4.1 11.5 %collective-permute-start.1 = (f32[1,32,256]{2,0,1:T(1,128)S(1)}, f32[1,32,256]{2,0,1:T(1,128)S(1)}, u32[]{:S(2)}, u32[]{:S(2)}) collective-permute-start(f32[1,32,256]{2,0,1:T(1,128)S(1)} %copy.41), channel_id=1, source_target_pairs={{0,16},{16,32},{32,48},{48,64},{64,80},{80,96},{96,112},{112,128},... | collective-permute-start | bytes 98312 | tf_op jit(solution)/shard_map/ppermute | solution.py:22
  15.6 1.9 %copy-start = (f32[128,32,256]{2,0,1:T(8,128)}, f32[128,32,256]{2,0,1:T(8,128)S(1)}, u32[]{:S(2)}) copy-start(f32[128,32,256]{2,0,1:T(8,128)S(1)} %get-tuple-element.9) | copy-start | bytes 12582916
  22.5 14.4 %collective-permute-start.2 = (f32[130,32,1]{0,1,2:T(8,128)S(1)}, f32[130,32,1]{0,1,2:T(8,128)S(1)}, u32[]{:S(2)}, u32[]{:S(2)}) collective-permute-start(f32[130,32,1]{0,1,2:T(8,128)S(1)} %copy.45), channel_id=1, source_target_pairs={{1,0},{2,1},{3,2},{4,3},{5,4},{6,5},{7,6},{8,7},{9,8},{10,9},{11,1... | collective-permute-start | bytes 49928 | tf_op jit(solution)/shard_map/ppermute | solution.py:23
  26.1 11.4 %collective-permute-start.3 = (f32[130,32,1]{0,1,2:T(8,128)S(1)}, f32[130,32,1]{0,1,2:T(8,128)S(1)}, u32[]{:S(2)}, u32[]{:S(2)}) collective-permute-start(f32[130,32,1]{0,1,2:T(8,128)S(1)} %copy.47), channel_id=1, source_target_pairs={{0,1},{1,2},{2,3},{3,4},{4,5},{5,6},{6,7},{7,8},{8,9},{9,10},{10,1... | collective-permute-start | bytes 49928 | tf_op jit(solution)/shard_map/ppermute | solution.py:22
  36.8 2.9 %copy-start.1 = (f32[32,256]{1,0:T(8,128)S(1)}, f32[32,256]{1,0:T(8,128)}, u32[]{:S(2)}) copy-start(f32[32,256]{1,0:T(8,128)} %param.3) | copy-start | bytes 98308

commit v3 on v2

--- a/solution.py
+++ b/solution.py
@@ -68,29 +68,34 @@
 
     lax.fori_loop(1, n, finish, 0)
 
-    cols = recv.shape[-1]
-    zero = jnp.zeros((rows, cols), jnp.float32)
+    cols = colour_ref.shape[-1]
+    span = cols // 128
+    zero = jnp.zeros((rows * span, 128), jnp.float32)
+
+    def value(block, k):
+        pieces = [block[(r * 4 + k) * span:(r * 4 + k + 1) * span] for r in range(rows)]
+        return pieces[0] if rows == 1 else jnp.concatenate(pieces, axis=0)
 
     def accumulate(d, carry):
         front, c0, c1, c2 = carry
         block = recv[d]
         seen = jnp.exp(-front)
         return (
-            front + block[:, 3, :],
-            c0 + block[:, 0, :] * seen,
-            c1 + block[:, 1, :] * seen,
-            c2 + block[:, 2, :] * seen,
+            front + value(block, 3),
+            c0 + value(block, 0) * seen,
+            c1 + value(block, 1) * seen,
+            c2 + value(block, 2) * seen,
         )
 
     front, c0, c1, c2 = lax.fori_loop(0, n, accumulate, (zero, zero, zero, zero))
-    colour_ref[0] = c0
-    colour_ref[1] = c1
-    colour_ref[2] = c2
-    transmit_ref[...] = jnp.exp(-front)
+    for k, c in enumerate((c0, c1, c2)):
+        colour_ref[k] = c.reshape(rows, cols)
+    transmit_ref[...] = jnp.exp(-front).reshape(rows, cols)
 
 
 def combine(stacked, n):
     rows, cols = stacked.shape[1], stacked.shape[3]
+    stacked = stacked.reshape(n, rows * 4 * cols // 128, 128)
     vmem = pltpu.MemorySpace.VMEM
     return pl.pallas_call(
         functools.partial(combine_kernel, n, rows),

time: 96.7 us -> 96.8 us (level)
  no operation moved by 1% of the time
where the time goes in v3:
time: 96.8 us; the launch traced here: 96.3 us
  matrix products  27.6 us (29%)
  Pallas kernels  25.6 us (26%)
  local copies, waits for them, and re-layouts  20.2 us (21%)
  starting transfers between devices  13.6 us (14%)
  other arithmetic  8.61 us (9%)
    dot_general x1, matrix products, local(): jnp.dot(below_mask, extinct.reshape(depth_count, -1), precision=lax.Preci...  27.6 us
    pallas_call x1, Pallas kernels, combine(): pl.pallas_call(functools.partial(combine_kernel, n, rows), out_shape=(jax...  25.6 us
    ppermute x2, starting transfers between devices, extended(): before = lax.ppermute(last, axis, up)  8.56 us
    mul x1, other arithmetic, local(): extinct = absorb[None] * jax.nn.softplus(density)  8.07 us
    mul x1, local copies, waits for them, and re-layouts, local(): extinct = absorb[None] * jax.nn.softplus(density)  5.57 us
    ppermute x2, starting transfers between devices, extended(): after = lax.ppermute(first, axis, down)  5.04 us
    slice x3, local copies, waits for them, and re-layouts, extended(): first = lax.slice_in_dim(value, 0, width, axis=dim)  4.97 us
    unnamed x6, local copies, waits for them, and re-layouts  3.98 us
  transfers between devices with their start and end apart: 4, of which 0 were waited for; matrix products, arithmetic and copies ran while one was open for 16% of the time, Pallas kernels for 0%

profile of v3, /device:TPU:7, one launch (start us, length us, event | category | flops | bytes accessed | tf_op | source)
XLA Modules:
  0.0 96.3 jit_solution(1511184777897702497)
XLA Ops:
  0.6 0.8 fusion.12
  1.5 2.6 %collective-permute-start = (f32[1,32,256]{2,0,1:T(1,128)S(1)}, f32[1,32,256]{2,0,1:T(1,128)S(1)}, u32[]{:S(2)}, u32[]{:S(2)}) collective-permute-start(f32[1,32,256]{2,0,1:T(1,128)S(1)} %copy.39), channel_id=1, source_target_pairs={{16,0},{32,16},{48,32},{64,48},{80,64},{96,80},{112,96},{128,112},... | collective-permute-start | bytes 98312 | tf_op jit(solution)/shard_map/ppermute | solution.py:23
  4.1 3.4 %collective-permute-start.1 = (f32[1,32,256]{2,0,1:T(1,128)S(1)}, f32[1,32,256]{2,0,1:T(1,128)S(1)}, u32[]{:S(2)}, u32[]{:S(2)}) collective-permute-start(f32[1,32,256]{2,0,1:T(1,128)S(1)} %copy.41), channel_id=1, source_target_pairs={{0,16},{16,32},{32,48},{48,64},{64,80},{80,96},{96,112},{112,128},... | collective-permute-start | bytes 98312 | tf_op jit(solution)/shard_map/ppermute | solution.py:22
  7.5 8.1 %fusion.1 = (f32[128,32,256]{2,0,1:T(8,128)}, f32[128,32,256]{2,0,1:T(8,128)S(1)}) fusion(f32[32,256]{1,0:T(8,128)} %param.3, f32[128,32,256]{2,1,0:T(8,128)} %param.2), kind=kLoop, calls=%fused_computation.5 | loop fusion | flops 7340032 | bytes 12615680 | tf_op jit(solution)/shard_map/mul | solution.py:127
  15.6 0.0 copy-start
  15.6 0.0 collective-permute-done
  15.6 0.0 collective-permute-done.1
  15.6 0.4 pad_maximum_fusion
  16.0 1.5 %copy-done = f32[128,32,256]{2,0,1:T(8,128)} copy-done((f32[128,32,256]{2,0,1:T(8,128)}, f32[128,32,256]{2,0,1:T(8,128)S(1)}, u32[]{:S(2)}) %copy-start) | copy-done | bytes 4194328
  17.5 2.1 %fusion.11 = (f32[130,32,1]{2,0,1:T(8,128)}, f32[130,32,1]{2,0,1:T(8,128)S(1)}) fusion(f32[130,32,256]{2,0,1:T(8,128)S(1)} %pad_maximum_fusion), kind=kLoop, calls=%fused_computation.26 | loop fusion | bytes 66560 | tf_op jit(solution)/shard_map/slice | solution.py:21
  19.7 2.8 %copy.45 = f32[130,32,1]{0,1,2:T(8,128)S(1)} copy(f32[130,32,1]{2,0,1:T(8,128)} %get-tuple-element.6) | data formatting | bytes 33280 | tf_op jit(solution)/shard_map/slice | solution.py:21
  22.5 2.5 %collective-permute-start.2 = (f32[130,32,1]{0,1,2:T(8,128)S(1)}, f32[130,32,1]{0,1,2:T(8,128)S(1)}, u32[]{:S(2)}, u32[]{:S(2)}) collective-permute-start(f32[130,32,1]{0,1,2:T(8,128)S(1)} %copy.45), channel_id=1, source_target_pairs={{1,0},{2,1},{3,2},{4,3},{5,4},{6,5},{7,6},{8,7},{9,8},{10,9},{11,1... | collective-permute-start | bytes 49928 | tf_op jit(solution)/shard_map/ppermute | solution.py:23
  24.9 1.2 %copy.47 = f32[130,32,1]{0,1,2:T(8,128)S(1)} copy(f32[130,32,1]{2,0,1:T(8,128)S(1)} %get-tuple-element.7) | data formatting | bytes 33280 | tf_op jit(solution)/shard_map/slice | solution.py:20
  26.1 5.1 %collective-permute-start.3 = (f32[130,32,1]{0,1,2:T(8,128)S(1)}, f32[130,32,1]{0,1,2:T(8,128)S(1)}, u32[]{:S(2)}, u32[]{:S(2)}) collective-permute-start(f32[130,32,1]{0,1,2:T(8,128)S(1)} %copy.47), channel_id=1, source_target_pairs={{0,1},{1,2},{2,3},{3,4},{4,5},{5,6},{6,7},{7,8},{8,9},{9,10},{10,1... | collective-permute-start | bytes 49928 | tf_op jit(solution)/shard_map/ppermute | solution.py:22
  31.3 5.6 %copy.38 = f32[128,32,256]{0,2,1:T(8,128)} copy(f32[128,32,256]{2,0,1:T(8,128)} %get-tuple-element.8) | data formatting | bytes 8388608 | tf_op jit(solution)/shard_map/mul | solution.py:127
  36.8 0.0 copy-start.1
  36.8 0.0 collective-permute-done.2
  36.8 0.7 copy.46
  37.6 0.0 collective-permute-done.3
  37.6 2.1 %copy.48 = f32[130,32,1]{2,0,1:T(8,128)} copy(f32[130,32,1]{0,1,2:T(8,128)S(1)} %collective-permute-done.3) | data formatting | bytes 33280 | tf_op jit(solution)/shard_map/ppermute | solution.py:22
  39.7 0.0 copy-done.1
  39.7 27.6 %multiply_reduce_fusion.2 = (f32[32,256]{1,0:T(8,128)S(1)}, f32[32,256]{1,0:T(8,128)S(1)}, f32[32,256]{1,0:T(8,128)S(1)}, f32[32,256]{1,0:T(8,128)S(1)}) fusion(f32[128,32,256]{2,1,0:T(8,128)} %param.2, f32[32,256]{1,0:T(8,128)S(1)} %copy-done.1, f32[1,32,256]{2,0,1:T(1,128)S(1)} %collective-permute-done, f32[128,32,256]{2,0,1:T(8,128)} %copy-done, ...), kind=kOutput, calls=%fused_computation.20 | convolution fusion | flops 1682948096 | bytes 12845568 | tf_op jit(solution)/shard_map/dot_general | solution.py:131
  67.4 0.1 pad_maximum_fusion.9
  67.6 0.7 reshape_reshape.3.stacked_ref
  68.3 25.6 %shard_map.41 = (f32[3,1,256]{2,1,0:T(1,128)}, f32[1,256]{1,0:T(1,128)}) custom-call(f32[32,8,128]{2,1,0:T(8,128)} %reshape_reshape.3.stacked_ref), custom_call_target="tpu_custom_call" | custom-call | tf_op jit(solution)/shard_map/pallas_call | solution.py:100
  93.8 1.3 %copy.60 = f32[3,1,256]{2,1,0:T(1,128)} copy(f32[3,1,256]{2,1,0:T(1,128)} %get-tuple-element.14) | data formatting | bytes 6144
  95.1 1.2 %copy.61 = f32[1,256]{1,0:T(1,128)} copy(f32[1,256]{1,0:T(1,128)} %get-tuple-element.15) | data formatting | bytes 2048
  (6 shorter events, 0.2 us)
Async XLA Ops:
  1.5 14.2 %collective-permute-start = (f32[1,32,256]{2,0,1:T(1,128)S(1)}, f32[1,32,256]{2,0,1:T(1,128)S(1)}, u32[]{:S(2)}, u32[]{:S(2)}) collective-permute-start(f32[1,32,256]{2,0,1:T(1,128)S(1)} %copy.39), channel_id=1, source_target_pairs={{16,0},{32,16},{48,32},{64,48},{80,64},{96,80},{112,96},{128,112},... | collective-permute-start | bytes 98312 | tf_op jit(solution)/shard_map/ppermute | solution.py:23
  4.1 11.5 %collective-permute-start.1 = (f32[1,32,256]{2,0,1:T(1,128)S(1)}, f32[1,32,256]{2,0,1:T(1,128)S(1)}, u32[]{:S(2)}, u32[]{:S(2)}) collective-permute-start(f32[1,32,256]{2,0,1:T(1,128)S(1)} %copy.41), channel_id=1, source_target_pairs={{0,16},{16,32},{32,48},{48,64},{64,80},{80,96},{96,112},{112,128},... | collective-permute-start | bytes 98312 | tf_op jit(solution)/shard_map/ppermute | solution.py:22
  15.6 1.9 %copy-start = (f32[128,32,256]{2,0,1:T(8,128)}, f32[128,32,256]{2,0,1:T(8,128)S(1)}, u32[]{:S(2)}) copy-start(f32[128,32,256]{2,0,1:T(8,128)S(1)} %get-tuple-element.9) | copy-start | bytes 12582916
  22.5 14.4 %collective-permute-start.2 = (f32[130,32,1]{0,1,2:T(8,128)S(1)}, f32[130,32,1]{0,1,2:T(8,128)S(1)}, u32[]{:S(2)}, u32[]{:S(2)}) collective-permute-start(f32[130,32,1]{0,1,2:T(8,128)S(1)} %copy.45), channel_id=1, source_target_pairs={{1,0},{2,1},{3,2},{4,3},{5,4},{6,5},{7,6},{8,7},{9,8},{10,9},{11,1... | collective-permute-start | bytes 49928 | tf_op jit(solution)/shard_map/ppermute | solution.py:23
  26.1 11.4 %collective-permute-start.3 = (f32[130,32,1]{0,1,2:T(8,128)S(1)}, f32[130,32,1]{0,1,2:T(8,128)S(1)}, u32[]{:S(2)}, u32[]{:S(2)}) collective-permute-start(f32[130,32,1]{0,1,2:T(8,128)S(1)} %copy.47), channel_id=1, source_target_pairs={{0,1},{1,2},{2,3},{3,4},{4,5},{5,6},{6,7},{7,8},{8,9},{9,10},{10,1... | collective-permute-start | bytes 49928 | tf_op jit(solution)/shard_map/ppermute | solution.py:22
  36.8 2.9 %copy-start.1 = (f32[32,256]{1,0:T(8,128)S(1)}, f32[32,256]{1,0:T(8,128)}, u32[]{:S(2)}) copy-start(f32[32,256]{1,0:T(8,128)} %param.3) | copy-start | bytes 98308

commit v4 on v3

--- a/solution.py
+++ b/solution.py
@@ -10,19 +10,6 @@
 SLOPES = (2.0, -1.5, 0.8)
 OFFSETS = (0.0, 0.5, -0.3)
 MESH_ID = pl.DeviceIdType.MESH
-
-
-def extended(value, sides, width):
-    for axis, dim in sides:
-        size, length = (lax.axis_size(axis), value.shape[dim])
-        up = [(i, (i + 1) % size) for i in range(size - 1)]
-        down = [(j, i) for i, j in up]
-        last = lax.slice_in_dim(value, length - width, length, axis=dim)
-        first = lax.slice_in_dim(value, 0, width, axis=dim)
-        before = lax.ppermute(last, axis, up)
-        after = lax.ppermute(first, axis, down)
-        value = jnp.concatenate([before, value, after], axis=dim)
-    return value
 
 
 def combine_kernel(n, rows, stacked_ref, colour_ref, transmit_ref, recv, send_sems, recv_sems, local_sem):
@@ -115,31 +102,99 @@
     )(stacked)
 
 
+def march_kernel(last, dens_ref, front_ref, back_ref, halo_ref, absorb_ref, out_ref):
+    rows, cols = dens_ref.shape[1], dens_ref.shape[2]
+    shape = (rows, 128)
+    lane = lax.broadcasted_iota(jnp.int32, shape, 1)
+    row = lax.broadcasted_iota(jnp.int32, shape, 0)
+    first_lane, last_lane = lane == 0, lane == 127
+    top_row, bottom_row = row == 0, row == rows - 1
+    halves = cols // 128
+    for h in range(halves):
+        lanes = slice(h * 128, (h + 1) * 128)
+        left_lanes = slice((h - 1) * 128, h * 128) if h > 0 else None
+        right_lanes = slice((h + 1) * 128, (h + 2) * 128) if h + 1 < halves else None
+        absorb = absorb_ref[:, lanes]
+
+        def plane(ref_plane):
+            return ref_plane[:, lanes]
+
+        def step(x, carry):
+            seen, c0, c1, c2, optical = carry
+            centre_plane = dens_ref.at[x]
+            d = centre_plane[:, lanes]
+            behind = jnp.where(x == 0, front_ref[:, lanes], dens_ref[jnp.maximum(x - 1, 0), :, lanes])
+            ahead = jnp.where(x == last, back_ref[:, lanes], dens_ref[jnp.minimum(x + 1, last), :, lanes])
+            halo = halo_ref[x]
+            from_left = pltpu.roll(d, 1, 1)
+            from_right = pltpu.roll(d, 127, 1)
+            if left_lanes is None:
+                edge_left = halo
+            else:
+                edge_left = pltpu.roll(centre_plane[:, left_lanes], 1, 1)
+            if right_lanes is None:
+                edge_right = halo
+            else:
+                edge_right = pltpu.roll(centre_plane[:, right_lanes], 127, 1)
+            left = jnp.where(first_lane, edge_left, from_left)
+            right = jnp.where(last_lane, edge_right, from_right)
+            above = jnp.where(top_row, 0.0, pltpu.roll(d, 1, 0))
+            below = jnp.where(bottom_row, 0.0, pltpu.roll(d, rows - 1, 0))
+            step_depth = (ahead - behind) * 0.5
+            step_row = (below - above) * 0.5
+            step_col = (right - left) * 0.5
+            facing = 0.48 * step_depth + 0.64 * step_row + 0.6 * step_col
+            length2 = step_depth * step_depth + step_row * step_row + step_col * step_col + 1.0
+            lighting = 0.25 + 0.75 * jnp.maximum(facing, 0.0) * lax.rsqrt(length2)
+            soft = jnp.maximum(d, 0.0) + jnp.log1p(jnp.exp(-jnp.abs(d)))
+            extinct = absorb * soft
+            passed = jnp.exp(-extinct)
+            weight = seen * (1.0 - passed) * lighting
+            tints = [1.0 / (1.0 + jnp.exp(-(slope * d + offset))) for slope, offset in zip(SLOPES, OFFSETS)]
+            return (
+                seen * passed,
+                c0 + weight * tints[0],
+                c1 + weight * tints[1],
+                c2 + weight * tints[2],
+                optical + extinct,
+            )
+
+        zero = jnp.zeros(shape, jnp.float32)
+        one = jnp.ones(shape, jnp.float32)
+        _, c0, c1, c2, optical = lax.fori_loop(0, last + 1, step, (one, zero, zero, zero, zero))
+        for k, value in enumerate((c0, c1, c2, optical)):
+            out_ref[k, :, lanes] = value
+
+
+def march(density, front, back, halo, absorb):
+    depth, rows, cols = density.shape
+    vmem = pltpu.MemorySpace.VMEM
+    return pl.pallas_call(
+        functools.partial(march_kernel, depth - 1),
+        out_shape=jax.ShapeDtypeStruct((4, rows, cols), jnp.float32),
+        in_specs=[pl.BlockSpec(memory_space=vmem)] * 5,
+        out_specs=pl.BlockSpec(memory_space=vmem),
+    )(density, front, back, halo, absorb)
+
+
+def shifted(value, axis, forward):
+    size = lax.axis_size(axis)
+    pairs = [(i, i + 1) for i in range(size - 1)]
+    if not forward:
+        pairs = [(j, i) for i, j in pairs]
+    return lax.ppermute(value, axis, pairs)
+
+
 def local(density, absorb):
-    padded = extended(density, (("gx", 0), ("gy", 2)), 1)
-    step_depth = (padded[2:, :, 1:-1] - padded[:-2, :, 1:-1]) * 0.5
-    step_col = (padded[1:-1, :, 2:] - padded[1:-1, :, :-2]) * 0.5
-    row_padded = jnp.pad(density, ((0, 0), (1, 1), (0, 0)))
-    step_row = (row_padded[:, 2:] - row_padded[:, :-2]) * 0.5
-    facing = 0.48 * step_depth + 0.64 * step_row + 0.6 * step_col
-    length = jnp.sqrt(step_depth * step_depth + step_row * step_row + step_col * step_col + 1.0)
-    lighting = 0.25 + 0.75 * jnp.maximum(facing, 0.0) / length
-    extinct = absorb[None] * jax.nn.softplus(density)
-    depth_count = density.shape[0]
-    depth_index = jnp.arange(depth_count)
-    below_mask = (depth_index[:, None] > depth_index[None, :]).astype(jnp.float32)
-    prefix = jnp.dot(
-        below_mask, extinct.reshape(depth_count, -1), precision=lax.Precision.HIGHEST
-    ).reshape(extinct.shape)
-    weight = jnp.exp(-prefix) * (1.0 - jnp.exp(-extinct)) * lighting
-    parts = [
-        jnp.sum(weight * jax.nn.sigmoid(slope * density + offset), 0)
-        for slope, offset in zip(SLOPES, OFFSETS)
-    ]
-    parts.append(jnp.sum(extinct, 0))
+    depth, nz, cols = density.shape
+    front = shifted(density[depth - 1], "gx", True)
+    back = shifted(density[0], "gx", False)
+    left = shifted(density[:, :, cols - 1:], "gy", True)
+    right = shifted(density[:, :, :1], "gy", False)
+    halo = jnp.concatenate([left, jnp.zeros((depth, nz, 126), jnp.float32), right], axis=2)
+    parts = march(density, front, back, halo, absorb)
     n = lax.axis_size("gx")
-    nz, cols = absorb.shape
-    stacked = jnp.stack(parts, axis=1).reshape(n, nz // n, 4, cols)
+    stacked = jnp.transpose(parts, (1, 0, 2)).reshape(n, nz // n, 4, cols)
     return combine(stacked, n)
 
 

time: 96.8 us -> 92.5 us (0.956)
  the two profiles are of different devices: /device:TPU:7 before, /device:TPU:25 now
where the time goes in v4:
time: 92.5 us; the launch traced here: 92.1 us
  Pallas kernels  54.7 us (59%)
  local copies, waits for them, and re-layouts  19.2 us (21%)
  starting transfers between devices  13.9 us (15%)
  other arithmetic  3.54 us (4%)
    pallas_call x1, Pallas kernels, march(): pl.pallas_call(functools.partial(march_kernel, depth - 1), out_shape=jax....  28.6 us
    pallas_call x1, Pallas kernels, combine(): pl.pallas_call(functools.partial(combine_kernel, n, rows), out_shape=(jax...  26.1 us
    ppermute x4, starting transfers between devices, shifted(): return lax.ppermute(value, axis, pairs)  13.9 us
    unnamed x8, local copies, waits for them, and re-layouts  7.64 us
    ppermute x2, local copies, waits for them, and re-layouts, shifted(): return lax.ppermute(value, axis, pairs)  4.72 us
    slice x1, local copies, waits for them, and re-layouts, local(): left = shifted(density[:, :, cols - 1:], 'gy', True)  4.27 us
    concatenate x1, other arithmetic, local(): jnp.concatenate([left, jnp.zeros((depth, nz, 126), jnp.float32), right],...  3.54 us
  transfers between devices with their start and end apart: 4, of which 0 were waited for; matrix products, arithmetic and copies ran while one was open for 11% of the time, Pallas kernels for 0%

profile of v4, /device:TPU:25, one launch (start us, length us, event | category | flops | bytes accessed | tf_op | source)
XLA Modules:
  0.0 92.1 jit_solution(15772986717004508250)
XLA Ops:
  0.6 4.3 %fusion = (f32[128,32,1]{2,1,0:T(8,128)}, f32[128,32,1]{2,1,0:T(8,128)S(1)}) fusion(f32[128,32,256]{2,1,0:T(8,128)} %dens_ref.1), kind=kLoop, calls=%fused_computation.3 | loop fusion | bytes 65536 | tf_op jit(solution)/shard_map/slice | solution.py:192
  4.9 2.7 %copy.10 = f32[128,32,1]{0,1,2:T(8,128)S(1)} copy(f32[128,32,1]{2,1,0:T(8,128)} %get-tuple-element.2) | data formatting | bytes 32768
  7.6 3.1 %collective-permute-start.2 = (f32[128,32,1]{0,1,2:T(8,128)S(1)}, f32[128,32,1]{0,1,2:T(8,128)S(1)}, u32[]{:S(2)}, u32[]{:S(2)}) collective-permute-start(f32[128,32,1]{0,1,2:T(8,128)S(1)} %copy.10), channel_id=1, source_target_pairs={{0,1},{1,2},{2,3},{3,4},{4,5},{5,6},{6,7},{7,8},{8,9},{9,10},{10,1... | collective-permute-start | bytes 49160 | tf_op jit(solution)/shard_map/ppermute | solution.py:185
  10.7 1.3 %copy.11 = f32[128,32,1]{0,1,2:T(8,128)S(1)} copy(f32[128,32,1]{2,1,0:T(8,128)S(1)} %get-tuple-element.3) | data formatting | bytes 32768
  12.0 4.3 %collective-permute-start.3 = (f32[128,32,1]{0,1,2:T(8,128)S(1)}, f32[128,32,1]{0,1,2:T(8,128)S(1)}, u32[]{:S(2)}, u32[]{:S(2)}) collective-permute-start(f32[128,32,1]{0,1,2:T(8,128)S(1)} %copy.11), channel_id=1, source_target_pairs={{1,0},{2,1},{3,2},{4,3},{5,4},{6,5},{7,6},{8,7},{9,8},{10,9},{11,1... | collective-permute-start | bytes 49160 | tf_op jit(solution)/shard_map/ppermute | solution.py:185
  16.3 0.8 slice_bitcast_fusion
  17.0 4.7 %collective-permute-start = (f32[32,256]{1,0:T(8,128)S(1)}, f32[32,256]{1,0:T(8,128)S(1)}, u32[]{:S(2)}, u32[]{:S(2)}) collective-permute-start(f32[32,256]{1,0:T(8,128)S(1)} %get-tuple-element.5), channel_id=1, source_target_pairs={{0,16},{16,32},{32,48},{48,64},{64,80},{80,96},{96,112},{112,128},... | collective-permute-start | bytes 98312 | tf_op jit(solution)/shard_map/ppermute | solution.py:185
  21.7 1.9 %collective-permute-start.1 = (f32[32,256]{1,0:T(8,128)S(1)}, f32[32,256]{1,0:T(8,128)S(1)}, u32[]{:S(2)}, u32[]{:S(2)}) collective-permute-start(f32[32,256]{1,0:T(8,128)S(1)} %get-tuple-element.4), channel_id=1, source_target_pairs={{16,0},{32,16},{48,32},{64,48},{80,64},{96,80},{112,96},{128,112},... | collective-permute-start | bytes 98312 | tf_op jit(solution)/shard_map/ppermute | solution.py:185
  23.6 0.1 pad.1.clone
  23.7 0.0 collective-permute-done.2
  23.7 1.9 %copy.7 = f32[128,32,1]{2,1,0:T(8,128)S(1)} copy(f32[128,32,1]{0,1,2:T(8,128)S(1)} %collective-permute-done.2) | data formatting | bytes 32768 | tf_op jit(solution)/shard_map/ppermute | solution.py:185
  25.6 0.0 collective-permute-done.3
  25.6 2.8 %copy.8 = f32[128,32,1]{2,1,0:T(8,128)} copy(f32[128,32,1]{0,1,2:T(8,128)S(1)} %collective-permute-done.3) | data formatting | bytes 32768 | tf_op jit(solution)/shard_map/ppermute | solution.py:185
  28.5 3.5 %pad_maximum_fusion.halo_ref = f32[128,32,128]{2,1,0:T(8,128)} fusion(f32[128,32,1]{2,1,0:T(8,128)} %copy.8, f32[128,32,1]{2,1,0:T(8,128)S(1)} %copy.7, f32[128]{0:T(128)S(1)} %pad.1.clone), kind=kLoop, calls=%fused_computation | loop fusion | flops 1048576 | bytes 2130432 | tf_op jit(solution)/shard_map/concatenate | solution.py:194
  32.0 0.0 collective-permute-done.front_ref
  32.0 0.0 copy-start
  32.0 0.0 collective-permute-done.1.back_ref
  32.0 0.6 copy-done
  32.6 0.0 copy-start.1
  32.6 0.6 copy-done.1
  33.2 28.6 %shard_map.41 = f32[4,32,256]{2,1,0:T(8,128)} custom-call(f32[128,32,256]{2,1,0:T(8,128)} %dens_ref.1, f32[32,256]{1,0:T(8,128)} %copy-done, f32[32,256]{1,0:T(8,128)} %copy-done.1, f32[128,32,128]{2,1,0:T(8,128)} %pad_maximum_fusion.halo_ref, f32[32,256]{1,0:T(8,128)} %absorb_ref.1), custom_call_target="tpu_custom_call" | custom-call | tf_op jit(solution)/shard_map/pallas_call | solution.py:172
  61.8 1.0 %copy.9 = f32[32,4,256]{2,1,0:T(4,128)S(1)} copy(f32[32,4,256]{2,0,1:T(8,128)} %bitcast.5) | data formatting | bytes 262144 | tf_op jit(solution)/shard_map/transpose | solution.py:197
  62.8 0.7 reshape_reshape.3.stacked_ref
  63.5 26.1 %shard_map.42 = (f32[3,1,256]{2,1,0:T(1,128)}, f32[1,256]{1,0:T(1,128)}) custom-call(f32[32,8,128]{2,1,0:T(8,128)} %reshape_reshape.3.stacked_ref), custom_call_target="tpu_custom_call" | custom-call | tf_op jit(solution)/shard_map/pallas_call | solution.py:87
  89.6 1.2 %copy.14 = f32[3,1,256]{2,1,0:T(1,128)} copy(f32[3,1,256]{2,1,0:T(1,128)} %get-tuple-element.8) | data formatting | bytes 6144
  90.9 1.2 %copy.15 = f32[1,256]{1,0:T(1,128)} copy(f32[1,256]{1,0:T(1,128)} %get-tuple-element.9) | data formatting | bytes 2048
  (1 shorter events, 0.0 us)
Async XLA Ops:
  7.6 16.2 %collective-permute-start.2 = (f32[128,32,1]{0,1,2:T(8,128)S(1)}, f32[128,32,1]{0,1,2:T(8,128)S(1)}, u32[]{:S(2)}, u32[]{:S(2)}) collective-permute-start(f32[128,32,1]{0,1,2:T(8,128)S(1)} %copy.10), channel_id=1, source_target_pairs={{0,1},{1,2},{2,3},{3,4},{4,5},{5,6},{6,7},{7,8},{8,9},{9,10},{10,1... | collective-permute-start | bytes 49160 | tf_op jit(solution)/shard_map/ppermute | solution.py:185
  12.0 13.6 %collective-permute-start.3 = (f32[128,32,1]{0,1,2:T(8,128)S(1)}, f32[128,32,1]{0,1,2:T(8,128)S(1)}, u32[]{:S(2)}, u32[]{:S(2)}) collective-permute-start(f32[128,32,1]{0,1,2:T(8,128)S(1)} %copy.11), channel_id=1, source_target_pairs={{1,0},{2,1},{3,2},{4,3},{5,4},{6,5},{7,6},{8,7},{9,8},{10,9},{11,1... | collective-permute-start | bytes 49160 | tf_op jit(solution)/shard_map/ppermute | solution.py:185
  17.0 15.0 %collective-permute-start = (f32[32,256]{1,0:T(8,128)S(1)}, f32[32,256]{1,0:T(8,128)S(1)}, u32[]{:S(2)}, u32[]{:S(2)}) collective-permute-start(f32[32,256]{1,0:T(8,128)S(1)} %get-tuple-element.5), channel_id=1, source_target_pairs={{0,16},{16,32},{32,48},{48,64},{64,80},{80,96},{96,112},{112,128},... | collective-permute-start | bytes 98312 | tf_op jit(solution)/shard_map/ppermute | solution.py:185
  21.7 10.3 %collective-permute-start.1 = (f32[32,256]{1,0:T(8,128)S(1)}, f32[32,256]{1,0:T(8,128)S(1)}, u32[]{:S(2)}, u32[]{:S(2)}) collective-permute-start(f32[32,256]{1,0:T(8,128)S(1)} %get-tuple-element.4), channel_id=1, source_target_pairs={{16,0},{32,16},{48,32},{64,48},{80,64},{96,80},{112,96},{128,112},... | collective-permute-start | bytes 98312 | tf_op jit(solution)/shard_map/ppermute | solution.py:185
  32.0 0.6 copy-start
  32.6 0.6 copy-start.1

commit v5 on v4

--- a/solution.py
+++ b/solution.py
@@ -102,7 +102,7 @@
     )(stacked)
 
 
-def march_kernel(last, dens_ref, front_ref, back_ref, halo_ref, absorb_ref, out_ref):
+def march_kernel(last, dens_ref, front_ref, back_ref, left_ref, right_ref, absorb_ref, out_ref):
     rows, cols = dens_ref.shape[1], dens_ref.shape[2]
     shape = (rows, 128)
     lane = lax.broadcasted_iota(jnp.int32, shape, 1)
@@ -125,15 +125,17 @@
             d = centre_plane[:, lanes]
             behind = jnp.where(x == 0, front_ref[:, lanes], dens_ref[jnp.maximum(x - 1, 0), :, lanes])
             ahead = jnp.where(x == last, back_ref[:, lanes], dens_ref[jnp.minimum(x + 1, last), :, lanes])
-            halo = halo_ref[x]
+            span = left_ref.shape[1]
+            halo_left = pltpu.roll(left_ref[...], lax.rem(span - x, span), 1)
+            halo_right = pltpu.roll(right_ref[...], lax.rem(span + 127 - x, span), 1)
             from_left = pltpu.roll(d, 1, 1)
             from_right = pltpu.roll(d, 127, 1)
             if left_lanes is None:
-                edge_left = halo
+                edge_left = halo_left
             else:
                 edge_left = pltpu.roll(centre_plane[:, left_lanes], 1, 1)
             if right_lanes is None:
-                edge_right = halo
+                edge_right = halo_right
             else:
                 edge_right = pltpu.roll(centre_plane[:, right_lanes], 127, 1)
             left = jnp.where(first_lane, edge_left, from_left)
@@ -166,15 +168,15 @@
             out_ref[k, :, lanes] = value
 
 
-def march(density, front, back, halo, absorb):
+def march(density, front, back, left, right, absorb):
     depth, rows, cols = density.shape
     vmem = pltpu.MemorySpace.VMEM
     return pl.pallas_call(
         functools.partial(march_kernel, depth - 1),
         out_shape=jax.ShapeDtypeStruct((4, rows, cols), jnp.float32),
-        in_specs=[pl.BlockSpec(memory_space=vmem)] * 5,
+        in_specs=[pl.BlockSpec(memory_space=vmem)] * 6,
         out_specs=pl.BlockSpec(memory_space=vmem),
-    )(density, front, back, halo, absorb)
+    )(density, front, back, left, right, absorb)
 
 
 def shifted(value, axis, forward):
@@ -189,10 +191,9 @@
     depth, nz, cols = density.shape
     front = shifted(density[depth - 1], "gx", True)
     back = shifted(density[0], "gx", False)
-    left = shifted(density[:, :, cols - 1:], "gy", True)
-    right = shifted(density[:, :, :1], "gy", False)
-    halo = jnp.concatenate([left, jnp.zeros((depth, nz, 126), jnp.float32), right], axis=2)
-    parts = march(density, front, back, halo, absorb)
+    left = shifted(jnp.transpose(density[:, :, cols - 1]), "gy", True)
+    right = shifted(jnp.transpose(density[:, :, 0]), "gy", False)
+    parts = march(density, front, back, left, right, absorb)
     n = lax.axis_size("gx")
     stacked = jnp.transpose(parts, (1, 0, 2)).reshape(n, nz // n, 4, cols)
     return combine(stacked, n)

time: 92.5 us -> 87.9 us (0.950)
  the two profiles are of different devices: /device:TPU:25 before, /device:TPU:7 now
where the time goes in v5:
time: 87.9 us; the launch traced here: 87.5 us
  Pallas kernels  56.7 us (65%)
  local copies, waits for them, and re-layouts  14.4 us (16%)
  starting transfers between devices  11.3 us (13%)
  waiting for transfers between devices  4.41 us (5%)
    pallas_call x1, Pallas kernels, march(): pl.pallas_call(functools.partial(march_kernel, depth - 1), out_shape=jax....  29.2 us
    pallas_call x1, Pallas kernels, combine(): pl.pallas_call(functools.partial(combine_kernel, n, rows), out_shape=(jax...  27.6 us
    ppermute x4, starting transfers between devices, shifted(): return lax.ppermute(value, axis, pairs)  11.3 us
    unnamed x12, local copies, waits for them, and re-layouts  7.67 us
    ppermute x4, waiting for transfers between devices, shifted(): return lax.ppermute(value, axis, pairs)  4.41 us
    slice x1, local copies, waits for them, and re-layouts, local(): right = shifted(jnp.transpose(density[:, :, 0]), 'gy', False)  4.26 us
  transfers between devices with their start and end apart: 4, of which 1 were waited for; matrix products, arithmetic and copies ran while one was open for 9% of the time, Pallas kernels for 0%

profile of v5, /device:TPU:7, one launch (start us, length us, event | category | flops | bytes accessed | tf_op | source)
XLA Modules:
  0.0 87.5 jit_solution(13838185644743683791)
XLA Ops:
  0.6 0.8 slice_bitcast_fusion
  1.4 4.1 %collective-permute-start = (f32[32,256]{1,0:T(8,128)S(1)}, f32[32,256]{1,0:T(8,128)S(1)}, u32[]{:S(2)}, u32[]{:S(2)}) collective-permute-start(f32[32,256]{1,0:T(8,128)S(1)} %get-tuple-element.5), channel_id=1, source_target_pairs={{0,16},{16,32},{32,48},{48,64},{64,80},{80,96},{96,112},{112,128},... | collective-permute-start | bytes 98312 | tf_op jit(solution)/shard_map/ppermute | solution.py:187
  5.5 1.9 %collective-permute-start.1 = (f32[32,256]{1,0:T(8,128)S(1)}, f32[32,256]{1,0:T(8,128)S(1)}, u32[]{:S(2)}, u32[]{:S(2)}) collective-permute-start(f32[32,256]{1,0:T(8,128)S(1)} %get-tuple-element.4), channel_id=1, source_target_pairs={{16,0},{32,16},{48,32},{64,48},{80,64},{96,80},{112,96},{128,112},... | collective-permute-start | bytes 98312 | tf_op jit(solution)/shard_map/ppermute | solution.py:187
  7.4 4.3 %fusion = (f32[128,32,1]{2,1,0:T(8,128)S(1)}, f32[128,32,1]{2,1,0:T(8,128)}) fusion(f32[128,32,256]{2,1,0:T(8,128)} %dens_ref.1), kind=kLoop, calls=%fused_computation.2 | loop fusion | bytes 65536 | tf_op jit(solution)/shard_map/slice | solution.py:195
  11.7 2.7 %copy.7 = f32[128,32,1]{0,1,2:T(8,128)S(1)} copy(f32[128,32,1]{2,1,0:T(8,128)} %get-tuple-element.3) | data formatting | bytes 32768
  14.4 3.1 %collective-permute-start.2 = (f32[32,128]{1,0:T(8,128)S(1)}, f32[32,128]{1,0:T(8,128)S(1)}, u32[]{:S(2)}, u32[]{:S(2)}) collective-permute-start(f32[32,128]{1,0:T(8,128)S(1)} %bitcast.12), channel_id=1, source_target_pairs={{0,1},{1,2},{2,3},{3,4},{4,5},{5,6},{6,7},{7,8},{8,9},{9,10},{10,1... | collective-permute-start | bytes 49160 | tf_op jit(solution)/shard_map/ppermute | solution.py:187
  17.5 1.3 %copy.8 = f32[128,32,1]{0,1,2:T(8,128)S(1)} copy(f32[128,32,1]{2,1,0:T(8,128)S(1)} %get-tuple-element.2) | data formatting | bytes 32768
  18.8 2.2 %collective-permute-start.3 = (f32[32,128]{1,0:T(8,128)S(1)}, f32[32,128]{1,0:T(8,128)S(1)}, u32[]{:S(2)}, u32[]{:S(2)}) collective-permute-start(f32[32,128]{1,0:T(8,128)S(1)} %bitcast.13), channel_id=1, source_target_pairs={{1,0},{2,1},{3,2},{4,3},{5,4},{6,5},{7,6},{8,7},{9,8},{10,9},{11,1... | collective-permute-start | bytes 49160 | tf_op jit(solution)/shard_map/ppermute | solution.py:187
  20.9 0.0 collective-permute-done.2.left_ref
  21.0 0.0 copy-start.2
  21.0 4.4 %collective-permute-done.3.right_ref = f32[32,128]{1,0:T(8,128)S(1)} collective-permute-done((f32[32,128]{1,0:T(8,128)S(1)}, f32[32,128]{1,0:T(8,128)S(1)}, u32[]{:S(2)}, u32[]{:S(2)}) %collective-permute-start.3) | collective-permute-done | bytes 16416 | tf_op jit(solution)/shard_map/ppermute | solution.py:187
  25.4 0.0 copy-start.3
  25.4 0.0 collective-permute-done.front_ref
  25.4 0.0 copy-start
  25.4 0.0 collective-permute-done.1.back_ref
  25.4 0.0 copy-done.2
  25.4 0.6 copy-done.3
  26.0 0.0 copy-done
  26.0 0.0 copy-start.1
  26.0 0.6 copy-done.1
  26.6 29.2 %shard_map.41 = f32[4,32,256]{2,1,0:T(8,128)} custom-call(f32[128,32,256]{2,1,0:T(8,128)} %dens_ref.1, f32[32,256]{1,0:T(8,128)} %copy-done, f32[32,256]{1,0:T(8,128)} %copy-done.1, f32[32,128]{1,0:T(8,128)} %copy-done.2, f32[32,128]{1,0:T(8,128)} %copy-done.3, f32[32,256]{1,0:T(8,128)} %absorb_ref.1), custom_call_target="tpu_custom_call" | custom-call | tf_op jit(solution)/shard_map/pallas_call | solution.py:174
  55.8 1.0 %copy.6 = f32[32,4,256]{2,1,0:T(4,128)S(1)} copy(f32[32,4,256]{2,0,1:T(8,128)} %bitcast.11) | data formatting | bytes 262144 | tf_op jit(solution)/shard_map/transpose | solution.py:198
  56.7 0.7 reshape_reshape.3.stacked_ref
  57.4 27.6 %shard_map.42 = (f32[3,1,256]{2,1,0:T(1,128)}, f32[1,256]{1,0:T(1,128)}) custom-call(f32[32,8,128]{2,1,0:T(8,128)} %reshape_reshape.3.stacked_ref), custom_call_target="tpu_custom_call" | custom-call | tf_op jit(solution)/shard_map/pallas_call | solution.py:87
  85.0 1.3 %copy.11 = f32[3,1,256]{2,1,0:T(1,128)} copy(f32[3,1,256]{2,1,0:T(1,128)} %get-tuple-element.8) | data formatting | bytes 6144
  86.3 1.2 %copy.12 = f32[1,256]{1,0:T(1,128)} copy(f32[1,256]{1,0:T(1,128)} %get-tuple-element.9) | data formatting | bytes 2048
Async XLA Ops:
  1.4 24.0 %collective-permute-start = (f32[32,256]{1,0:T(8,128)S(1)}, f32[32,256]{1,0:T(8,128)S(1)}, u32[]{:S(2)}, u32[]{:S(2)}) collective-permute-start(f32[32,256]{1,0:T(8,128)S(1)} %get-tuple-element.5), channel_id=1, source_target_pairs={{0,16},{16,32},{32,48},{48,64},{64,80},{80,96},{96,112},{112,128},... | collective-permute-start | bytes 98312 | tf_op jit(solution)/shard_map/ppermute | solution.py:187
  5.5 19.9 %collective-permute-start.1 = (f32[32,256]{1,0:T(8,128)S(1)}, f32[32,256]{1,0:T(8,128)S(1)}, u32[]{:S(2)}, u32[]{:S(2)}) collective-permute-start(f32[32,256]{1,0:T(8,128)S(1)} %get-tuple-element.4), channel_id=1, source_target_pairs={{16,0},{32,16},{48,32},{64,48},{80,64},{96,80},{112,96},{128,112},... | collective-permute-start | bytes 98312 | tf_op jit(solution)/shard_map/ppermute | solution.py:187
  14.4 6.6 %collective-permute-start.2 = (f32[32,128]{1,0:T(8,128)S(1)}, f32[32,128]{1,0:T(8,128)S(1)}, u32[]{:S(2)}, u32[]{:S(2)}) collective-permute-start(f32[32,128]{1,0:T(8,128)S(1)} %bitcast.12), channel_id=1, source_target_pairs={{0,1},{1,2},{2,3},{3,4},{4,5},{5,6},{6,7},{7,8},{8,9},{9,10},{10,1... | collective-permute-start | bytes 49160 | tf_op jit(solution)/shard_map/ppermute | solution.py:187
  18.8 6.6 %collective-permute-start.3 = (f32[32,128]{1,0:T(8,128)S(1)}, f32[32,128]{1,0:T(8,128)S(1)}, u32[]{:S(2)}, u32[]{:S(2)}) collective-permute-start(f32[32,128]{1,0:T(8,128)S(1)} %bitcast.13), channel_id=1, source_target_pairs={{1,0},{2,1},{3,2},{4,3},{5,4},{6,5},{7,6},{8,7},{9,8},{10,9},{11,1... | collective-permute-start | bytes 49160 | tf_op jit(solution)/shard_map/ppermute | solution.py:187
  21.0 4.4 %copy-start.2 = (f32[32,128]{1,0:T(8,128)}, f32[32,128]{1,0:T(8,128)S(1)}, u32[]{:S(2)}) copy-start(f32[32,128]{1,0:T(8,128)S(1)} %collective-permute-done.2.left_ref) | copy-start | bytes 49156
  25.4 0.6 copy-start.3
  25.4 0.6 copy-start
  26.0 0.6 copy-start.1

commit v6 on v5

--- a/solution.py
+++ b/solution.py
@@ -9,6 +9,9 @@
 
 SLOPES = (2.0, -1.5, 0.8)
 OFFSETS = (0.0, 0.5, -0.3)
+HALF_SLOPES = tuple(0.5 * v for v in SLOPES)
+HALF_OFFSETS = tuple(0.5 * v for v in OFFSETS)
+LOG2_E = 1.4426950408889634
 MESH_ID = pl.DeviceIdType.MESH
 
 
@@ -115,12 +118,13 @@
         left_lanes = slice((h - 1) * 128, h * 128) if h > 0 else None
         right_lanes = slice((h + 1) * 128, (h + 2) * 128) if h + 1 < halves else None
         absorb = absorb_ref[:, lanes]
+        fade = absorb * (-LOG2_E)
 
         def plane(ref_plane):
             return ref_plane[:, lanes]
 
         def step(x, carry):
-            seen, c0, c1, c2, optical = carry
+            seen, total, t0, t1, t2, softsum = carry
             centre_plane = dens_ref.at[x]
             d = centre_plane[:, lanes]
             behind = jnp.where(x == 0, front_ref[:, lanes], dens_ref[jnp.maximum(x - 1, 0), :, lanes])
@@ -142,30 +146,33 @@
             right = jnp.where(last_lane, edge_right, from_right)
             above = jnp.where(top_row, 0.0, pltpu.roll(d, 1, 0))
             below = jnp.where(bottom_row, 0.0, pltpu.roll(d, rows - 1, 0))
-            step_depth = (ahead - behind) * 0.5
-            step_row = (below - above) * 0.5
-            step_col = (right - left) * 0.5
-            facing = 0.48 * step_depth + 0.64 * step_row + 0.6 * step_col
-            length2 = step_depth * step_depth + step_row * step_row + step_col * step_col + 1.0
-            lighting = 0.25 + 0.75 * jnp.maximum(facing, 0.0) * lax.rsqrt(length2)
-            soft = jnp.maximum(d, 0.0) + jnp.log1p(jnp.exp(-jnp.abs(d)))
-            extinct = absorb * soft
-            passed = jnp.exp(-extinct)
-            weight = seen * (1.0 - passed) * lighting
-            tints = [1.0 / (1.0 + jnp.exp(-(slope * d + offset))) for slope, offset in zip(SLOPES, OFFSETS)]
+            step_depth = ahead - behind
+            step_row = below - above
+            step_col = right - left
+            facing = 0.18 * step_depth + 0.24 * step_row + 0.225 * step_col
+            length2 = 0.25 * (step_depth * step_depth + step_row * step_row + step_col * step_col) + 1.0
+            lighting = 0.25 + jnp.maximum(facing, 0.0) * lax.rsqrt(length2)
+            soft = jnp.log(1.0 + jnp.exp(d))
+            passed = jnp.exp2(fade * soft)
+            seen_after = seen * passed
+            weight = (seen - seen_after) * lighting
             return (
-                seen * passed,
-                c0 + weight * tints[0],
-                c1 + weight * tints[1],
-                c2 + weight * tints[2],
-                optical + extinct,
+                seen_after,
+                total + weight,
+                t0 + weight * jnp.tanh(HALF_SLOPES[0] * d + HALF_OFFSETS[0]),
+                t1 + weight * jnp.tanh(HALF_SLOPES[1] * d + HALF_OFFSETS[1]),
+                t2 + weight * jnp.tanh(HALF_SLOPES[2] * d + HALF_OFFSETS[2]),
+                softsum + soft,
             )
 
         zero = jnp.zeros(shape, jnp.float32)
         one = jnp.ones(shape, jnp.float32)
-        _, c0, c1, c2, optical = lax.fori_loop(0, last + 1, step, (one, zero, zero, zero, zero))
-        for k, value in enumerate((c0, c1, c2, optical)):
-            out_ref[k, :, lanes] = value
+        _, total, t0, t1, t2, softsum = lax.fori_loop(
+            0, last + 1, step, (one, zero, zero, zero, zero, zero)
+        )
+        for k, value in enumerate((t0, t1, t2)):
+            out_ref[k, :, lanes] = 0.5 * (total + value)
+        out_ref[3, :, lanes] = absorb * softsum
 
 
 def march(density, front, back, left, right, absorb):

time: 87.9 us -> 88.6 us (level)
  no operation moved by 1% of the time
where the time goes in v6:
time: 88.6 us; the launch traced here: 88.2 us
  Pallas kernels  57.4 us (65%)
  local copies, waits for them, and re-layouts  14.4 us (16%)
  starting transfers between devices  11.3 us (13%)
  waiting for transfers between devices  4.41 us (5%)
    pallas_call x1, Pallas kernels, march(): pl.pallas_call(functools.partial(march_kernel, depth - 1), out_shape=jax....  29.8 us
    pallas_call x1, Pallas kernels, combine(): pl.pallas_call(functools.partial(combine_kernel, n, rows), out_shape=(jax...  27.6 us
    ppermute x4, starting transfers between devices, shifted(): return lax.ppermute(value, axis, pairs)  11.3 us
    unnamed x12, local copies, waits for them, and re-layouts  7.67 us
    ppermute x4, waiting for transfers between devices, shifted(): return lax.ppermute(value, axis, pairs)  4.41 us
    slice x1, local copies, waits for them, and re-layouts, local(): right = shifted(jnp.transpose(density[:, :, 0]), 'gy', False)  4.26 us
  transfers between devices with their start and end apart: 4, of which 1 were waited for; matrix products, arithmetic and copies ran while one was open for 9% of the time, Pallas kernels for 0%

profile of v6, /device:TPU:7, one launch (start us, length us, event | category | flops | bytes accessed | tf_op | source)
XLA Modules:
  0.0 88.2 jit_solution(5537092700738103549)
XLA Ops:
  0.6 0.8 slice_bitcast_fusion
  1.4 4.1 %collective-permute-start = (f32[32,256]{1,0:T(8,128)S(1)}, f32[32,256]{1,0:T(8,128)S(1)}, u32[]{:S(2)}, u32[]{:S(2)}) collective-permute-start(f32[32,256]{1,0:T(8,128)S(1)} %get-tuple-element.5), channel_id=1, source_target_pairs={{0,16},{16,32},{32,48},{48,64},{64,80},{80,96},{96,112},{112,128},... | collective-permute-start | bytes 98312 | tf_op jit(solution)/shard_map/ppermute | solution.py:194
  5.5 1.9 %collective-permute-start.1 = (f32[32,256]{1,0:T(8,128)S(1)}, f32[32,256]{1,0:T(8,128)S(1)}, u32[]{:S(2)}, u32[]{:S(2)}) collective-permute-start(f32[32,256]{1,0:T(8,128)S(1)} %get-tuple-element.4), channel_id=1, source_target_pairs={{16,0},{32,16},{48,32},{64,48},{80,64},{96,80},{112,96},{128,112},... | collective-permute-start | bytes 98312 | tf_op jit(solution)/shard_map/ppermute | solution.py:194
  7.4 4.3 %fusion = (f32[128,32,1]{2,1,0:T(8,128)S(1)}, f32[128,32,1]{2,1,0:T(8,128)}) fusion(f32[128,32,256]{2,1,0:T(8,128)} %dens_ref.1), kind=kLoop, calls=%fused_computation.2 | loop fusion | bytes 65536 | tf_op jit(solution)/shard_map/slice | solution.py:202
  11.7 2.7 %copy.7 = f32[128,32,1]{0,1,2:T(8,128)S(1)} copy(f32[128,32,1]{2,1,0:T(8,128)} %get-tuple-element.3) | data formatting | bytes 32768
  14.4 3.1 %collective-permute-start.2 = (f32[32,128]{1,0:T(8,128)S(1)}, f32[32,128]{1,0:T(8,128)S(1)}, u32[]{:S(2)}, u32[]{:S(2)}) collective-permute-start(f32[32,128]{1,0:T(8,128)S(1)} %bitcast.12), channel_id=1, source_target_pairs={{0,1},{1,2},{2,3},{3,4},{4,5},{5,6},{6,7},{7,8},{8,9},{9,10},{10,1... | collective-permute-start | bytes 49160 | tf_op jit(solution)/shard_map/ppermute | solution.py:194
  17.5 1.3 %copy.8 = f32[128,32,1]{0,1,2:T(8,128)S(1)} copy(f32[128,32,1]{2,1,0:T(8,128)S(1)} %get-tuple-element.2) | data formatting | bytes 32768
  18.8 2.2 %collective-permute-start.3 = (f32[32,128]{1,0:T(8,128)S(1)}, f32[32,128]{1,0:T(8,128)S(1)}, u32[]{:S(2)}, u32[]{:S(2)}) collective-permute-start(f32[32,128]{1,0:T(8,128)S(1)} %bitcast.13), channel_id=1, source_target_pairs={{1,0},{2,1},{3,2},{4,3},{5,4},{6,5},{7,6},{8,7},{9,8},{10,9},{11,1... | collective-permute-start | bytes 49160 | tf_op jit(solution)/shard_map/ppermute | solution.py:194
  20.9 0.0 collective-permute-done.2.left_ref
  21.0 0.0 copy-start.2
  21.0 4.4 %collective-permute-done.3.right_ref = f32[32,128]{1,0:T(8,128)S(1)} collective-permute-done((f32[32,128]{1,0:T(8,128)S(1)}, f32[32,128]{1,0:T(8,128)S(1)}, u32[]{:S(2)}, u32[]{:S(2)}) %collective-permute-start.3) | collective-permute-done | bytes 16416 | tf_op jit(solution)/shard_map/ppermute | solution.py:194
  25.4 0.0 copy-start.3
  25.4 0.0 collective-permute-done.front_ref
  25.4 0.0 copy-start
  25.4 0.0 collective-permute-done.1.back_ref
  25.4 0.0 copy-done.2
  25.4 0.6 copy-done.3
  26.0 0.0 copy-done
  26.0 0.0 copy-start.1
  26.0 0.6 copy-done.1
  26.6 29.8 %shard_map.41 = f32[4,32,256]{2,1,0:T(8,128)} custom-call(f32[128,32,256]{2,1,0:T(8,128)} %dens_ref.1, f32[32,256]{1,0:T(8,128)} %copy-done, f32[32,256]{1,0:T(8,128)} %copy-done.1, f32[32,128]{1,0:T(8,128)} %copy-done.2, f32[32,128]{1,0:T(8,128)} %copy-done.3, f32[32,256]{1,0:T(8,128)} %absorb_ref.1), custom_call_target="tpu_custom_call" | custom-call | tf_op jit(solution)/shard_map/pallas_call | solution.py:181
  56.4 1.0 %copy.6 = f32[32,4,256]{2,1,0:T(4,128)S(1)} copy(f32[32,4,256]{2,0,1:T(8,128)} %bitcast.11) | data formatting | bytes 262144 | tf_op jit(solution)/shard_map/transpose | solution.py:205
  57.4 0.7 reshape_reshape.3.stacked_ref
  58.1 27.6 %shard_map.42 = (f32[3,1,256]{2,1,0:T(1,128)}, f32[1,256]{1,0:T(1,128)}) custom-call(f32[32,8,128]{2,1,0:T(8,128)} %reshape_reshape.3.stacked_ref), custom_call_target="tpu_custom_call" | custom-call | tf_op jit(solution)/shard_map/pallas_call | solution.py:90
  85.7 1.3 %copy.11 = f32[3,1,256]{2,1,0:T(1,128)} copy(f32[3,1,256]{2,1,0:T(1,128)} %get-tuple-element.8) | data formatting | bytes 6144
  87.0 1.2 %copy.12 = f32[1,256]{1,0:T(1,128)} copy(f32[1,256]{1,0:T(1,128)} %get-tuple-element.9) | data formatting | bytes 2048
Async XLA Ops:
  1.4 24.0 %collective-permute-start = (f32[32,256]{1,0:T(8,128)S(1)}, f32[32,256]{1,0:T(8,128)S(1)}, u32[]{:S(2)}, u32[]{:S(2)}) collective-permute-start(f32[32,256]{1,0:T(8,128)S(1)} %get-tuple-element.5), channel_id=1, source_target_pairs={{0,16},{16,32},{32,48},{48,64},{64,80},{80,96},{96,112},{112,128},... | collective-permute-start | bytes 98312 | tf_op jit(solution)/shard_map/ppermute | solution.py:194
  5.5 19.9 %collective-permute-start.1 = (f32[32,256]{1,0:T(8,128)S(1)}, f32[32,256]{1,0:T(8,128)S(1)}, u32[]{:S(2)}, u32[]{:S(2)}) collective-permute-start(f32[32,256]{1,0:T(8,128)S(1)} %get-tuple-element.4), channel_id=1, source_target_pairs={{16,0},{32,16},{48,32},{64,48},{80,64},{96,80},{112,96},{128,112},... | collective-permute-start | bytes 98312 | tf_op jit(solution)/shard_map/ppermute | solution.py:194
  14.4 6.6 %collective-permute-start.2 = (f32[32,128]{1,0:T(8,128)S(1)}, f32[32,128]{1,0:T(8,128)S(1)}, u32[]{:S(2)}, u32[]{:S(2)}) collective-permute-start(f32[32,128]{1,0:T(8,128)S(1)} %bitcast.12), channel_id=1, source_target_pairs={{0,1},{1,2},{2,3},{3,4},{4,5},{5,6},{6,7},{7,8},{8,9},{9,10},{10,1... | collective-permute-start | bytes 49160 | tf_op jit(solution)/shard_map/ppermute | solution.py:194
  18.8 6.6 %collective-permute-start.3 = (f32[32,128]{1,0:T(8,128)S(1)}, f32[32,128]{1,0:T(8,128)S(1)}, u32[]{:S(2)}, u32[]{:S(2)}) collective-permute-start(f32[32,128]{1,0:T(8,128)S(1)} %bitcast.13), channel_id=1, source_target_pairs={{1,0},{2,1},{3,2},{4,3},{5,4},{6,5},{7,6},{8,7},{9,8},{10,9},{11,1... | collective-permute-start | bytes 49160 | tf_op jit(solution)/shard_map/ppermute | solution.py:194
  21.0 4.4 %copy-start.2 = (f32[32,128]{1,0:T(8,128)}, f32[32,128]{1,0:T(8,128)S(1)}, u32[]{:S(2)}) copy-start(f32[32,128]{1,0:T(8,128)S(1)} %collective-permute-done.2.left_ref) | copy-start | bytes 49156
  25.4 0.6 copy-start.3
  25.4 0.6 copy-start
  26.0 0.6 copy-start.1

commit v7 on v6

--- a/solution.py
+++ b/solution.py
@@ -168,7 +168,7 @@
         zero = jnp.zeros(shape, jnp.float32)
         one = jnp.ones(shape, jnp.float32)
         _, total, t0, t1, t2, softsum = lax.fori_loop(
-            0, last + 1, step, (one, zero, zero, zero, zero, zero)
+            0, last + 1, step, (one, zero, zero, zero, zero, zero), unroll=4
         )
         for k, value in enumerate((t0, t1, t2)):
             out_ref[k, :, lanes] = 0.5 * (total + value)

time: 88.6 us -> 72.1 us (0.81)
  Pallas kernels: 57.4 us -> 40.9 us
    pallas_call x1, Pallas kernels: 29.8 us -> 13.3 us  [march(): pl.pallas_call(functools.partial(march_kernel, depth - 1), out_shape=jax....]
  transfers between devices with their start and end apart: 4 -> 4, of which waited for: 1 -> 1; matrix products, arithmetic and copies ran while one was open for 9% -> 11% of each run, Pallas kernels for 0% -> 0%
where the time goes in v7:
time: 72.1 us; the launch traced here: 71.7 us
  Pallas kernels  40.9 us (57%)
  local copies, waits for them, and re-layouts  14.4 us (20%)
  starting transfers between devices  11.3 us (16%)
  waiting for transfers between devices  4.41 us (6%)
    pallas_call x1, Pallas kernels, combine(): pl.pallas_call(functools.partial(combine_kernel, n, rows), out_shape=(jax...  27.6 us
    pallas_call x1, Pallas kernels, march(): pl.pallas_call(functools.partial(march_kernel, depth - 1), out_shape=jax....  13.3 us
    ppermute x4, starting transfers between devices, shifted(): return lax.ppermute(value, axis, pairs)  11.3 us
    unnamed x12, local copies, waits for them, and re-layouts  7.67 us
    ppermute x4, waiting for transfers between devices, shifted(): return lax.ppermute(value, axis, pairs)  4.41 us
    slice x1, local copies, waits for them, and re-layouts, local(): right = shifted(jnp.transpose(density[:, :, 0]), 'gy', False)  4.26 us
  transfers between devices with their start and end apart: 4, of which 1 were waited for; matrix products, arithmetic and copies ran while one was open for 11% of the time, Pallas kernels for 0%

profile of v7, /device:TPU:7, one launch (start us, length us, event | category | flops | bytes accessed | tf_op | source)
XLA Modules:
  0.0 71.7 jit_solution(10520530987932382462)
XLA Ops:
  0.6 0.8 %slice_bitcast_fusion = (f32[32,256]{1,0:T(8,128)S(1)}, f32[32,256]{1,0:T(8,128)S(1)}) fusion(f32[128,32,256]{2,1,0:T(8,128)} %dens_ref.1), kind=kLoop, calls=%fused_computation | loop fusion | bytes 131072 | tf_op jit(solution)/shard_map/squeeze | solution.py:200
  1.4 4.1 %collective-permute-start = (f32[32,256]{1,0:T(8,128)S(1)}, f32[32,256]{1,0:T(8,128)S(1)}, u32[]{:S(2)}, u32[]{:S(2)}) collective-permute-start(f32[32,256]{1,0:T(8,128)S(1)} %get-tuple-element.5), channel_id=1, source_target_pairs={{0,16},{16,32},{32,48},{48,64},{64,80},{80,96},{96,112},{112,128},... | collective-permute-start | bytes 98312 | tf_op jit(solution)/shard_map/ppermute | solution.py:194
  5.5 1.9 %collective-permute-start.1 = (f32[32,256]{1,0:T(8,128)S(1)}, f32[32,256]{1,0:T(8,128)S(1)}, u32[]{:S(2)}, u32[]{:S(2)}) collective-permute-start(f32[32,256]{1,0:T(8,128)S(1)} %get-tuple-element.4), channel_id=1, source_target_pairs={{16,0},{32,16},{48,32},{64,48},{80,64},{96,80},{112,96},{128,112},... | collective-permute-start | bytes 98312 | tf_op jit(solution)/shard_map/ppermute | solution.py:194
  7.4 4.3 %fusion = (f32[128,32,1]{2,1,0:T(8,128)S(1)}, f32[128,32,1]{2,1,0:T(8,128)}) fusion(f32[128,32,256]{2,1,0:T(8,128)} %dens_ref.1), kind=kLoop, calls=%fused_computation.2 | loop fusion | bytes 65536 | tf_op jit(solution)/shard_map/slice | solution.py:202
  11.7 2.7 %copy.7 = f32[128,32,1]{0,1,2:T(8,128)S(1)} copy(f32[128,32,1]{2,1,0:T(8,128)} %get-tuple-element.3) | data formatting | bytes 32768
  14.4 3.1 %collective-permute-start.2 = (f32[32,128]{1,0:T(8,128)S(1)}, f32[32,128]{1,0:T(8,128)S(1)}, u32[]{:S(2)}, u32[]{:S(2)}) collective-permute-start(f32[32,128]{1,0:T(8,128)S(1)} %bitcast.12), channel_id=1, source_target_pairs={{0,1},{1,2},{2,3},{3,4},{4,5},{5,6},{6,7},{7,8},{8,9},{9,10},{10,1... | collective-permute-start | bytes 49160 | tf_op jit(solution)/shard_map/ppermute | solution.py:194
  17.5 1.3 %copy.8 = f32[128,32,1]{0,1,2:T(8,128)S(1)} copy(f32[128,32,1]{2,1,0:T(8,128)S(1)} %get-tuple-element.2) | data formatting | bytes 32768
  18.8 2.2 %collective-permute-start.3 = (f32[32,128]{1,0:T(8,128)S(1)}, f32[32,128]{1,0:T(8,128)S(1)}, u32[]{:S(2)}, u32[]{:S(2)}) collective-permute-start(f32[32,128]{1,0:T(8,128)S(1)} %bitcast.13), channel_id=1, source_target_pairs={{1,0},{2,1},{3,2},{4,3},{5,4},{6,5},{7,6},{8,7},{9,8},{10,9},{11,1... | collective-permute-start | bytes 49160 | tf_op jit(solution)/shard_map/ppermute | solution.py:194
  20.9 0.0 collective-permute-done.2.left_ref
  21.0 0.0 copy-start.2
  21.0 4.4 %collective-permute-done.3.right_ref = f32[32,128]{1,0:T(8,128)S(1)} collective-permute-done((f32[32,128]{1,0:T(8,128)S(1)}, f32[32,128]{1,0:T(8,128)S(1)}, u32[]{:S(2)}, u32[]{:S(2)}) %collective-permute-start.3) | collective-permute-done | bytes 16416 | tf_op jit(solution)/shard_map/ppermute | solution.py:194
  25.4 0.0 copy-start.3
  25.4 0.0 collective-permute-done.front_ref
  25.4 0.0 copy-start
  25.4 0.0 collective-permute-done.1.back_ref
  25.4 0.0 copy-done.2
  25.4 0.6 copy-done.3
  26.0 0.0 copy-done
  26.0 0.0 copy-start.1
  26.0 0.6 copy-done.1
  26.6 13.3 %shard_map.41 = f32[4,32,256]{2,1,0:T(8,128)} custom-call(f32[128,32,256]{2,1,0:T(8,128)} %dens_ref.1, f32[32,256]{1,0:T(8,128)} %copy-done, f32[32,256]{1,0:T(8,128)} %copy-done.1, f32[32,128]{1,0:T(8,128)} %copy-done.2, f32[32,128]{1,0:T(8,128)} %copy-done.3, f32[32,256]{1,0:T(8,128)} %absorb_ref.1), custom_call_target="tpu_custom_call" | custom-call | tf_op jit(solution)/shard_map/pallas_call | solution.py:181
  39.9 1.0 %copy.6 = f32[32,4,256]{2,1,0:T(4,128)S(1)} copy(f32[32,4,256]{2,0,1:T(8,128)} %bitcast.11) | data formatting | bytes 262144 | tf_op jit(solution)/shard_map/transpose | solution.py:205
  40.9 0.7 reshape_reshape.3.stacked_ref
  41.6 27.6 %shard_map.42 = (f32[3,1,256]{2,1,0:T(1,128)}, f32[1,256]{1,0:T(1,128)}) custom-call(f32[32,8,128]{2,1,0:T(8,128)} %reshape_reshape.3.stacked_ref), custom_call_target="tpu_custom_call" | custom-call | tf_op jit(solution)/shard_map/pallas_call | solution.py:90
  69.2 1.3 %copy.11 = f32[3,1,256]{2,1,0:T(1,128)} copy(f32[3,1,256]{2,1,0:T(1,128)} %get-tuple-element.8) | data formatting | bytes 6144
  70.4 1.2 %copy.12 = f32[1,256]{1,0:T(1,128)} copy(f32[1,256]{1,0:T(1,128)} %get-tuple-element.9) | data formatting | bytes 2048
Async XLA Ops:
  1.4 24.0 %collective-permute-start = (f32[32,256]{1,0:T(8,128)S(1)}, f32[32,256]{1,0:T(8,128)S(1)}, u32[]{:S(2)}, u32[]{:S(2)}) collective-permute-start(f32[32,256]{1,0:T(8,128)S(1)} %get-tuple-element.5), channel_id=1, source_target_pairs={{0,16},{16,32},{32,48},{48,64},{64,80},{80,96},{96,112},{112,128},... | collective-permute-start | bytes 98312 | tf_op jit(solution)/shard_map/ppermute | solution.py:194
  5.5 19.9 %collective-permute-start.1 = (f32[32,256]{1,0:T(8,128)S(1)}, f32[32,256]{1,0:T(8,128)S(1)}, u32[]{:S(2)}, u32[]{:S(2)}) collective-permute-start(f32[32,256]{1,0:T(8,128)S(1)} %get-tuple-element.4), channel_id=1, source_target_pairs={{16,0},{32,16},{48,32},{64,48},{80,64},{96,80},{112,96},{128,112},... | collective-permute-start | bytes 98312 | tf_op jit(solution)/shard_map/ppermute | solution.py:194
  14.4 6.6 %collective-permute-start.2 = (f32[32,128]{1,0:T(8,128)S(1)}, f32[32,128]{1,0:T(8,128)S(1)}, u32[]{:S(2)}, u32[]{:S(2)}) collective-permute-start(f32[32,128]{1,0:T(8,128)S(1)} %bitcast.12), channel_id=1, source_target_pairs={{0,1},{1,2},{2,3},{3,4},{4,5},{5,6},{6,7},{7,8},{8,9},{9,10},{10,1... | collective-permute-start | bytes 49160 | tf_op jit(solution)/shard_map/ppermute | solution.py:194
  18.8 6.6 %collective-permute-start.3 = (f32[32,128]{1,0:T(8,128)S(1)}, f32[32,128]{1,0:T(8,128)S(1)}, u32[]{:S(2)}, u32[]{:S(2)}) collective-permute-start(f32[32,128]{1,0:T(8,128)S(1)} %bitcast.13), channel_id=1, source_target_pairs={{1,0},{2,1},{3,2},{4,3},{5,4},{6,5},{7,6},{8,7},{9,8},{10,9},{11,1... | collective-permute-start | bytes 49160 | tf_op jit(solution)/shard_map/ppermute | solution.py:194
  21.0 4.4 %copy-start.2 = (f32[32,128]{1,0:T(8,128)}, f32[32,128]{1,0:T(8,128)S(1)}, u32[]{:S(2)}) copy-start(f32[32,128]{1,0:T(8,128)S(1)} %collective-permute-done.2.left_ref) | copy-start | bytes 49156
  25.4 0.6 copy-start.3
  25.4 0.6 copy-start
  26.0 0.6 copy-start.1

commit v8 on v7

--- a/solution.py
+++ b/solution.py
@@ -186,6 +186,37 @@
     )(density, front, back, left, right, absorb)
 
 
+def edge_kernel(dens_ref, first_ref, last_ref):
+    depth, rows, cols = dens_ref.shape
+    lane = lax.broadcasted_iota(jnp.int32, (rows, depth), 1)
+
+    def step(x, carry):
+        first, last = carry
+        here = lane == x
+        low = dens_ref[x, :, 0:128]
+        high = dens_ref[x, :, cols - 128:cols]
+        first = jnp.where(here, jnp.broadcast_to(low[:, 0:1], (rows, depth)), first)
+        last = jnp.where(here, jnp.broadcast_to(high[:, 127:128], (rows, depth)), last)
+        return first, last
+
+    zero = jnp.zeros((rows, depth), jnp.float32)
+    first, last = lax.fori_loop(0, depth, step, (zero, zero), unroll=8)
+    first_ref[...] = first
+    last_ref[...] = last
+
+
+def edges(density):
+    depth, rows, cols = density.shape
+    vmem = pltpu.MemorySpace.VMEM
+    plane = jax.ShapeDtypeStruct((rows, depth), jnp.float32)
+    return pl.pallas_call(
+        edge_kernel,
+        out_shape=(plane, plane),
+        in_specs=[pl.BlockSpec(memory_space=vmem)],
+        out_specs=(pl.BlockSpec(memory_space=vmem), pl.BlockSpec(memory_space=vmem)),
+    )(density)
+
+
 def shifted(value, axis, forward):
     size = lax.axis_size(axis)
     pairs = [(i, i + 1) for i in range(size - 1)]
@@ -198,8 +229,9 @@
     depth, nz, cols = density.shape
     front = shifted(density[depth - 1], "gx", True)
     back = shifted(density[0], "gx", False)
-    left = shifted(jnp.transpose(density[:, :, cols - 1]), "gy", True)
-    right = shifted(jnp.transpose(density[:, :, 0]), "gy", False)
+    first_col, last_col = edges(density)
+    left = shifted(last_col, "gy", True)
+    right = shifted(first_col, "gy", False)
     parts = march(density, front, back, left, right, absorb)
     n = lax.axis_size("gx")
     stacked = jnp.transpose(parts, (1, 0, 2)).reshape(n, nz // n, 4, cols)

time: 72.1 us -> 68 us (0.943)
  local copies, waits for them, and re-layouts: 14.4 us -> 6.18 us
  Pallas kernels: 40.9 us -> 44.8 us
    pallas_call x0 -> x1, Pallas kernels: none -> 5.33 us  [edges(): pl.pallas_call(edge_kernel, out_shape=(plane, plane), in_specs=[pl.BlockS...]
    slice x1 -> x0, local copies, waits for them, and re-layouts: 4.26 us -> none  [local(): right = shifted(jnp.transpose(density[:, :, 0]), 'gy', False)]
    unnamed x12 -> x10, local copies, waits for them, and re-layouts: 7.67 us -> 3.71 us
    pallas_call x1, Pallas kernels: 27.6 us -> 26.1 us  [combine(): pl.pallas_call(functools.partial(combine_kernel, n, rows), out_shape=(jax...]
  transfers between devices with their start and end apart: 4 -> 4, of which waited for: 1 -> 1; matrix products, arithmetic and copies ran while one was open for 11% -> 0% of each run, Pallas kernels for 0% -> 8%
where the time goes in v8:
time: 68 us; the launch traced here: 67.6 us
  Pallas kernels  44.8 us (66%)
  starting transfers between devices  11.3 us (17%)
  local copies, waits for them, and re-layouts  6.18 us (9%)
  waiting for transfers between devices  4.63 us (7%)
  between operations  0.71 us (1%)
    pallas_call x1, Pallas kernels, combine(): pl.pallas_call(functools.partial(combine_kernel, n, rows), out_shape=(jax...  26.1 us
    pallas_call x1, Pallas kernels, march(): pl.pallas_call(functools.partial(march_kernel, depth - 1), out_shape=jax....  13.3 us
    ppermute x4, starting transfers between devices, shifted(): return lax.ppermute(value, axis, pairs)  11.3 us
    pallas_call x1, Pallas kernels, edges(): pl.pallas_call(edge_kernel, out_shape=(plane, plane), in_specs=[pl.BlockS...  5.33 us
    ppermute x4, waiting for transfers between devices, shifted(): return lax.ppermute(value, axis, pairs)  4.63 us
    unnamed x10, local copies, waits for them, and re-layouts  3.71 us
  transfers between devices with their start and end apart: 4, of which 1 were waited for; matrix products, arithmetic and copies ran while one was open for 0% of the time, Pallas kernels for 8%

profile of v8, /device:TPU:7, one launch (start us, length us, event | category | flops | bytes accessed | tf_op | source)
XLA Modules:
  0.0 67.6 jit_solution(11231357350290524980)
XLA Ops:
  0.6 0.8 %slice_bitcast_fusion = (f32[32,256]{1,0:T(8,128)S(1)}, f32[32,256]{1,0:T(8,128)S(1)}) fusion(f32[128,32,256]{2,1,0:T(8,128)} %dens_ref.3), kind=kLoop, calls=%fused_computation | loop fusion | bytes 131072 | tf_op jit(solution)/shard_map/squeeze | solution.py:231
  1.4 2.6 %collective-permute-start.1 = (f32[32,256]{1,0:T(8,128)S(1)}, f32[32,256]{1,0:T(8,128)S(1)}, u32[]{:S(2)}, u32[]{:S(2)}) collective-permute-start(f32[32,256]{1,0:T(8,128)S(1)} %get-tuple-element.6), channel_id=1, source_target_pairs={{16,0},{32,16},{48,32},{64,48},{80,64},{96,80},{112,96},{128,112},... | collective-permute-start | bytes 98312 | tf_op jit(solution)/shard_map/ppermute | solution.py:225
  4.0 3.4 %collective-permute-start = (f32[32,256]{1,0:T(8,128)S(1)}, f32[32,256]{1,0:T(8,128)S(1)}, u32[]{:S(2)}, u32[]{:S(2)}) collective-permute-start(f32[32,256]{1,0:T(8,128)S(1)} %get-tuple-element.7), channel_id=1, source_target_pairs={{0,16},{16,32},{32,48},{48,64},{64,80},{80,96},{96,112},{112,128},... | collective-permute-start | bytes 98312 | tf_op jit(solution)/shard_map/ppermute | solution.py:225
  7.4 5.3 %shard_map.41 = (f32[32,128]{1,0:T(8,128)}, f32[32,128]{1,0:T(8,128)}) custom-call(f32[128,32,256]{2,1,0:T(8,128)} %dens_ref.3), custom_call_target="tpu_custom_call" | custom-call | tf_op jit(solution)/shard_map/pallas_call | solution.py:212
  12.8 3.1 %collective-permute-start.2 = (f32[32,128]{1,0:T(8,128)}, f32[32,128]{1,0:T(8,128)S(1)}, u32[]{:S(2)}, u32[]{:S(2)}) collective-permute-start(f32[32,128]{1,0:T(8,128)} %get-tuple-element.4), channel_id=1, source_target_pairs={{0,1},{1,2},{2,3},{3,4},{4,5},{5,6},{6,7},{7,8},{8,9},{9,10},{10,1... | collective-permute-start | bytes 49160 | tf_op jit(solution)/shard_map/ppermute | solution.py:225
  15.9 2.2 %collective-permute-start.3 = (f32[32,128]{1,0:T(8,128)}, f32[32,128]{1,0:T(8,128)S(1)}, u32[]{:S(2)}, u32[]{:S(2)}) collective-permute-start(f32[32,128]{1,0:T(8,128)} %get-tuple-element.5), channel_id=1, source_target_pairs={{1,0},{2,1},{3,2},{4,3},{5,4},{6,5},{7,6},{8,7},{9,8},{10,9},{11,1... | collective-permute-start | bytes 49160 | tf_op jit(solution)/shard_map/ppermute | solution.py:225
  18.1 0.0 collective-permute-done.2.left_ref
  18.1 0.0 copy-start.2
  18.1 4.6 %collective-permute-done.3.right_ref = f32[32,128]{1,0:T(8,128)S(1)} collective-permute-done((f32[32,128]{1,0:T(8,128)}, f32[32,128]{1,0:T(8,128)S(1)}, u32[]{:S(2)}, u32[]{:S(2)}) %collective-permute-start.3) | collective-permute-done | bytes 16416 | tf_op jit(solution)/shard_map/ppermute | solution.py:225
  22.7 0.0 copy-start.3
  22.7 0.0 collective-permute-done.1.back_ref
  22.7 0.0 copy-start
  22.7 0.0 collective-permute-done.front_ref
  22.7 0.0 copy-done.2
  22.7 0.6 copy-done.3
  23.3 0.0 copy-done
  23.3 0.0 copy-start.1
  23.3 0.6 copy-done.1
  23.9 13.3 %shard_map.42 = f32[4,32,256]{2,1,0:T(8,128)} custom-call(f32[128,32,256]{2,1,0:T(8,128)} %dens_ref.3, f32[32,256]{1,0:T(8,128)} %copy-done.1, f32[32,256]{1,0:T(8,128)} %copy-done, f32[32,128]{1,0:T(8,128)} %copy-done.2, f32[32,128]{1,0:T(8,128)} %copy-done.3, f32[32,256]{1,0:T(8,128)} %absorb_ref.1), custom_call_target="tpu_custom_call" | custom-call | tf_op jit(solution)/shard_map/pallas_call | solution.py:181
  37.2 1.0 %copy.4 = f32[32,4,256]{2,1,0:T(4,128)S(1)} copy(f32[32,4,256]{2,0,1:T(8,128)} %bitcast.5) | data formatting | bytes 262144 | tf_op jit(solution)/shard_map/transpose | solution.py:237
  38.2 0.7 %reshape_reshape.3.stacked_ref = f32[32,8,128]{2,1,0:T(8,128)} reshape(f32[32,4,256]{2,1,0:T(4,128)S(1)} %copy.4) | data formatting | bytes 262144 | tf_op jit(solution)/shard_map/reshape;reshape | solution.py:88
  38.9 26.1 %shard_map.43 = (f32[3,1,256]{2,1,0:T(1,128)}, f32[1,256]{1,0:T(1,128)}) custom-call(f32[32,8,128]{2,1,0:T(8,128)} %reshape_reshape.3.stacked_ref), custom_call_target="tpu_custom_call" | custom-call | tf_op jit(solution)/shard_map/pallas_call | solution.py:90
  65.1 1.3 %copy.7 = f32[3,1,256]{2,1,0:T(1,128)} copy(f32[3,1,256]{2,1,0:T(1,128)} %get-tuple-element.10) | data formatting | bytes 6144
  66.3 1.2 %copy.8 = f32[1,256]{1,0:T(1,128)} copy(f32[1,256]{1,0:T(1,128)} %get-tuple-element.11) | data formatting | bytes 2048
Async XLA Ops:
  1.4 21.3 %collective-permute-start.1 = (f32[32,256]{1,0:T(8,128)S(1)}, f32[32,256]{1,0:T(8,128)S(1)}, u32[]{:S(2)}, u32[]{:S(2)}) collective-permute-start(f32[32,256]{1,0:T(8,128)S(1)} %get-tuple-element.6), channel_id=1, source_target_pairs={{16,0},{32,16},{48,32},{64,48},{80,64},{96,80},{112,96},{128,112},... | collective-permute-start | bytes 98312 | tf_op jit(solution)/shard_map/ppermute | solution.py:225
  4.0 18.7 %collective-permute-start = (f32[32,256]{1,0:T(8,128)S(1)}, f32[32,256]{1,0:T(8,128)S(1)}, u32[]{:S(2)}, u32[]{:S(2)}) collective-permute-start(f32[32,256]{1,0:T(8,128)S(1)} %get-tuple-element.7), channel_id=1, source_target_pairs={{0,16},{16,32},{32,48},{48,64},{64,80},{80,96},{96,112},{112,128},... | collective-permute-start | bytes 98312 | tf_op jit(solution)/shard_map/ppermute | solution.py:225
  12.8 5.3 %collective-permute-start.2 = (f32[32,128]{1,0:T(8,128)}, f32[32,128]{1,0:T(8,128)S(1)}, u32[]{:S(2)}, u32[]{:S(2)}) collective-permute-start(f32[32,128]{1,0:T(8,128)} %get-tuple-element.4), channel_id=1, source_target_pairs={{0,1},{1,2},{2,3},{3,4},{4,5},{5,6},{6,7},{7,8},{8,9},{9,10},{10,1... | collective-permute-start | bytes 49160 | tf_op jit(solution)/shard_map/ppermute | solution.py:225
  15.9 6.8 %collective-permute-start.3 = (f32[32,128]{1,0:T(8,128)}, f32[32,128]{1,0:T(8,128)S(1)}, u32[]{:S(2)}, u32[]{:S(2)}) collective-permute-start(f32[32,128]{1,0:T(8,128)} %get-tuple-element.5), channel_id=1, source_target_pairs={{1,0},{2,1},{3,2},{4,3},{5,4},{6,5},{7,6},{8,7},{9,8},{10,9},{11,1... | collective-permute-start | bytes 49160 | tf_op jit(solution)/shard_map/ppermute | solution.py:225
  18.1 4.6 %copy-start.2 = (f32[32,128]{1,0:T(8,128)}, f32[32,128]{1,0:T(8,128)S(1)}, u32[]{:S(2)}) copy-start(f32[32,128]{1,0:T(8,128)S(1)} %collective-permute-done.2.left_ref) | copy-start | bytes 49156
  22.7 0.6 copy-start.3
  22.7 0.6 copy-start
  23.3 0.6 copy-start.1

commit v9 on v8

--- a/solution.py
+++ b/solution.py
@@ -15,97 +15,8 @@
 MESH_ID = pl.DeviceIdType.MESH
 
 
-def combine_kernel(n, rows, stacked_ref, colour_ref, transmit_ref, recv, send_sems, recv_sems, local_sem):
-    me = lax.axis_index("gx")
-    col = lax.axis_index("gy")
-
-    def peer_of(i):
-        return lax.rem(me + i, n)
-
-    def link(peer, slot):
-        return pltpu.make_async_remote_copy(
-            src_ref=stacked_ref.at[peer],
-            dst_ref=recv.at[slot],
-            send_sem=send_sems.at[peer],
-            recv_sem=recv_sems.at[slot],
-            device_id=(peer, col),
-            device_id_type=MESH_ID,
-        )
-
-    barrier = pltpu.get_barrier_semaphore()
-
-    def greet(i, carry):
-        pl.semaphore_signal(barrier, inc=1, device_id=(peer_of(i), col), device_id_type=MESH_ID)
-        return carry
-
-    lax.fori_loop(1, n, greet, 0)
-    pl.semaphore_wait(barrier, n - 1)
-
-    def send(i, carry):
-        link(peer_of(i), me).start()
-        return carry
-
-    lax.fori_loop(1, n, send, 0)
-    own = pltpu.make_async_copy(stacked_ref.at[me], recv.at[me], local_sem)
-    own.start()
-    own.wait()
-
-    def finish(i, carry):
-        peer = peer_of(i)
-        link(peer, peer).wait_send()
-        link(peer, peer).wait_recv()
-        return carry
-
-    lax.fori_loop(1, n, finish, 0)
-
-    cols = colour_ref.shape[-1]
-    span = cols // 128
-    zero = jnp.zeros((rows * span, 128), jnp.float32)
-
-    def value(block, k):
-        pieces = [block[(r * 4 + k) * span:(r * 4 + k + 1) * span] for r in range(rows)]
-        return pieces[0] if rows == 1 else jnp.concatenate(pieces, axis=0)
-
-    def accumulate(d, carry):
-        front, c0, c1, c2 = carry
-        block = recv[d]
-        seen = jnp.exp(-front)
-        return (
-            front + value(block, 3),
-            c0 + value(block, 0) * seen,
-            c1 + value(block, 1) * seen,
-            c2 + value(block, 2) * seen,
-        )
-
-    front, c0, c1, c2 = lax.fori_loop(0, n, accumulate, (zero, zero, zero, zero))
-    for k, c in enumerate((c0, c1, c2)):
-        colour_ref[k] = c.reshape(rows, cols)
-    transmit_ref[...] = jnp.exp(-front).reshape(rows, cols)
-
-
-def combine(stacked, n):
-    rows, cols = stacked.shape[1], stacked.shape[3]
-    stacked = stacked.reshape(n, rows * 4 * cols // 128, 128)
-    vmem = pltpu.MemorySpace.VMEM
-    return pl.pallas_call(
-        functools.partial(combine_kernel, n, rows),
-        out_shape=(
-            jax.ShapeDtypeStruct((3, rows, cols), jnp.float32),
-            jax.ShapeDtypeStruct((rows, cols), jnp.float32),
-        ),
-        in_specs=[pl.BlockSpec(memory_space=vmem)],
-        out_specs=(pl.BlockSpec(memory_space=vmem), pl.BlockSpec(memory_space=vmem)),
-        scratch_shapes=[
-            pltpu.VMEM(stacked.shape, jnp.float32),
-            pltpu.SemaphoreType.DMA((n,)),
-            pltpu.SemaphoreType.DMA((n,)),
-            pltpu.SemaphoreType.DMA,
-        ],
-        compiler_params=pltpu.CompilerParams(collective_id=0, has_side_effects=True),
-    )(stacked)
-
-
-def march_kernel(last, dens_ref, front_ref, back_ref, left_ref, right_ref, absorb_ref, out_ref):
+def march_kernel(last, n, dens_ref, front_ref, back_ref, left_ref, right_ref, absorb_ref,
+                 colour_ref, transmit_ref, out_ref, part, recv, send_sems, recv_sems, local_sem):
     rows, cols = dens_ref.shape[1], dens_ref.shape[2]
     shape = (rows, 128)
     lane = lax.broadcasted_iota(jnp.int32, shape, 1)
@@ -113,6 +24,15 @@
     first_lane, last_lane = lane == 0, lane == 127
     top_row, bottom_row = row == 0, row == rows - 1
     halves = cols // 128
+    me = lax.axis_index("gx")
+    col = lax.axis_index("gy")
+    barrier = pltpu.get_barrier_semaphore()
+
+    def greet(i, carry):
+        pl.semaphore_signal(barrier, inc=1, device_id=(lax.rem(me + i, n), col), device_id_type=MESH_ID)
+        return carry
+
+    lax.fori_loop(1, n, greet, 0)
     for h in range(halves):
         lanes = slice(h * 128, (h + 1) * 128)
         left_lanes = slice((h - 1) * 128, h * 128) if h > 0 else None
@@ -174,15 +94,92 @@
             out_ref[k, :, lanes] = 0.5 * (total + value)
         out_ref[3, :, lanes] = absorb * softsum
 
-
-def march(density, front, back, left, right, absorb):
+    share = rows // n
+    for z in range(rows):
+        for k in range(4):
+            for h in range(halves):
+                r = ((z % share) * 4 + k) * halves + h
+                part[z // share, r:r + 1, :] = out_ref[k, z:z + 1, h * 128:(h + 1) * 128]
+    exchange_and_combine(n, share, halves, me, col, barrier, part, recv, send_sems, recv_sems,
+                         local_sem, colour_ref, transmit_ref)
+
+
+def exchange_and_combine(n, share, halves, me, col, barrier, part, recv, send_sems, recv_sems,
+                         local_sem, colour_ref, transmit_ref):
+    def link(peer, slot):
+        return pltpu.make_async_remote_copy(
+            src_ref=part.at[peer],
+            dst_ref=recv.at[slot],
+            send_sem=send_sems.at[peer],
+            recv_sem=recv_sems.at[slot],
+            device_id=(peer, col),
+            device_id_type=MESH_ID,
+        )
+
+    pl.semaphore_wait(barrier, n - 1)
+
+    def send(i, carry):
+        link(lax.rem(me + i, n), me).start()
+        return carry
+
+    lax.fori_loop(1, n, send, 0)
+    own = pltpu.make_async_copy(part.at[me], recv.at[me], local_sem)
+    own.start()
+    own.wait()
+
+    def finish(i, carry):
+        peer = lax.rem(me + i, n)
+        link(peer, peer).wait_send()
+        link(peer, peer).wait_recv()
+        return carry
+
+    lax.fori_loop(1, n, finish, 0)
+    cols = colour_ref.shape[-1]
+    zero = jnp.zeros((share * halves, 128), jnp.float32)
+
+    def value(block, k):
+        pieces = [block[(r * 4 + k) * halves:(r * 4 + k + 1) * halves] for r in range(share)]
+        return pieces[0] if share == 1 else jnp.concatenate(pieces, axis=0)
+
+    def accumulate(d, carry):
+        front, c0, c1, c2 = carry
+        block = recv[d]
+        seen = jnp.exp(-front)
+        return (
+            front + value(block, 3),
+            c0 + value(block, 0) * seen,
+            c1 + value(block, 1) * seen,
+            c2 + value(block, 2) * seen,
+        )
+
+    front, c0, c1, c2 = lax.fori_loop(0, n, accumulate, (zero, zero, zero, zero))
+    for k, c in enumerate((c0, c1, c2)):
+        colour_ref[k] = c.reshape(share, cols)
+    transmit_ref[...] = jnp.exp(-front).reshape(share, cols)
+
+
+def march(density, front, back, left, right, absorb, n):
     depth, rows, cols = density.shape
+    share = rows // n
+    tiles = (n, share * 4 * cols // 128, 128)
     vmem = pltpu.MemorySpace.VMEM
     return pl.pallas_call(
-        functools.partial(march_kernel, depth - 1),
-        out_shape=jax.ShapeDtypeStruct((4, rows, cols), jnp.float32),
+        functools.partial(march_kernel, depth - 1, n),
+        out_shape=(
+            jax.ShapeDtypeStruct((3, share, cols), jnp.float32),
+            jax.ShapeDtypeStruct((share, cols), jnp.float32),
+        ),
         in_specs=[pl.BlockSpec(memory_space=vmem)] * 6,
-        out_specs=pl.BlockSpec(memory_space=vmem),
+        out_specs=(pl.BlockSpec(memory_space=vmem), pl.BlockSpec(memory_space=vmem)),
+        scratch_shapes=[
+            pltpu.VMEM((4, rows, cols), jnp.float32),
+            pltpu.VMEM(tiles, jnp.float32),
+            pltpu.VMEM(tiles, jnp.float32),
+            pltpu.SemaphoreType.DMA((n,)),
+            pltpu.SemaphoreType.DMA((n,)),
+            pltpu.SemaphoreType.DMA,
+        ],
+        compiler_params=pltpu.CompilerParams(collective_id=0, has_side_effects=True),
     )(density, front, back, left, right, absorb)
 
 
@@ -232,10 +229,7 @@
     first_col, last_col = edges(density)
     left = shifted(last_col, "gy", True)
     right = shifted(first_col, "gy", False)
-    parts = march(density, front, back, left, right, absorb)
-    n = lax.axis_size("gx")
-    stacked = jnp.transpose(parts, (1, 0, 2)).reshape(n, nz // n, 4, cols)
-    return combine(stacked, n)
+    return march(density, front, back, left, right, absorb, lax.axis_size("gx"))
 
 
 def solution(mesh):

time: 68 us -> 62.4 us (0.918)
  Pallas kernels: 44.8 us -> 40.9 us
  local copies, waits for them, and re-layouts: 6.18 us -> 4.48 us
    pallas_call x2 -> x1, Pallas kernels: 39.4 us -> 35.6 us  [march(): pl.pallas_call(functools.partial(march_kernel, depth - 1, n), out_shape=(...]
    transpose x1 -> x0, local copies, waits for them, and re-layouts: 0.99 us -> none  [local(): stacked = jnp.transpose(parts, (1, 0, 2)).reshape(n, nz // n, 4, cols)]
    another operation x1 -> x0, local copies, waits for them, and re-layouts: 0.7 us -> none  [combine(): stacked = stacked.reshape(n, rows * 4 * cols // 128, 128)]
  transfers between devices with their start and end apart: 4 -> 4, of which waited for: 1 -> 1; matrix products, arithmetic and copies ran while one was open for 0% -> 0% of each run, Pallas kernels for 8% -> 9%
where the time goes in v9:
time: 62.4 us; the launch traced here: 62 us
  Pallas kernels  40.9 us (66%)
  starting transfers between devices  11.3 us (18%)
  waiting for transfers between devices  4.62 us (7%)
  local copies, waits for them, and re-layouts  4.48 us (7%)
  between operations  0.7 us (1%)
    pallas_call x1, Pallas kernels, march(): pl.pallas_call(functools.partial(march_kernel, depth - 1, n), out_shape=(...  35.6 us
    ppermute x4, starting transfers between devices, shifted(): return lax.ppermute(value, axis, pairs)  11.3 us
    pallas_call x1, Pallas kernels, edges(): pl.pallas_call(edge_kernel, out_shape=(plane, plane), in_specs=[pl.BlockS...  5.33 us
    ppermute x4, waiting for transfers between devices, shifted(): return lax.ppermute(value, axis, pairs)  4.62 us
    unnamed x10, local copies, waits for them, and re-layouts  3.69 us
  transfers between devices with their start and end apart: 4, of which 1 were waited for; matrix products, arithmetic and copies ran while one was open for 0% of the time, Pallas kernels for 9%

profile of v9, /device:TPU:7, one launch (start us, length us, event | category | flops | bytes accessed | tf_op | source)
XLA Modules:
  0.0 62.0 jit_solution(5163826068227732712)
XLA Ops:
  0.6 0.8 %slice_bitcast_fusion = (f32[32,256]{1,0:T(8,128)S(1)}, f32[32,256]{1,0:T(8,128)S(1)}) fusion(f32[128,32,256]{2,1,0:T(8,128)} %dens_ref.3), kind=kLoop, calls=%fused_computation | loop fusion | bytes 131072 | tf_op jit(solution)/shard_map/squeeze | solution.py:228
  1.4 4.1 %collective-permute-start = (f32[32,256]{1,0:T(8,128)S(1)}, f32[32,256]{1,0:T(8,128)S(1)}, u32[]{:S(2)}, u32[]{:S(2)}) collective-permute-start(f32[32,256]{1,0:T(8,128)S(1)} %get-tuple-element.7), channel_id=1, source_target_pairs={{0,16},{16,32},{32,48},{48,64},{64,80},{80,96},{96,112},{112,128},... | collective-permute-start | bytes 98312 | tf_op jit(solution)/shard_map/ppermute | solution.py:222
  5.5 1.9 %collective-permute-start.1 = (f32[32,256]{1,0:T(8,128)S(1)}, f32[32,256]{1,0:T(8,128)S(1)}, u32[]{:S(2)}, u32[]{:S(2)}) collective-permute-start(f32[32,256]{1,0:T(8,128)S(1)} %get-tuple-element.6), channel_id=1, source_target_pairs={{16,0},{32,16},{48,32},{64,48},{80,64},{96,80},{112,96},{128,112},... | collective-permute-start | bytes 98312 | tf_op jit(solution)/shard_map/ppermute | solution.py:222
  7.4 5.3 %shard_map.41 = (f32[32,128]{1,0:T(8,128)}, f32[32,128]{1,0:T(8,128)}) custom-call(f32[128,32,256]{2,1,0:T(8,128)} %dens_ref.3), custom_call_target="tpu_custom_call" | custom-call | tf_op jit(solution)/shard_map/pallas_call | solution.py:209
  12.8 3.1 %collective-permute-start.2 = (f32[32,128]{1,0:T(8,128)}, f32[32,128]{1,0:T(8,128)S(1)}, u32[]{:S(2)}, u32[]{:S(2)}) collective-permute-start(f32[32,128]{1,0:T(8,128)} %get-tuple-element.4), channel_id=1, source_target_pairs={{0,1},{1,2},{2,3},{3,4},{4,5},{5,6},{6,7},{7,8},{8,9},{9,10},{10,1... | collective-permute-start | bytes 49160 | tf_op jit(solution)/shard_map/ppermute | solution.py:222
  15.9 2.2 %collective-permute-start.3 = (f32[32,128]{1,0:T(8,128)}, f32[32,128]{1,0:T(8,128)S(1)}, u32[]{:S(2)}, u32[]{:S(2)}) collective-permute-start(f32[32,128]{1,0:T(8,128)} %get-tuple-element.5), channel_id=1, source_target_pairs={{1,0},{2,1},{3,2},{4,3},{5,4},{6,5},{7,6},{8,7},{9,8},{10,9},{11,1... | collective-permute-start | bytes 49160 | tf_op jit(solution)/shard_map/ppermute | solution.py:222
  18.1 0.0 collective-permute-done.2.left_ref
  18.1 0.0 copy-start.2
  18.1 4.6 %collective-permute-done.3.right_ref = f32[32,128]{1,0:T(8,128)S(1)} collective-permute-done((f32[32,128]{1,0:T(8,128)}, f32[32,128]{1,0:T(8,128)S(1)}, u32[]{:S(2)}, u32[]{:S(2)}) %collective-permute-start.3) | collective-permute-done | bytes 16416 | tf_op jit(solution)/shard_map/ppermute | solution.py:222
  22.7 0.0 copy-start.3
  22.7 0.0 collective-permute-done.front_ref
  22.7 0.0 copy-start
  22.7 0.0 collective-permute-done.1.back_ref
  22.7 0.0 copy-done.2
  22.7 0.6 copy-done.3
  23.3 0.0 copy-done
  23.3 0.0 copy-start.1
  23.3 0.6 copy-done.1
  23.9 35.6 %shard_map.42 = (f32[3,1,256]{2,1,0:T(1,128)}, f32[1,256]{1,0:T(1,128)}) custom-call(f32[128,32,256]{2,1,0:T(8,128)} %dens_ref.3, f32[32,256]{1,0:T(8,128)} %copy-done, f32[32,256]{1,0:T(8,128)} %copy-done.1, f32[32,128]{1,0:T(8,128)} %copy-done.2, f32[32,128]{1,0:T(8,128)} %copy-done.3, f32[32,256]{1,0:T(8,128)} %absorb_ref.1), custom_call_target="tpu_custom_call" | custom-call | tf_op jit(solution)/shard_map/pallas_call | solution.py:166
  59.5 1.2 %copy.6 = f32[3,1,256]{2,1,0:T(1,128)} copy(f32[3,1,256]{2,1,0:T(1,128)} %get-tuple-element.10) | data formatting | bytes 6144
  60.8 1.2 %copy.7 = f32[1,256]{1,0:T(1,128)} copy(f32[1,256]{1,0:T(1,128)} %get-tuple-element.11) | data formatting | bytes 2048
Async XLA Ops:
  1.4 21.3 %collective-permute-start = (f32[32,256]{1,0:T(8,128)S(1)}, f32[32,256]{1,0:T(8,128)S(1)}, u32[]{:S(2)}, u32[]{:S(2)}) collective-permute-start(f32[32,256]{1,0:T(8,128)S(1)} %get-tuple-element.7), channel_id=1, source_target_pairs={{0,16},{16,32},{32,48},{48,64},{64,80},{80,96},{96,112},{112,128},... | collective-permute-start | bytes 98312 | tf_op jit(solution)/shard_map/ppermute | solution.py:222
  5.5 17.2 %collective-permute-start.1 = (f32[32,256]{1,0:T(8,128)S(1)}, f32[32,256]{1,0:T(8,128)S(1)}, u32[]{:S(2)}, u32[]{:S(2)}) collective-permute-start(f32[32,256]{1,0:T(8,128)S(1)} %get-tuple-element.6), channel_id=1, source_target_pairs={{16,0},{32,16},{48,32},{64,48},{80,64},{96,80},{112,96},{128,112},... | collective-permute-start | bytes 98312 | tf_op jit(solution)/shard_map/ppermute | solution.py:222
  12.8 5.3 %collective-permute-start.2 = (f32[32,128]{1,0:T(8,128)}, f32[32,128]{1,0:T(8,128)S(1)}, u32[]{:S(2)}, u32[]{:S(2)}) collective-permute-start(f32[32,128]{1,0:T(8,128)} %get-tuple-element.4), channel_id=1, source_target_pairs={{0,1},{1,2},{2,3},{3,4},{4,5},{5,6},{6,7},{7,8},{8,9},{9,10},{10,1... | collective-permute-start | bytes 49160 | tf_op jit(solution)/shard_map/ppermute | solution.py:222
  15.9 6.8 %collective-permute-start.3 = (f32[32,128]{1,0:T(8,128)}, f32[32,128]{1,0:T(8,128)S(1)}, u32[]{:S(2)}, u32[]{:S(2)}) collective-permute-start(f32[32,128]{1,0:T(8,128)} %get-tuple-element.5), channel_id=1, source_target_pairs={{1,0},{2,1},{3,2},{4,3},{5,4},{6,5},{7,6},{8,7},{9,8},{10,9},{11,1... | collective-permute-start | bytes 49160 | tf_op jit(solution)/shard_map/ppermute | solution.py:222
  18.1 4.6 %copy-start.2 = (f32[32,128]{1,0:T(8,128)}, f32[32,128]{1,0:T(8,128)S(1)}, u32[]{:S(2)}) copy-start(f32[32,128]{1,0:T(8,128)S(1)} %collective-permute-done.2.left_ref) | copy-start | bytes 49156
  22.7 0.6 copy-start.3
  22.7 0.6 copy-start
  23.3 0.6 copy-start.1

commit v10 on v9

--- a/solution.py
+++ b/solution.py
@@ -183,34 +183,42 @@
     )(density, front, back, left, right, absorb)
 
 
-def edge_kernel(dens_ref, first_ref, last_ref):
-    depth, rows, cols = dens_ref.shape
+def edge_kernel(chunk, dens_ref, first_ref, last_ref):
+    _, rows, cols = dens_ref.shape
+    depth = first_ref.shape[1]
     lane = lax.broadcasted_iota(jnp.int32, (rows, depth), 1)
-
-    def step(x, carry):
+    start = pl.program_id(0) * chunk
+
+    @pl.when(pl.program_id(0) == 0)
+    def _():
+        first_ref[...] = jnp.zeros((rows, depth), jnp.float32)
+        last_ref[...] = jnp.zeros((rows, depth), jnp.float32)
+
+    def step(t, carry):
         first, last = carry
-        here = lane == x
-        low = dens_ref[x, :, 0:128]
-        high = dens_ref[x, :, cols - 128:cols]
+        here = lane == start + t
+        low = dens_ref[t, :, 0:128]
+        high = dens_ref[t, :, cols - 128:cols]
         first = jnp.where(here, jnp.broadcast_to(low[:, 0:1], (rows, depth)), first)
         last = jnp.where(here, jnp.broadcast_to(high[:, 127:128], (rows, depth)), last)
         return first, last
 
-    zero = jnp.zeros((rows, depth), jnp.float32)
-    first, last = lax.fori_loop(0, depth, step, (zero, zero), unroll=8)
+    first, last = lax.fori_loop(0, chunk, step, (first_ref[...], last_ref[...]), unroll=8)
     first_ref[...] = first
     last_ref[...] = last
 
 
 def edges(density):
     depth, rows, cols = density.shape
-    vmem = pltpu.MemorySpace.VMEM
+    chunk = 16 if depth % 16 == 0 else depth
     plane = jax.ShapeDtypeStruct((rows, depth), jnp.float32)
+    resident = pl.BlockSpec((rows, depth), lambda i: (0, 0))
     return pl.pallas_call(
-        edge_kernel,
+        functools.partial(edge_kernel, chunk),
         out_shape=(plane, plane),
-        in_specs=[pl.BlockSpec(memory_space=vmem)],
-        out_specs=(pl.BlockSpec(memory_space=vmem), pl.BlockSpec(memory_space=vmem)),
+        grid=(depth // chunk,),
+        in_specs=[pl.BlockSpec((chunk, rows, cols), lambda i: (i, 0, 0))],
+        out_specs=(resident, resident),
     )(density)
 
 

time: 62.4 us -> 63.6 us (1.019)
  Pallas kernels: 40.9 us -> 42.1 us
    pallas_call x1, Pallas kernels: 5.33 us -> 6.54 us  [edges(): pl.pallas_call(functools.partial(edge_kernel, chunk), out_shape=(plane, p...]
  transfers between devices with their start and end apart: 4 -> 4, of which waited for: 1 -> 1; matrix products, arithmetic and copies ran while one was open for 0% -> 0% of each run, Pallas kernels for 9% -> 10%
where the time goes in v10:
time: 63.6 us; the launch traced here: 63.2 us
  Pallas kernels  42.1 us (66%)
  starting transfers between devices  11.3 us (18%)
  waiting for transfers between devices  4.62 us (7%)
  local copies, waits for them, and re-layouts  4.48 us (7%)
  between operations  0.7 us (1%)
    pallas_call x1, Pallas kernels, march(): pl.pallas_call(functools.partial(march_kernel, depth - 1, n), out_shape=(...  35.6 us
    ppermute x4, starting transfers between devices, shifted(): return lax.ppermute(value, axis, pairs)  11.3 us
    pallas_call x1, Pallas kernels, edges(): pl.pallas_call(functools.partial(edge_kernel, chunk), out_shape=(plane, p...  6.54 us
    ppermute x4, waiting for transfers between devices, shifted(): return lax.ppermute(value, axis, pairs)  4.62 us
    unnamed x10, local copies, waits for them, and re-layouts  3.69 us
  transfers between devices with their start and end apart: 4, of which 1 were waited for; matrix products, arithmetic and copies ran while one was open for 0% of the time, Pallas kernels for 10%

profile of v10, /device:TPU:7, one launch (start us, length us, event | category | flops | bytes accessed | tf_op | source)
XLA Modules:
  0.0 63.2 jit_solution(474125541031460464)
XLA Ops:
  0.6 0.8 %slice_bitcast_fusion = (f32[32,256]{1,0:T(8,128)S(1)}, f32[32,256]{1,0:T(8,128)S(1)}) fusion(f32[128,32,256]{2,1,0:T(8,128)} %dens_ref.3), kind=kLoop, calls=%fused_computation | loop fusion | bytes 131072 | tf_op jit(solution)/shard_map/squeeze | solution.py:236
  1.4 4.1 %collective-permute-start = (f32[32,256]{1,0:T(8,128)S(1)}, f32[32,256]{1,0:T(8,128)S(1)}, u32[]{:S(2)}, u32[]{:S(2)}) collective-permute-start(f32[32,256]{1,0:T(8,128)S(1)} %get-tuple-element.7), channel_id=1, source_target_pairs={{0,16},{16,32},{32,48},{48,64},{64,80},{80,96},{96,112},{112,128},... | collective-permute-start | bytes 98312 | tf_op jit(solution)/shard_map/ppermute | solution.py:230
  5.5 1.9 %collective-permute-start.1 = (f32[32,256]{1,0:T(8,128)S(1)}, f32[32,256]{1,0:T(8,128)S(1)}, u32[]{:S(2)}, u32[]{:S(2)}) collective-permute-start(f32[32,256]{1,0:T(8,128)S(1)} %get-tuple-element.6), channel_id=1, source_target_pairs={{16,0},{32,16},{48,32},{64,48},{80,64},{96,80},{112,96},{128,112},... | collective-permute-start | bytes 98312 | tf_op jit(solution)/shard_map/ppermute | solution.py:230
  7.4 6.5 %shard_map.41 = (f32[32,128]{1,0:T(8,128)}, f32[32,128]{1,0:T(8,128)}) custom-call(f32[128,32,256]{2,1,0:T(8,128)} %dens_ref.3), custom_call_target="tpu_custom_call" | custom-call | tf_op jit(solution)/shard_map/pallas_call | solution.py:216
  14.0 3.1 %collective-permute-start.2 = (f32[32,128]{1,0:T(8,128)}, f32[32,128]{1,0:T(8,128)S(1)}, u32[]{:S(2)}, u32[]{:S(2)}) collective-permute-start(f32[32,128]{1,0:T(8,128)} %get-tuple-element.4), channel_id=1, source_target_pairs={{0,1},{1,2},{2,3},{3,4},{4,5},{5,6},{6,7},{7,8},{8,9},{9,10},{10,1... | collective-permute-start | bytes 49160 | tf_op jit(solution)/shard_map/ppermute | solution.py:230
  17.1 2.2 %collective-permute-start.3 = (f32[32,128]{1,0:T(8,128)}, f32[32,128]{1,0:T(8,128)S(1)}, u32[]{:S(2)}, u32[]{:S(2)}) collective-permute-start(f32[32,128]{1,0:T(8,128)} %get-tuple-element.5), channel_id=1, source_target_pairs={{1,0},{2,1},{3,2},{4,3},{5,4},{6,5},{7,6},{8,7},{9,8},{10,9},{11,1... | collective-permute-start | bytes 49160 | tf_op jit(solution)/shard_map/ppermute | solution.py:230
  19.3 0.0 collective-permute-done.2.left_ref
  19.3 0.0 copy-start.2
  19.3 4.6 %collective-permute-done.3.right_ref = f32[32,128]{1,0:T(8,128)S(1)} collective-permute-done((f32[32,128]{1,0:T(8,128)}, f32[32,128]{1,0:T(8,128)S(1)}, u32[]{:S(2)}, u32[]{:S(2)}) %collective-permute-start.3) | collective-permute-done | bytes 16416 | tf_op jit(solution)/shard_map/ppermute | solution.py:230
  23.9 0.0 copy-start.3
  23.9 0.0 collective-permute-done.front_ref
  23.9 0.0 copy-start
  23.9 0.0 collective-permute-done.1.back_ref
  23.9 0.0 copy-done.2
  23.9 0.6 copy-done.3
  24.5 0.0 copy-done
  24.5 0.0 copy-start.1
  24.5 0.6 copy-done.1
  25.1 35.6 %shard_map.42 = (f32[3,1,256]{2,1,0:T(1,128)}, f32[1,256]{1,0:T(1,128)}) custom-call(f32[128,32,256]{2,1,0:T(8,128)} %dens_ref.3, f32[32,256]{1,0:T(8,128)} %copy-done, f32[32,256]{1,0:T(8,128)} %copy-done.1, f32[32,128]{1,0:T(8,128)} %copy-done.2, f32[32,128]{1,0:T(8,128)} %copy-done.3, f32[32,256]{1,0:T(8,128)} %absorb_ref.1), custom_call_target="tpu_custom_call" | custom-call | tf_op jit(solution)/shard_map/pallas_call | solution.py:166
  60.8 1.2 %copy.6 = f32[3,1,256]{2,1,0:T(1,128)} copy(f32[3,1,256]{2,1,0:T(1,128)} %get-tuple-element.10) | data formatting | bytes 6144
  62.0 1.2 %copy.7 = f32[1,256]{1,0:T(1,128)} copy(f32[1,256]{1,0:T(1,128)} %get-tuple-element.11) | data formatting | bytes 2048
Async XLA Ops:
  1.4 22.5 %collective-permute-start = (f32[32,256]{1,0:T(8,128)S(1)}, f32[32,256]{1,0:T(8,128)S(1)}, u32[]{:S(2)}, u32[]{:S(2)}) collective-permute-start(f32[32,256]{1,0:T(8,128)S(1)} %get-tuple-element.7), channel_id=1, source_target_pairs={{0,16},{16,32},{32,48},{48,64},{64,80},{80,96},{96,112},{112,128},... | collective-permute-start | bytes 98312 | tf_op jit(solution)/shard_map/ppermute | solution.py:230
  5.5 18.4 %collective-permute-start.1 = (f32[32,256]{1,0:T(8,128)S(1)}, f32[32,256]{1,0:T(8,128)S(1)}, u32[]{:S(2)}, u32[]{:S(2)}) collective-permute-start(f32[32,256]{1,0:T(8,128)S(1)} %get-tuple-element.6), channel_id=1, source_target_pairs={{16,0},{32,16},{48,32},{64,48},{80,64},{96,80},{112,96},{128,112},... | collective-permute-start | bytes 98312 | tf_op jit(solution)/shard_map/ppermute | solution.py:230
  14.0 5.3 %collective-permute-start.2 = (f32[32,128]{1,0:T(8,128)}, f32[32,128]{1,0:T(8,128)S(1)}, u32[]{:S(2)}, u32[]{:S(2)}) collective-permute-start(f32[32,128]{1,0:T(8,128)} %get-tuple-element.4), channel_id=1, source_target_pairs={{0,1},{1,2},{2,3},{3,4},{4,5},{5,6},{6,7},{7,8},{8,9},{9,10},{10,1... | collective-permute-start | bytes 49160 | tf_op jit(solution)/shard_map/ppermute | solution.py:230
  17.1 6.8 %collective-permute-start.3 = (f32[32,128]{1,0:T(8,128)}, f32[32,128]{1,0:T(8,128)S(1)}, u32[]{:S(2)}, u32[]{:S(2)}) collective-permute-start(f32[32,128]{1,0:T(8,128)} %get-tuple-element.5), channel_id=1, source_target_pairs={{1,0},{2,1},{3,2},{4,3},{5,4},{6,5},{7,6},{8,7},{9,8},{10,9},{11,1... | collective-permute-start | bytes 49160 | tf_op jit(solution)/shard_map/ppermute | solution.py:230
  19.3 4.6 %copy-start.2 = (f32[32,128]{1,0:T(8,128)}, f32[32,128]{1,0:T(8,128)S(1)}, u32[]{:S(2)}) copy-start(f32[32,128]{1,0:T(8,128)S(1)} %collective-permute-done.2.left_ref) | copy-start | bytes 49156
  23.9 0.6 copy-start.3
  23.9 0.6 copy-start
  24.5 0.6 copy-start.1

commit v11 on v9

--- a/solution.py
+++ b/solution.py
@@ -185,21 +185,11 @@
 
 def edge_kernel(dens_ref, first_ref, last_ref):
     depth, rows, cols = dens_ref.shape
-    lane = lax.broadcasted_iota(jnp.int32, (rows, depth), 1)
-
-    def step(x, carry):
-        first, last = carry
-        here = lane == x
-        low = dens_ref[x, :, 0:128]
-        high = dens_ref[x, :, cols - 128:cols]
-        first = jnp.where(here, jnp.broadcast_to(low[:, 0:1], (rows, depth)), first)
-        last = jnp.where(here, jnp.broadcast_to(high[:, 127:128], (rows, depth)), last)
-        return first, last
-
-    zero = jnp.zeros((rows, depth), jnp.float32)
-    first, last = lax.fori_loop(0, depth, step, (zero, zero), unroll=8)
-    first_ref[...] = first
-    last_ref[...] = last
+    for z in range(rows):
+        low = jnp.transpose(dens_ref[:, z, 0:128])
+        high = jnp.transpose(dens_ref[:, z, cols - 128:cols])
+        first_ref[z:z + 1, :] = low[0:1, :]
+        last_ref[z:z + 1, :] = high[127:128, :]
 
 
 def edges(density):

time: 62.4 us -> 61.9 us (level)
  transfers between devices with their start and end apart: 4 -> 4, of which waited for: 1 -> 1; matrix products, arithmetic and copies ran while one was open for 0% -> 0% of each run, Pallas kernels for 9% -> 8%
where the time goes in v11:
time: 61.9 us; the launch traced here: 61.5 us
  Pallas kernels  40.4 us (65%)
  starting transfers between devices  11.3 us (18%)
  waiting for transfers between devices  4.62 us (7%)
  local copies, waits for them, and re-layouts  4.48 us (7%)
  between operations  0.7 us (1%)
    pallas_call x1, Pallas kernels, march(): pl.pallas_call(functools.partial(march_kernel, depth - 1, n), out_shape=(...  35.6 us
    ppermute x4, starting transfers between devices, shifted(): return lax.ppermute(value, axis, pairs)  11.3 us
    pallas_call x1, Pallas kernels, edges(): pl.pallas_call(edge_kernel, out_shape=(plane, plane), in_specs=[pl.BlockS...  4.81 us
    ppermute x4, waiting for transfers between devices, shifted(): return lax.ppermute(value, axis, pairs)  4.62 us
    unnamed x10, local copies, waits for them, and re-layouts  3.69 us
  transfers between devices with their start and end apart: 4, of which 1 were waited for; matrix products, arithmetic and copies ran while one was open for 0% of the time, Pallas kernels for 8%

profile of v11, /device:TPU:7, one launch (start us, length us, event | category | flops | bytes accessed | tf_op | source)
XLA Modules:
  0.0 61.5 jit_solution(6882625187732374591)
XLA Ops:
  0.6 0.8 %slice_bitcast_fusion = (f32[32,256]{1,0:T(8,128)S(1)}, f32[32,256]{1,0:T(8,128)S(1)}) fusion(f32[128,32,256]{2,1,0:T(8,128)} %dens_ref.3), kind=kLoop, calls=%fused_computation | loop fusion | bytes 131072 | tf_op jit(solution)/shard_map/squeeze | solution.py:218
  1.4 4.1 %collective-permute-start = (f32[32,256]{1,0:T(8,128)S(1)}, f32[32,256]{1,0:T(8,128)S(1)}, u32[]{:S(2)}, u32[]{:S(2)}) collective-permute-start(f32[32,256]{1,0:T(8,128)S(1)} %get-tuple-element.7), channel_id=1, source_target_pairs={{0,16},{16,32},{32,48},{48,64},{64,80},{80,96},{96,112},{112,128},... | collective-permute-start | bytes 98312 | tf_op jit(solution)/shard_map/ppermute | solution.py:212
  5.5 1.9 %collective-permute-start.1 = (f32[32,256]{1,0:T(8,128)S(1)}, f32[32,256]{1,0:T(8,128)S(1)}, u32[]{:S(2)}, u32[]{:S(2)}) collective-permute-start(f32[32,256]{1,0:T(8,128)S(1)} %get-tuple-element.6), channel_id=1, source_target_pairs={{16,0},{32,16},{48,32},{64,48},{80,64},{96,80},{112,96},{128,112},... | collective-permute-start | bytes 98312 | tf_op jit(solution)/shard_map/ppermute | solution.py:212
  7.4 4.8 %shard_map.41 = (f32[32,128]{1,0:T(8,128)}, f32[32,128]{1,0:T(8,128)}) custom-call(f32[128,32,256]{2,1,0:T(8,128)} %dens_ref.3), custom_call_target="tpu_custom_call" | custom-call | tf_op jit(solution)/shard_map/pallas_call | solution.py:199
  12.3 3.1 %collective-permute-start.2 = (f32[32,128]{1,0:T(8,128)}, f32[32,128]{1,0:T(8,128)S(1)}, u32[]{:S(2)}, u32[]{:S(2)}) collective-permute-start(f32[32,128]{1,0:T(8,128)} %get-tuple-element.4), channel_id=1, source_target_pairs={{0,1},{1,2},{2,3},{3,4},{4,5},{5,6},{6,7},{7,8},{8,9},{9,10},{10,1... | collective-permute-start | bytes 49160 | tf_op jit(solution)/shard_map/ppermute | solution.py:212
  15.4 2.2 %collective-permute-start.3 = (f32[32,128]{1,0:T(8,128)}, f32[32,128]{1,0:T(8,128)S(1)}, u32[]{:S(2)}, u32[]{:S(2)}) collective-permute-start(f32[32,128]{1,0:T(8,128)} %get-tuple-element.5), channel_id=1, source_target_pairs={{1,0},{2,1},{3,2},{4,3},{5,4},{6,5},{7,6},{8,7},{9,8},{10,9},{11,1... | collective-permute-start | bytes 49160 | tf_op jit(solution)/shard_map/ppermute | solution.py:212
  17.5 0.0 collective-permute-done.2.left_ref
  17.5 0.0 copy-start.2
  17.6 4.6 %collective-permute-done.3.right_ref = f32[32,128]{1,0:T(8,128)S(1)} collective-permute-done((f32[32,128]{1,0:T(8,128)}, f32[32,128]{1,0:T(8,128)S(1)}, u32[]{:S(2)}, u32[]{:S(2)}) %collective-permute-start.3) | collective-permute-done | bytes 16416 | tf_op jit(solution)/shard_map/ppermute | solution.py:212
  22.2 0.0 copy-start.3
  22.2 0.0 collective-permute-done.front_ref
  22.2 0.0 copy-start
  22.2 0.0 collective-permute-done.1.back_ref
  22.2 0.0 copy-done.2
  22.2 0.6 copy-done.3
  22.8 0.0 copy-done
  22.8 0.0 copy-start.1
  22.8 0.6 copy-done.1
  23.4 35.6 %shard_map.42 = (f32[3,1,256]{2,1,0:T(1,128)}, f32[1,256]{1,0:T(1,128)}) custom-call(f32[128,32,256]{2,1,0:T(8,128)} %dens_ref.3, f32[32,256]{1,0:T(8,128)} %copy-done, f32[32,256]{1,0:T(8,128)} %copy-done.1, f32[32,128]{1,0:T(8,128)} %copy-done.2, f32[32,128]{1,0:T(8,128)} %copy-done.3, f32[32,256]{1,0:T(8,128)} %absorb_ref.1), custom_call_target="tpu_custom_call" | custom-call | tf_op jit(solution)/shard_map/pallas_call | solution.py:166
  59.0 1.2 %copy.6 = f32[3,1,256]{2,1,0:T(1,128)} copy(f32[3,1,256]{2,1,0:T(1,128)} %get-tuple-element.10) | data formatting | bytes 6144
  60.3 1.2 %copy.7 = f32[1,256]{1,0:T(1,128)} copy(f32[1,256]{1,0:T(1,128)} %get-tuple-element.11) | data formatting | bytes 2048
Async XLA Ops:
  1.4 20.8 %collective-permute-start = (f32[32,256]{1,0:T(8,128)S(1)}, f32[32,256]{1,0:T(8,128)S(1)}, u32[]{:S(2)}, u32[]{:S(2)}) collective-permute-start(f32[32,256]{1,0:T(8,128)S(1)} %get-tuple-element.7), channel_id=1, source_target_pairs={{0,16},{16,32},{32,48},{48,64},{64,80},{80,96},{96,112},{112,128},... | collective-permute-start | bytes 98312 | tf_op jit(solution)/shard_map/ppermute | solution.py:212
  5.5 16.7 %collective-permute-start.1 = (f32[32,256]{1,0:T(8,128)S(1)}, f32[32,256]{1,0:T(8,128)S(1)}, u32[]{:S(2)}, u32[]{:S(2)}) collective-permute-start(f32[32,256]{1,0:T(8,128)S(1)} %get-tuple-element.6), channel_id=1, source_target_pairs={{16,0},{32,16},{48,32},{64,48},{80,64},{96,80},{112,96},{128,112},... | collective-permute-start | bytes 98312 | tf_op jit(solution)/shard_map/ppermute | solution.py:212
  12.3 5.3 %collective-permute-start.2 = (f32[32,128]{1,0:T(8,128)}, f32[32,128]{1,0:T(8,128)S(1)}, u32[]{:S(2)}, u32[]{:S(2)}) collective-permute-start(f32[32,128]{1,0:T(8,128)} %get-tuple-element.4), channel_id=1, source_target_pairs={{0,1},{1,2},{2,3},{3,4},{4,5},{5,6},{6,7},{7,8},{8,9},{9,10},{10,1... | collective-permute-start | bytes 49160 | tf_op jit(solution)/shard_map/ppermute | solution.py:212
  15.4 6.8 %collective-permute-start.3 = (f32[32,128]{1,0:T(8,128)}, f32[32,128]{1,0:T(8,128)S(1)}, u32[]{:S(2)}, u32[]{:S(2)}) collective-permute-start(f32[32,128]{1,0:T(8,128)} %get-tuple-element.5), channel_id=1, source_target_pairs={{1,0},{2,1},{3,2},{4,3},{5,4},{6,5},{7,6},{8,7},{9,8},{10,9},{11,1... | collective-permute-start | bytes 49160 | tf_op jit(solution)/shard_map/ppermute | solution.py:212
  17.5 4.6 %copy-start.2 = (f32[32,128]{1,0:T(8,128)}, f32[32,128]{1,0:T(8,128)S(1)}, u32[]{:S(2)}) copy-start(f32[32,128]{1,0:T(8,128)S(1)} %collective-permute-done.2.left_ref) | copy-start | bytes 49156
  22.2 0.6 copy-start.3
  22.2 0.6 %copy-start = (f32[32,256]{1,0:T(8,128)}, f32[32,256]{1,0:T(8,128)S(1)}, u32[]{:S(2)}) copy-start(f32[32,256]{1,0:T(8,128)S(1)} %collective-permute-done.front_ref) | copy-start | bytes 98308
  22.8 0.6 copy-start.1

commit v12 on v11

--- a/solution.py
+++ b/solution.py
@@ -16,7 +16,8 @@
 
 
 def march_kernel(last, n, dens_ref, front_ref, back_ref, left_ref, right_ref, absorb_ref,
-                 colour_ref, transmit_ref, out_ref, part, recv, send_sems, recv_sems, local_sem):
+                 colour_ref, transmit_ref, out_ref, part, mixed, recv_pair, recv,
+                 send_pair, got_pair, send_sems, recv_sems, local_sem):
     rows, cols = dens_ref.shape[1], dens_ref.shape[2]
     shape = (rows, 128)
     lane = lax.broadcasted_iota(jnp.int32, shape, 1)
@@ -28,11 +29,18 @@
     col = lax.axis_index("gy")
     barrier = pltpu.get_barrier_semaphore()
 
+    pairs = n // 2
+    parity = lax.rem(me, 2)
+    chip = me // 2
+    sems = (send_pair, got_pair, send_sems, recv_sems, local_sem)
+
     def greet(i, carry):
-        pl.semaphore_signal(barrier, inc=1, device_id=(lax.rem(me + i, n), col), device_id_type=MESH_ID)
-        return carry
-
-    lax.fori_loop(1, n, greet, 0)
+        peer = 2 * lax.rem(chip + i, pairs) + parity
+        pl.semaphore_signal(barrier, inc=1, device_id=(peer, col), device_id_type=MESH_ID)
+        return carry
+
+    pl.semaphore_signal(barrier, inc=1, device_id=(me + 1 - 2 * parity, col), device_id_type=MESH_ID)
+    lax.fori_loop(1, pairs, greet, 0)
     for h in range(halves):
         lanes = slice(h * 128, (h + 1) * 128)
         left_lanes = slice((h - 1) * 128, h * 128) if h > 0 else None
@@ -95,45 +103,91 @@
         out_ref[3, :, lanes] = absorb * softsum
 
     share = rows // n
+    pairs = n // 2
     for z in range(rows):
+        owner = z // share
+        slot = (owner % 2) * pairs + owner // 2
         for k in range(4):
             for h in range(halves):
                 r = ((z % share) * 4 + k) * halves + h
-                part[z // share, r:r + 1, :] = out_ref[k, z:z + 1, h * 128:(h + 1) * 128]
-    exchange_and_combine(n, share, halves, me, col, barrier, part, recv, send_sems, recv_sems,
-                         local_sem, colour_ref, transmit_ref)
-
-
-def exchange_and_combine(n, share, halves, me, col, barrier, part, recv, send_sems, recv_sems,
-                         local_sem, colour_ref, transmit_ref):
-    def link(peer, slot):
+                part[slot, r:r + 1, :] = out_ref[k, z:z + 1, h * 128:(h + 1) * 128]
+    exchange_and_combine(n, share, halves, me, col, barrier, part, mixed, recv_pair, recv,
+                         sems, colour_ref, transmit_ref)
+
+
+def merge(front, back, share, halves):
+    def rows_of(k):
+        return [(r * 4 + k) * halves + h for r in range(share) for h in range(halves)]
+
+    seen = jnp.exp(-jnp.concatenate([front[i:i + 1] for i in rows_of(3)], axis=0))
+    pieces = [None] * (share * 4 * halves)
+    for k in range(4):
+        idx = rows_of(k)
+        f = jnp.concatenate([front[i:i + 1] for i in idx], axis=0)
+        b = jnp.concatenate([back[i:i + 1] for i in idx], axis=0)
+        merged = f + b if k == 3 else f + seen * b
+        for j, i in enumerate(idx):
+            pieces[i] = merged[j:j + 1]
+    return jnp.concatenate(pieces, axis=0)
+
+
+def exchange_and_combine(n, share, halves, me, col, barrier, part, mixed, recv_pair, recv,
+                         sems, colour_ref, transmit_ref):
+    pairs = n // 2
+    parity = lax.rem(me, 2)
+    partner = me + 1 - 2 * parity
+    chip = me // 2
+    send_pair, got_pair, send_sems, recv_sems, local_sem = sems
+    pl.semaphore_wait(barrier, pairs)
+
+    swap = pltpu.make_async_remote_copy(
+        src_ref=part.at[pl.ds((1 - parity) * pairs, pairs)],
+        dst_ref=recv_pair,
+        send_sem=send_pair,
+        recv_sem=got_pair,
+        device_id=(partner, col),
+        device_id_type=MESH_ID,
+    )
+    swap.start()
+    swap.wait()
+
+    def combine_pair(j, carry):
+        mine = part[parity * pairs + j]
+        theirs = recv_pair[j]
+        first = parity == 0
+        front = jnp.where(first, mine, theirs)
+        back = jnp.where(first, theirs, mine)
+        mixed[j] = merge(front, back, share, halves)
+        return carry
+
+    lax.fori_loop(0, pairs, combine_pair, 0)
+
+    def link(j, slot):
         return pltpu.make_async_remote_copy(
-            src_ref=part.at[peer],
+            src_ref=mixed.at[j],
             dst_ref=recv.at[slot],
-            send_sem=send_sems.at[peer],
+            send_sem=send_sems.at[j],
             recv_sem=recv_sems.at[slot],
-            device_id=(peer, col),
+            device_id=(2 * j + parity, col),
             device_id_type=MESH_ID,
         )
 
-    pl.semaphore_wait(barrier, n - 1)
-
     def send(i, carry):
-        link(lax.rem(me + i, n), me).start()
-        return carry
-
-    lax.fori_loop(1, n, send, 0)
-    own = pltpu.make_async_copy(part.at[me], recv.at[me], local_sem)
+        link(lax.rem(chip + i, pairs), chip).start()
+        return carry
+
+    lax.fori_loop(1, pairs, send, 0)
+    own = pltpu.make_async_copy(mixed.at[chip], recv.at[chip], local_sem)
     own.start()
     own.wait()
 
     def finish(i, carry):
-        peer = lax.rem(me + i, n)
-        link(peer, peer).wait_send()
-        link(peer, peer).wait_recv()
-        return carry
-
-    lax.fori_loop(1, n, finish, 0)
+        j = lax.rem(chip + i, pairs)
+        link(j, j).wait_send()
+        link(j, j).wait_recv()
+        return carry
+
+    lax.fori_loop(1, pairs, finish, 0)
     cols = colour_ref.shape[-1]
     zero = jnp.zeros((share * halves, 128), jnp.float32)
 
@@ -152,7 +206,7 @@
             c2 + value(block, 2) * seen,
         )
 
-    front, c0, c1, c2 = lax.fori_loop(0, n, accumulate, (zero, zero, zero, zero))
+    front, c0, c1, c2 = lax.fori_loop(0, pairs, accumulate, (zero, zero, zero, zero))
     for k, c in enumerate((c0, c1, c2)):
         colour_ref[k] = c.reshape(share, cols)
     transmit_ref[...] = jnp.exp(-front).reshape(share, cols)
@@ -162,6 +216,7 @@
     depth, rows, cols = density.shape
     share = rows // n
     tiles = (n, share * 4 * cols // 128, 128)
+    half_tiles = (n // 2,) + tiles[1:]
     vmem = pltpu.MemorySpace.VMEM
     return pl.pallas_call(
         functools.partial(march_kernel, depth - 1, n),
@@ -174,9 +229,13 @@
         scratch_shapes=[
             pltpu.VMEM((4, rows, cols), jnp.float32),
             pltpu.VMEM(tiles, jnp.float32),
-            pltpu.VMEM(tiles, jnp.float32),
-            pltpu.SemaphoreType.DMA((n,)),
-            pltpu.SemaphoreType.DMA((n,)),
+            pltpu.VMEM(half_tiles, jnp.float32),
+            pltpu.VMEM(half_tiles, jnp.float32),
+            pltpu.VMEM(half_tiles, jnp.float32),
+            pltpu.SemaphoreType.DMA,
+            pltpu.SemaphoreType.DMA,
+            pltpu.SemaphoreType.DMA((n // 2,)),
+            pltpu.SemaphoreType.DMA((n // 2,)),
             pltpu.SemaphoreType.DMA,
         ],
         compiler_params=pltpu.CompilerParams(collective_id=0, has_side_effects=True),

time: 61.9 us -> 60.5 us (0.977)
  Pallas kernels: 40.4 us -> 39 us
    pallas_call x1, Pallas kernels: 35.6 us -> 34.2 us  [march(): pl.pallas_call(functools.partial(march_kernel, depth - 1, n), out_shape=(...]
where the time goes in v12:
time: 60.5 us; the launch traced here: 60.1 us
  Pallas kernels  39 us (64%)
  starting transfers between devices  11.3 us (19%)
  waiting for transfers between devices  4.62 us (8%)
  local copies, waits for them, and re-layouts  4.48 us (7%)
  between operations  0.7 us (1%)
    pallas_call x1, Pallas kernels, march(): pl.pallas_call(functools.partial(march_kernel, depth - 1, n), out_shape=(...  34.2 us
    ppermute x4, starting transfers between devices, shifted(): return lax.ppermute(value, axis, pairs)  11.3 us
    pallas_call x1, Pallas kernels, edges(): pl.pallas_call(edge_kernel, out_shape=(plane, plane), in_specs=[pl.BlockS...  4.81 us
    ppermute x4, waiting for transfers between devices, shifted(): return lax.ppermute(value, axis, pairs)  4.62 us
    unnamed x10, local copies, waits for them, and re-layouts  3.69 us
  transfers between devices with their start and end apart: 4, of which 1 were waited for; matrix products, arithmetic and copies ran while one was open for 0% of the time, Pallas kernels for 8%

profile of v12, /device:TPU:7, one launch (start us, length us, event | category | flops | bytes accessed | tf_op | source)
XLA Modules:
  0.0 60.1 jit_solution(5484291315359798539)
XLA Ops:
  0.6 0.8 %slice_bitcast_fusion = (f32[32,256]{1,0:T(8,128)S(1)}, f32[32,256]{1,0:T(8,128)S(1)}) fusion(f32[128,32,256]{2,1,0:T(8,128)} %dens_ref.3), kind=kLoop, calls=%fused_computation | loop fusion | bytes 131072 | tf_op jit(solution)/shard_map/squeeze | solution.py:277
  1.4 4.1 %collective-permute-start = (f32[32,256]{1,0:T(8,128)S(1)}, f32[32,256]{1,0:T(8,128)S(1)}, u32[]{:S(2)}, u32[]{:S(2)}) collective-permute-start(f32[32,256]{1,0:T(8,128)S(1)} %get-tuple-element.7), channel_id=1, source_target_pairs={{0,16},{16,32},{32,48},{48,64},{64,80},{80,96},{96,112},{112,128},... | collective-permute-start | bytes 98312 | tf_op jit(solution)/shard_map/ppermute | solution.py:271
  5.5 1.9 %collective-permute-start.1 = (f32[32,256]{1,0:T(8,128)S(1)}, f32[32,256]{1,0:T(8,128)S(1)}, u32[]{:S(2)}, u32[]{:S(2)}) collective-permute-start(f32[32,256]{1,0:T(8,128)S(1)} %get-tuple-element.6), channel_id=1, source_target_pairs={{16,0},{32,16},{48,32},{64,48},{80,64},{96,80},{112,96},{128,112},... | collective-permute-start | bytes 98312 | tf_op jit(solution)/shard_map/ppermute | solution.py:271
  7.4 4.8 %shard_map.41 = (f32[32,128]{1,0:T(8,128)}, f32[32,128]{1,0:T(8,128)}) custom-call(f32[128,32,256]{2,1,0:T(8,128)} %dens_ref.3), custom_call_target="tpu_custom_call" | custom-call | tf_op jit(solution)/shard_map/pallas_call | solution.py:258
  12.3 3.1 %collective-permute-start.2 = (f32[32,128]{1,0:T(8,128)}, f32[32,128]{1,0:T(8,128)S(1)}, u32[]{:S(2)}, u32[]{:S(2)}) collective-permute-start(f32[32,128]{1,0:T(8,128)} %get-tuple-element.4), channel_id=1, source_target_pairs={{0,1},{1,2},{2,3},{3,4},{4,5},{5,6},{6,7},{7,8},{8,9},{9,10},{10,1... | collective-permute-start | bytes 49160 | tf_op jit(solution)/shard_map/ppermute | solution.py:271
  15.4 2.2 %collective-permute-start.3 = (f32[32,128]{1,0:T(8,128)}, f32[32,128]{1,0:T(8,128)S(1)}, u32[]{:S(2)}, u32[]{:S(2)}) collective-permute-start(f32[32,128]{1,0:T(8,128)} %get-tuple-element.5), channel_id=1, source_target_pairs={{1,0},{2,1},{3,2},{4,3},{5,4},{6,5},{7,6},{8,7},{9,8},{10,9},{11,1... | collective-permute-start | bytes 49160 | tf_op jit(solution)/shard_map/ppermute | solution.py:271
  17.5 0.0 collective-permute-done.2.left_ref
  17.5 0.0 copy-start.2
  17.6 4.6 %collective-permute-done.3.right_ref = f32[32,128]{1,0:T(8,128)S(1)} collective-permute-done((f32[32,128]{1,0:T(8,128)}, f32[32,128]{1,0:T(8,128)S(1)}, u32[]{:S(2)}, u32[]{:S(2)}) %collective-permute-start.3) | collective-permute-done | bytes 16416 | tf_op jit(solution)/shard_map/ppermute | solution.py:271
  22.2 0.0 copy-start.3
  22.2 0.0 collective-permute-done.front_ref
  22.2 0.0 copy-start
  22.2 0.0 collective-permute-done.1.back_ref
  22.2 0.0 copy-done.2
  22.2 0.6 copy-done.3
  22.8 0.0 copy-done
  22.8 0.0 copy-start.1
  22.8 0.6 %copy-done.1 = f32[32,256]{1,0:T(8,128)} copy-done((f32[32,256]{1,0:T(8,128)}, f32[32,256]{1,0:T(8,128)S(1)}, u32[]{:S(2)}) %copy-start.1) | copy-done | bytes 32792
  23.4 34.2 %shard_map.42 = (f32[3,1,256]{2,1,0:T(1,128)}, f32[1,256]{1,0:T(1,128)}) custom-call(f32[128,32,256]{2,1,0:T(8,128)} %dens_ref.3, f32[32,256]{1,0:T(8,128)} %copy-done, f32[32,256]{1,0:T(8,128)} %copy-done.1, f32[32,128]{1,0:T(8,128)} %copy-done.2, f32[32,128]{1,0:T(8,128)} %copy-done.3, f32[32,256]{1,0:T(8,128)} %absorb_ref.1), custom_call_target="tpu_custom_call" | custom-call | tf_op jit(solution)/shard_map/pallas_call | solution.py:221
  57.6 1.2 %copy.6 = f32[3,1,256]{2,1,0:T(1,128)} copy(f32[3,1,256]{2,1,0:T(1,128)} %get-tuple-element.10) | data formatting | bytes 6144
  58.8 1.2 %copy.7 = f32[1,256]{1,0:T(1,128)} copy(f32[1,256]{1,0:T(1,128)} %get-tuple-element.11) | data formatting | bytes 2048
Async XLA Ops:
  1.4 20.8 %collective-permute-start = (f32[32,256]{1,0:T(8,128)S(1)}, f32[32,256]{1,0:T(8,128)S(1)}, u32[]{:S(2)}, u32[]{:S(2)}) collective-permute-start(f32[32,256]{1,0:T(8,128)S(1)} %get-tuple-element.7), channel_id=1, source_target_pairs={{0,16},{16,32},{32,48},{48,64},{64,80},{80,96},{96,112},{112,128},... | collective-permute-start | bytes 98312 | tf_op jit(solution)/shard_map/ppermute | solution.py:271
  5.5 16.7 %collective-permute-start.1 = (f32[32,256]{1,0:T(8,128)S(1)}, f32[32,256]{1,0:T(8,128)S(1)}, u32[]{:S(2)}, u32[]{:S(2)}) collective-permute-start(f32[32,256]{1,0:T(8,128)S(1)} %get-tuple-element.6), channel_id=1, source_target_pairs={{16,0},{32,16},{48,32},{64,48},{80,64},{96,80},{112,96},{128,112},... | collective-permute-start | bytes 98312 | tf_op jit(solution)/shard_map/ppermute | solution.py:271
  12.3 5.3 %collective-permute-start.2 = (f32[32,128]{1,0:T(8,128)}, f32[32,128]{1,0:T(8,128)S(1)}, u32[]{:S(2)}, u32[]{:S(2)}) collective-permute-start(f32[32,128]{1,0:T(8,128)} %get-tuple-element.4), channel_id=1, source_target_pairs={{0,1},{1,2},{2,3},{3,4},{4,5},{5,6},{6,7},{7,8},{8,9},{9,10},{10,1... | collective-permute-start | bytes 49160 | tf_op jit(solution)/shard_map/ppermute | solution.py:271
  15.4 6.8 %collective-permute-start.3 = (f32[32,128]{1,0:T(8,128)}, f32[32,128]{1,0:T(8,128)S(1)}, u32[]{:S(2)}, u32[]{:S(2)}) collective-permute-start(f32[32,128]{1,0:T(8,128)} %get-tuple-element.5), channel_id=1, source_target_pairs={{1,0},{2,1},{3,2},{4,3},{5,4},{6,5},{7,6},{8,7},{9,8},{10,9},{11,1... | collective-permute-start | bytes 49160 | tf_op jit(solution)/shard_map/ppermute | solution.py:271
  17.5 4.6 %copy-start.2 = (f32[32,128]{1,0:T(8,128)}, f32[32,128]{1,0:T(8,128)S(1)}, u32[]{:S(2)}) copy-start(f32[32,128]{1,0:T(8,128)S(1)} %collective-permute-done.2.left_ref) | copy-start | bytes 49156
  22.2 0.6 copy-start.3
  22.2 0.6 %copy-start = (f32[32,256]{1,0:T(8,128)}, f32[32,256]{1,0:T(8,128)S(1)}, u32[]{:S(2)}) copy-start(f32[32,256]{1,0:T(8,128)S(1)} %collective-permute-done.front_ref) | copy-start | bytes 98308
  22.8 0.6 %copy-start.1 = (f32[32,256]{1,0:T(8,128)}, f32[32,256]{1,0:T(8,128)S(1)}, u32[]{:S(2)}) copy-start(f32[32,256]{1,0:T(8,128)S(1)} %collective-permute-done.1.back_ref) | copy-start | bytes 98308

commit v13 on v12

--- a/solution.py
+++ b/solution.py
@@ -96,7 +96,7 @@
         zero = jnp.zeros(shape, jnp.float32)
         one = jnp.ones(shape, jnp.float32)
         _, total, t0, t1, t2, softsum = lax.fori_loop(
-            0, last + 1, step, (one, zero, zero, zero, zero, zero), unroll=4
+            0, last + 1, step, (one, zero, zero, zero, zero, zero), unroll=8
         )
         for k, value in enumerate((t0, t1, t2)):
             out_ref[k, :, lanes] = 0.5 * (total + value)

time: 60.5 us -> 58.6 us (0.969)
  Pallas kernels: 39 us -> 37.1 us
    pallas_call x1, Pallas kernels: 34.2 us -> 32.3 us  [march(): pl.pallas_call(functools.partial(march_kernel, depth - 1, n), out_shape=(...]
where the time goes in v13:
time: 58.6 us; the launch traced here: 58.1 us
  Pallas kernels  37.1 us (63%)
  starting transfers between devices  11.3 us (19%)
  waiting for transfers between devices  4.62 us (8%)
  local copies, waits for them, and re-layouts  4.48 us (8%)
  between operations  0.7 us (1%)
    pallas_call x1, Pallas kernels, march(): pl.pallas_call(functools.partial(march_kernel, depth - 1, n), out_shape=(...  32.3 us
    ppermute x4, starting transfers between devices, shifted(): return lax.ppermute(value, axis, pairs)  11.3 us
    pallas_call x1, Pallas kernels, edges(): pl.pallas_call(edge_kernel, out_shape=(plane, plane), in_specs=[pl.BlockS...  4.81 us
    ppermute x4, waiting for transfers between devices, shifted(): return lax.ppermute(value, axis, pairs)  4.62 us
    unnamed x10, local copies, waits for them, and re-layouts  3.69 us
  transfers between devices with their start and end apart: 4, of which 1 were waited for; matrix products, arithmetic and copies ran while one was open for 0% of the time, Pallas kernels for 8%

profile of v13, /device:TPU:7, one launch (start us, length us, event | category | flops | bytes accessed | tf_op | source)
XLA Modules:
  0.0 58.1 jit_solution(11749168219052498067)
XLA Ops:
  0.6 0.8 %slice_bitcast_fusion = (f32[32,256]{1,0:T(8,128)S(1)}, f32[32,256]{1,0:T(8,128)S(1)}) fusion(f32[128,32,256]{2,1,0:T(8,128)} %dens_ref.3), kind=kLoop, calls=%fused_computation | loop fusion | bytes 131072 | tf_op jit(solution)/shard_map/squeeze | solution.py:277
  1.4 4.1 %collective-permute-start = (f32[32,256]{1,0:T(8,128)S(1)}, f32[32,256]{1,0:T(8,128)S(1)}, u32[]{:S(2)}, u32[]{:S(2)}) collective-permute-start(f32[32,256]{1,0:T(8,128)S(1)} %get-tuple-element.7), channel_id=1, source_target_pairs={{0,16},{16,32},{32,48},{48,64},{64,80},{80,96},{96,112},{112,128},... | collective-permute-start | bytes 98312 | tf_op jit(solution)/shard_map/ppermute | solution.py:271
  5.5 1.9 %collective-permute-start.1 = (f32[32,256]{1,0:T(8,128)S(1)}, f32[32,256]{1,0:T(8,128)S(1)}, u32[]{:S(2)}, u32[]{:S(2)}) collective-permute-start(f32[32,256]{1,0:T(8,128)S(1)} %get-tuple-element.6), channel_id=1, source_target_pairs={{16,0},{32,16},{48,32},{64,48},{80,64},{96,80},{112,96},{128,112},... | collective-permute-start | bytes 98312 | tf_op jit(solution)/shard_map/ppermute | solution.py:271
  7.4 4.8 %shard_map.41 = (f32[32,128]{1,0:T(8,128)}, f32[32,128]{1,0:T(8,128)}) custom-call(f32[128,32,256]{2,1,0:T(8,128)} %dens_ref.3), custom_call_target="tpu_custom_call" | custom-call | tf_op jit(solution)/shard_map/pallas_call | solution.py:258
  12.3 3.1 %collective-permute-start.2 = (f32[32,128]{1,0:T(8,128)}, f32[32,128]{1,0:T(8,128)S(1)}, u32[]{:S(2)}, u32[]{:S(2)}) collective-permute-start(f32[32,128]{1,0:T(8,128)} %get-tuple-element.4), channel_id=1, source_target_pairs={{0,1},{1,2},{2,3},{3,4},{4,5},{5,6},{6,7},{7,8},{8,9},{9,10},{10,1... | collective-permute-start | bytes 49160 | tf_op jit(solution)/shard_map/ppermute | solution.py:271
  15.4 2.2 %collective-permute-start.3 = (f32[32,128]{1,0:T(8,128)}, f32[32,128]{1,0:T(8,128)S(1)}, u32[]{:S(2)}, u32[]{:S(2)}) collective-permute-start(f32[32,128]{1,0:T(8,128)} %get-tuple-element.5), channel_id=1, source_target_pairs={{1,0},{2,1},{3,2},{4,3},{5,4},{6,5},{7,6},{8,7},{9,8},{10,9},{11,1... | collective-permute-start | bytes 49160 | tf_op jit(solution)/shard_map/ppermute | solution.py:271
  17.5 0.0 collective-permute-done.2.left_ref
  17.5 0.0 copy-start.2
  17.6 4.6 %collective-permute-done.3.right_ref = f32[32,128]{1,0:T(8,128)S(1)} collective-permute-done((f32[32,128]{1,0:T(8,128)}, f32[32,128]{1,0:T(8,128)S(1)}, u32[]{:S(2)}, u32[]{:S(2)}) %collective-permute-start.3) | collective-permute-done | bytes 16416 | tf_op jit(solution)/shard_map/ppermute | solution.py:271
  22.2 0.0 copy-start.3
  22.2 0.0 collective-permute-done.front_ref
  22.2 0.0 copy-start
  22.2 0.0 collective-permute-done.1.back_ref
  22.2 0.0 copy-done.2
  22.2 0.6 copy-done.3
  22.8 0.0 copy-done
  22.8 0.0 copy-start.1
  22.8 0.6 %copy-done.1 = f32[32,256]{1,0:T(8,128)} copy-done((f32[32,256]{1,0:T(8,128)}, f32[32,256]{1,0:T(8,128)S(1)}, u32[]{:S(2)}) %copy-start.1) | copy-done | bytes 32792
  23.4 32.3 %shard_map.42 = (f32[3,1,256]{2,1,0:T(1,128)}, f32[1,256]{1,0:T(1,128)}) custom-call(f32[128,32,256]{2,1,0:T(8,128)} %dens_ref.3, f32[32,256]{1,0:T(8,128)} %copy-done, f32[32,256]{1,0:T(8,128)} %copy-done.1, f32[32,128]{1,0:T(8,128)} %copy-done.2, f32[32,128]{1,0:T(8,128)} %copy-done.3, f32[32,256]{1,0:T(8,128)} %absorb_ref.1), custom_call_target="tpu_custom_call" | custom-call | tf_op jit(solution)/shard_map/pallas_call | solution.py:221
  55.7 1.2 %copy.6 = f32[3,1,256]{2,1,0:T(1,128)} copy(f32[3,1,256]{2,1,0:T(1,128)} %get-tuple-element.10) | data formatting | bytes 6144
  56.9 1.2 %copy.7 = f32[1,256]{1,0:T(1,128)} copy(f32[1,256]{1,0:T(1,128)} %get-tuple-element.11) | data formatting | bytes 2048
Async XLA Ops:
  1.4 20.8 %collective-permute-start = (f32[32,256]{1,0:T(8,128)S(1)}, f32[32,256]{1,0:T(8,128)S(1)}, u32[]{:S(2)}, u32[]{:S(2)}) collective-permute-start(f32[32,256]{1,0:T(8,128)S(1)} %get-tuple-element.7), channel_id=1, source_target_pairs={{0,16},{16,32},{32,48},{48,64},{64,80},{80,96},{96,112},{112,128},... | collective-permute-start | bytes 98312 | tf_op jit(solution)/shard_map/ppermute | solution.py:271
  5.5 16.7 %collective-permute-start.1 = (f32[32,256]{1,0:T(8,128)S(1)}, f32[32,256]{1,0:T(8,128)S(1)}, u32[]{:S(2)}, u32[]{:S(2)}) collective-permute-start(f32[32,256]{1,0:T(8,128)S(1)} %get-tuple-element.6), channel_id=1, source_target_pairs={{16,0},{32,16},{48,32},{64,48},{80,64},{96,80},{112,96},{128,112},... | collective-permute-start | bytes 98312 | tf_op jit(solution)/shard_map/ppermute | solution.py:271
  12.3 5.3 %collective-permute-start.2 = (f32[32,128]{1,0:T(8,128)}, f32[32,128]{1,0:T(8,128)S(1)}, u32[]{:S(2)}, u32[]{:S(2)}) collective-permute-start(f32[32,128]{1,0:T(8,128)} %get-tuple-element.4), channel_id=1, source_target_pairs={{0,1},{1,2},{2,3},{3,4},{4,5},{5,6},{6,7},{7,8},{8,9},{9,10},{10,1... | collective-permute-start | bytes 49160 | tf_op jit(solution)/shard_map/ppermute | solution.py:271
  15.4 6.8 %collective-permute-start.3 = (f32[32,128]{1,0:T(8,128)}, f32[32,128]{1,0:T(8,128)S(1)}, u32[]{:S(2)}, u32[]{:S(2)}) collective-permute-start(f32[32,128]{1,0:T(8,128)} %get-tuple-element.5), channel_id=1, source_target_pairs={{1,0},{2,1},{3,2},{4,3},{5,4},{6,5},{7,6},{8,7},{9,8},{10,9},{11,1... | collective-permute-start | bytes 49160 | tf_op jit(solution)/shard_map/ppermute | solution.py:271
  17.5 4.6 %copy-start.2 = (f32[32,128]{1,0:T(8,128)}, f32[32,128]{1,0:T(8,128)S(1)}, u32[]{:S(2)}) copy-start(f32[32,128]{1,0:T(8,128)S(1)} %collective-permute-done.2.left_ref) | copy-start | bytes 49156
  22.2 0.6 %copy-start.3 = (f32[32,128]{1,0:T(8,128)}, f32[32,128]{1,0:T(8,128)S(1)}, u32[]{:S(2)}) copy-start(f32[32,128]{1,0:T(8,128)S(1)} %collective-permute-done.3.right_ref) | copy-start | bytes 49156
  22.2 0.6 %copy-start = (f32[32,256]{1,0:T(8,128)}, f32[32,256]{1,0:T(8,128)S(1)}, u32[]{:S(2)}) copy-start(f32[32,256]{1,0:T(8,128)S(1)} %collective-permute-done.front_ref) | copy-start | bytes 98308
  22.8 0.6 %copy-start.1 = (f32[32,256]{1,0:T(8,128)}, f32[32,256]{1,0:T(8,128)S(1)}, u32[]{:S(2)}) copy-start(f32[32,256]{1,0:T(8,128)S(1)} %collective-permute-done.1.back_ref) | copy-start | bytes 98308

commit v14 on v13

--- a/solution.py
+++ b/solution.py
@@ -96,7 +96,7 @@
         zero = jnp.zeros(shape, jnp.float32)
         one = jnp.ones(shape, jnp.float32)
         _, total, t0, t1, t2, softsum = lax.fori_loop(
-            0, last + 1, step, (one, zero, zero, zero, zero, zero), unroll=8
+            0, last + 1, step, (one, zero, zero, zero, zero, zero), unroll=16
         )
         for k, value in enumerate((t0, t1, t2)):
             out_ref[k, :, lanes] = 0.5 * (total + value)

time: 58.6 us -> 58.4 us (level)
  no operation moved by 1% of the time
where the time goes in v14:
time: 58.4 us; the launch traced here: 58 us
  Pallas kernels  36.9 us (63%)
  starting transfers between devices  11.3 us (19%)
  waiting for transfers between devices  4.62 us (8%)
  local copies, waits for them, and re-layouts  4.48 us (8%)
  between operations  0.7 us (1%)
    pallas_call x1, Pallas kernels, march(): pl.pallas_call(functools.partial(march_kernel, depth - 1, n), out_shape=(...  32.1 us
    ppermute x4, starting transfers between devices, shifted(): return lax.ppermute(value, axis, pairs)  11.3 us
    pallas_call x1, Pallas kernels, edges(): pl.pallas_call(edge_kernel, out_shape=(plane, plane), in_specs=[pl.BlockS...  4.81 us
    ppermute x4, waiting for transfers between devices, shifted(): return lax.ppermute(value, axis, pairs)  4.62 us
    unnamed x10, local copies, waits for them, and re-layouts  3.69 us
  transfers between devices with their start and end apart: 4, of which 1 were waited for; matrix products, arithmetic and copies ran while one was open for 0% of the time, Pallas kernels for 8%

profile of v14, /device:TPU:7, one launch (start us, length us, event | category | flops | bytes accessed | tf_op | source)
XLA Modules:
  0.0 58.0 jit_solution(12286787248373519585)
XLA Ops:
  0.6 0.8 %slice_bitcast_fusion = (f32[32,256]{1,0:T(8,128)S(1)}, f32[32,256]{1,0:T(8,128)S(1)}) fusion(f32[128,32,256]{2,1,0:T(8,128)} %dens_ref.3), kind=kLoop, calls=%fused_computation | loop fusion | bytes 131072 | tf_op jit(solution)/shard_map/squeeze | solution.py:277
  1.4 4.1 %collective-permute-start = (f32[32,256]{1,0:T(8,128)S(1)}, f32[32,256]{1,0:T(8,128)S(1)}, u32[]{:S(2)}, u32[]{:S(2)}) collective-permute-start(f32[32,256]{1,0:T(8,128)S(1)} %get-tuple-element.7), channel_id=1, source_target_pairs={{0,16},{16,32},{32,48},{48,64},{64,80},{80,96},{96,112},{112,128},... | collective-permute-start | bytes 98312 | tf_op jit(solution)/shard_map/ppermute | solution.py:271
  5.5 1.9 %collective-permute-start.1 = (f32[32,256]{1,0:T(8,128)S(1)}, f32[32,256]{1,0:T(8,128)S(1)}, u32[]{:S(2)}, u32[]{:S(2)}) collective-permute-start(f32[32,256]{1,0:T(8,128)S(1)} %get-tuple-element.6), channel_id=1, source_target_pairs={{16,0},{32,16},{48,32},{64,48},{80,64},{96,80},{112,96},{128,112},... | collective-permute-start | bytes 98312 | tf_op jit(solution)/shard_map/ppermute | solution.py:271
  7.4 4.8 %shard_map.41 = (f32[32,128]{1,0:T(8,128)}, f32[32,128]{1,0:T(8,128)}) custom-call(f32[128,32,256]{2,1,0:T(8,128)} %dens_ref.3), custom_call_target="tpu_custom_call" | custom-call | tf_op jit(solution)/shard_map/pallas_call | solution.py:258
  12.3 3.1 %collective-permute-start.2 = (f32[32,128]{1,0:T(8,128)}, f32[32,128]{1,0:T(8,128)S(1)}, u32[]{:S(2)}, u32[]{:S(2)}) collective-permute-start(f32[32,128]{1,0:T(8,128)} %get-tuple-element.4), channel_id=1, source_target_pairs={{0,1},{1,2},{2,3},{3,4},{4,5},{5,6},{6,7},{7,8},{8,9},{9,10},{10,1... | collective-permute-start | bytes 49160 | tf_op jit(solution)/shard_map/ppermute | solution.py:271
  15.4 2.2 %collective-permute-start.3 = (f32[32,128]{1,0:T(8,128)}, f32[32,128]{1,0:T(8,128)S(1)}, u32[]{:S(2)}, u32[]{:S(2)}) collective-permute-start(f32[32,128]{1,0:T(8,128)} %get-tuple-element.5), channel_id=1, source_target_pairs={{1,0},{2,1},{3,2},{4,3},{5,4},{6,5},{7,6},{8,7},{9,8},{10,9},{11,1... | collective-permute-start | bytes 49160 | tf_op jit(solution)/shard_map/ppermute | solution.py:271
  17.5 0.0 collective-permute-done.2.left_ref
  17.5 0.0 copy-start.2
  17.6 4.6 %collective-permute-done.3.right_ref = f32[32,128]{1,0:T(8,128)S(1)} collective-permute-done((f32[32,128]{1,0:T(8,128)}, f32[32,128]{1,0:T(8,128)S(1)}, u32[]{:S(2)}, u32[]{:S(2)}) %collective-permute-start.3) | collective-permute-done | bytes 16416 | tf_op jit(solution)/shard_map/ppermute | solution.py:271
  22.2 0.0 copy-start.3
  22.2 0.0 collective-permute-done.front_ref
  22.2 0.0 copy-start
  22.2 0.0 collective-permute-done.1.back_ref
  22.2 0.0 copy-done.2
  22.2 0.6 copy-done.3
  22.8 0.0 copy-done
  22.8 0.0 copy-start.1
  22.8 0.6 %copy-done.1 = f32[32,256]{1,0:T(8,128)} copy-done((f32[32,256]{1,0:T(8,128)}, f32[32,256]{1,0:T(8,128)S(1)}, u32[]{:S(2)}) %copy-start.1) | copy-done | bytes 32792
  23.4 32.1 %shard_map.42 = (f32[3,1,256]{2,1,0:T(1,128)}, f32[1,256]{1,0:T(1,128)}) custom-call(f32[128,32,256]{2,1,0:T(8,128)} %dens_ref.3, f32[32,256]{1,0:T(8,128)} %copy-done, f32[32,256]{1,0:T(8,128)} %copy-done.1, f32[32,128]{1,0:T(8,128)} %copy-done.2, f32[32,128]{1,0:T(8,128)} %copy-done.3, f32[32,256]{1,0:T(8,128)} %absorb_ref.1), custom_call_target="tpu_custom_call" | custom-call | tf_op jit(solution)/shard_map/pallas_call | solution.py:221
  55.5 1.2 %copy.6 = f32[3,1,256]{2,1,0:T(1,128)} copy(f32[3,1,256]{2,1,0:T(1,128)} %get-tuple-element.10) | data formatting | bytes 6144
  56.8 1.2 %copy.7 = f32[1,256]{1,0:T(1,128)} copy(f32[1,256]{1,0:T(1,128)} %get-tuple-element.11) | data formatting | bytes 2048
Async XLA Ops:
  1.4 20.8 %collective-permute-start = (f32[32,256]{1,0:T(8,128)S(1)}, f32[32,256]{1,0:T(8,128)S(1)}, u32[]{:S(2)}, u32[]{:S(2)}) collective-permute-start(f32[32,256]{1,0:T(8,128)S(1)} %get-tuple-element.7), channel_id=1, source_target_pairs={{0,16},{16,32},{32,48},{48,64},{64,80},{80,96},{96,112},{112,128},... | collective-permute-start | bytes 98312 | tf_op jit(solution)/shard_map/ppermute | solution.py:271
  5.5 16.7 %collective-permute-start.1 = (f32[32,256]{1,0:T(8,128)S(1)}, f32[32,256]{1,0:T(8,128)S(1)}, u32[]{:S(2)}, u32[]{:S(2)}) collective-permute-start(f32[32,256]{1,0:T(8,128)S(1)} %get-tuple-element.6), channel_id=1, source_target_pairs={{16,0},{32,16},{48,32},{64,48},{80,64},{96,80},{112,96},{128,112},... | collective-permute-start | bytes 98312 | tf_op jit(solution)/shard_map/ppermute | solution.py:271
  12.3 5.3 %collective-permute-start.2 = (f32[32,128]{1,0:T(8,128)}, f32[32,128]{1,0:T(8,128)S(1)}, u32[]{:S(2)}, u32[]{:S(2)}) collective-permute-start(f32[32,128]{1,0:T(8,128)} %get-tuple-element.4), channel_id=1, source_target_pairs={{0,1},{1,2},{2,3},{3,4},{4,5},{5,6},{6,7},{7,8},{8,9},{9,10},{10,1... | collective-permute-start | bytes 49160 | tf_op jit(solution)/shard_map/ppermute | solution.py:271
  15.4 6.8 %collective-permute-start.3 = (f32[32,128]{1,0:T(8,128)}, f32[32,128]{1,0:T(8,128)S(1)}, u32[]{:S(2)}, u32[]{:S(2)}) collective-permute-start(f32[32,128]{1,0:T(8,128)} %get-tuple-element.5), channel_id=1, source_target_pairs={{1,0},{2,1},{3,2},{4,3},{5,4},{6,5},{7,6},{8,7},{9,8},{10,9},{11,1... | collective-permute-start | bytes 49160 | tf_op jit(solution)/shard_map/ppermute | solution.py:271
  17.5 4.6 %copy-start.2 = (f32[32,128]{1,0:T(8,128)}, f32[32,128]{1,0:T(8,128)S(1)}, u32[]{:S(2)}) copy-start(f32[32,128]{1,0:T(8,128)S(1)} %collective-permute-done.2.left_ref) | copy-start | bytes 49156
  22.2 0.6 %copy-start.3 = (f32[32,128]{1,0:T(8,128)}, f32[32,128]{1,0:T(8,128)S(1)}, u32[]{:S(2)}) copy-start(f32[32,128]{1,0:T(8,128)S(1)} %collective-permute-done.3.right_ref) | copy-start | bytes 49156
  22.2 0.6 %copy-start = (f32[32,256]{1,0:T(8,128)}, f32[32,256]{1,0:T(8,128)S(1)}, u32[]{:S(2)}) copy-start(f32[32,256]{1,0:T(8,128)S(1)} %collective-permute-done.front_ref) | copy-start | bytes 98308
  22.8 0.6 %copy-start.1 = (f32[32,256]{1,0:T(8,128)}, f32[32,256]{1,0:T(8,128)S(1)}, u32[]{:S(2)}) copy-start(f32[32,256]{1,0:T(8,128)S(1)} %collective-permute-done.1.back_ref) | copy-start | bytes 98308

commit v15 on v14

--- a/solution.py
+++ b/solution.py
@@ -242,42 +242,73 @@
     )(density, front, back, left, right, absorb)
 
 
-def edge_kernel(dens_ref, first_ref, last_ref):
+def halo_kernel(dens_ref, front_ref, back_ref, left_ref, right_ref,
+                first_col, last_col, lands, send_sems, recv_sems):
     depth, rows, cols = dens_ref.shape
+    nx, ny = lax.axis_size("gx"), lax.axis_size("gy")
+    gx, gy = lax.axis_index("gx"), lax.axis_index("gy")
+    ahead_x, behind_x = lax.rem(gx + 1, nx), lax.rem(gx + nx - 1, nx)
+    ahead_y, behind_y = lax.rem(gy + 1, ny), lax.rem(gy + ny - 1, ny)
+    barrier = pltpu.get_barrier_semaphore()
+    for peer in ((ahead_x, gy), (behind_x, gy), (gx, ahead_y), (gx, behind_y)):
+        pl.semaphore_signal(barrier, inc=1, device_id=peer, device_id_type=MESH_ID)
     for z in range(rows):
         low = jnp.transpose(dens_ref[:, z, 0:128])
         high = jnp.transpose(dens_ref[:, z, cols - 128:cols])
-        first_ref[z:z + 1, :] = low[0:1, :]
-        last_ref[z:z + 1, :] = high[127:128, :]
-
-
-def edges(density):
+        first_col[z:z + 1, :] = low[0:1, :]
+        last_col[z:z + 1, :] = high[127:128, :]
+    pl.semaphore_wait(barrier, 4)
+    front_land, back_land, left_land, right_land = lands
+    copies = [
+        (dens_ref.at[depth - 1], front_land, (ahead_x, gy)),
+        (dens_ref.at[0], back_land, (behind_x, gy)),
+        (last_col, left_land, (gx, ahead_y)),
+        (first_col, right_land, (gx, behind_y)),
+    ]
+    started = []
+    for i, (src, dst, peer) in enumerate(copies):
+        copy = pltpu.make_async_remote_copy(
+            src_ref=src, dst_ref=dst, send_sem=send_sems.at[i], recv_sem=recv_sems.at[i],
+            device_id=peer, device_id_type=MESH_ID,
+        )
+        copy.start()
+        started.append(copy)
+    for copy in started:
+        copy.wait()
+    front_ref[...] = jnp.where(gx == 0, 0.0, front_land[...])
+    back_ref[...] = jnp.where(gx == nx - 1, 0.0, back_land[...])
+    left_ref[...] = jnp.where(gy == 0, 0.0, left_land[...])
+    right_ref[...] = jnp.where(gy == ny - 1, 0.0, right_land[...])
+
+
+def halos(density):
     depth, rows, cols = density.shape
     vmem = pltpu.MemorySpace.VMEM
-    plane = jax.ShapeDtypeStruct((rows, depth), jnp.float32)
+    plane = jax.ShapeDtypeStruct((rows, cols), jnp.float32)
+    column = jax.ShapeDtypeStruct((rows, depth), jnp.float32)
     return pl.pallas_call(
-        edge_kernel,
-        out_shape=(plane, plane),
+        halo_kernel,
+        out_shape=(plane, plane, column, column),
         in_specs=[pl.BlockSpec(memory_space=vmem)],
-        out_specs=(pl.BlockSpec(memory_space=vmem), pl.BlockSpec(memory_space=vmem)),
+        out_specs=tuple(pl.BlockSpec(memory_space=vmem) for _ in range(4)),
+        scratch_shapes=[
+            pltpu.VMEM((rows, depth), jnp.float32),
+            pltpu.VMEM((rows, depth), jnp.float32),
+            (
+                pltpu.VMEM((rows, cols), jnp.float32),
+                pltpu.VMEM((rows, cols), jnp.float32),
+                pltpu.VMEM((rows, depth), jnp.float32),
+                pltpu.VMEM((rows, depth), jnp.float32),
+            ),
+            pltpu.SemaphoreType.DMA((4,)),
+            pltpu.SemaphoreType.DMA((4,)),
+        ],
+        compiler_params=pltpu.CompilerParams(collective_id=1, has_side_effects=True),
     )(density)
 
 
-def shifted(value, axis, forward):
-    size = lax.axis_size(axis)
-    pairs = [(i, i + 1) for i in range(size - 1)]
-    if not forward:
-        pairs = [(j, i) for i, j in pairs]
-    return lax.ppermute(value, axis, pairs)
-
-
 def local(density, absorb):
-    depth, nz, cols = density.shape
-    front = shifted(density[depth - 1], "gx", True)
-    back = shifted(density[0], "gx", False)
-    first_col, last_col = edges(density)
-    left = shifted(last_col, "gy", True)
-    right = shifted(first_col, "gy", False)
+    front, back, left, right = halos(density)
     return march(density, front, back, left, right, absorb, lax.axis_size("gx"))
 
 

time: 58.4 us -> 47.3 us (0.81)
  the two profiles are of different devices: /device:TPU:7 before, /device:TPU:1 now
where the time goes in v15:
time: 47.3 us; the launch traced here: 47.1 us
  Pallas kernels  43.9 us (93%)
  local copies, waits for them, and re-layouts  2.48 us (5%)
  between operations  0.65 us (1%)
    pallas_call x1, Pallas kernels, march(): pl.pallas_call(functools.partial(march_kernel, depth - 1, n), out_shape=(...  29.2 us
    pallas_call x1, Pallas kernels, halos(): pl.pallas_call(halo_kernel, out_shape=(plane, plane, column, column), in_...  14.7 us
    unnamed x2, local copies, waits for them, and re-layouts  2.48 us

profile of v15, /device:TPU:1, one launch (start us, length us, event | category | flops | bytes accessed | tf_op | source)
XLA Modules:
  0.0 47.1 jit_solution(2998707038783379722)
XLA Ops:
  0.6 14.7 %shard_map.41 = (f32[32,256]{1,0:T(8,128)}, f32[32,256]{1,0:T(8,128)}, f32[32,128]{1,0:T(8,128)}, f32[32,128]{1,0:T(8,128)}) custom-call(f32[128,32,256]{2,1,0:T(8,128)} %dens_ref.3), custom_call_target="tpu_custom_call" | custom-call | tf_op jit(solution)/shard_map/pallas_call | solution.py:289
  15.4 29.2 %shard_map.42 = (f32[3,1,256]{2,1,0:T(1,128)}, f32[1,256]{1,0:T(1,128)}) custom-call(f32[128,32,256]{2,1,0:T(8,128)} %dens_ref.3, f32[32,256]{1,0:T(8,128)} %get-tuple-element.6.front_ref, f32[32,256]{1,0:T(8,128)} %get-tuple-element.7.back_ref, f32[32,128]{1,0:T(8,128)} %get-tuple-element.8.left_ref, f32[32,128]{1,0:T(8,128)} %get-tuple-element.9.right_ref, ...), custom_call_target="tpu_custom_call" | custom-call | tf_op jit(solution)/shard_map/pallas_call | solution.py:221
  44.6 1.3 %copy.6 = f32[3,1,256]{2,1,0:T(1,128)} copy(f32[3,1,256]{2,1,0:T(1,128)} %get-tuple-element.12) | data formatting | bytes 6144
  45.8 1.2 %copy.7 = f32[1,256]{1,0:T(1,128)} copy(f32[1,256]{1,0:T(1,128)} %get-tuple-element.13) | data formatting | bytes 2048

commit v16 on v15

--- a/solution.py
+++ b/solution.py
@@ -16,7 +16,7 @@
 
 
 def march_kernel(last, n, dens_ref, front_ref, back_ref, left_ref, right_ref, absorb_ref,
-                 colour_ref, transmit_ref, out_ref, part, mixed, recv_pair, recv,
+                 colour_ref, out_ref, part, mixed, recv_pair, recv,
                  send_pair, got_pair, send_sems, recv_sems, local_sem):
     rows, cols = dens_ref.shape[1], dens_ref.shape[2]
     shape = (rows, 128)
@@ -112,7 +112,7 @@
                 r = ((z % share) * 4 + k) * halves + h
                 part[slot, r:r + 1, :] = out_ref[k, z:z + 1, h * 128:(h + 1) * 128]
     exchange_and_combine(n, share, halves, me, col, barrier, part, mixed, recv_pair, recv,
-                         sems, colour_ref, transmit_ref)
+                         sems, colour_ref)
 
 
 def merge(front, back, share, halves):
@@ -132,7 +132,7 @@
 
 
 def exchange_and_combine(n, share, halves, me, col, barrier, part, mixed, recv_pair, recv,
-                         sems, colour_ref, transmit_ref):
+                         sems, colour_ref):
     pairs = n // 2
     parity = lax.rem(me, 2)
     partner = me + 1 - 2 * parity
@@ -188,6 +188,11 @@
         return carry
 
     lax.fori_loop(1, pairs, finish, 0)
+    colour_ref[...] = recv[...]
+
+
+def finish_kernel(share, halves, recv_ref, colour_ref, transmit_ref):
+    pairs = recv_ref.shape[0]
     cols = colour_ref.shape[-1]
     zero = jnp.zeros((share * halves, 128), jnp.float32)
 
@@ -197,7 +202,7 @@
 
     def accumulate(d, carry):
         front, c0, c1, c2 = carry
-        block = recv[d]
+        block = recv_ref[d]
         seen = jnp.exp(-front)
         return (
             front + value(block, 3),
@@ -210,6 +215,19 @@
     for k, c in enumerate((c0, c1, c2)):
         colour_ref[k] = c.reshape(share, cols)
     transmit_ref[...] = jnp.exp(-front).reshape(share, cols)
+
+
+def finish(gathered, share, cols):
+    vmem = pltpu.MemorySpace.VMEM
+    return pl.pallas_call(
+        functools.partial(finish_kernel, share, cols // 128),
+        out_shape=(
+            jax.ShapeDtypeStruct((3, share, cols), jnp.float32),
+            jax.ShapeDtypeStruct((share, cols), jnp.float32),
+        ),
+        in_specs=[pl.BlockSpec(memory_space=vmem)],
+        out_specs=(pl.BlockSpec(memory_space=vmem), pl.BlockSpec(memory_space=vmem)),
+    )(gathered)
 
 
 def march(density, front, back, left, right, absorb, n):
@@ -220,12 +238,9 @@
     vmem = pltpu.MemorySpace.VMEM
     return pl.pallas_call(
         functools.partial(march_kernel, depth - 1, n),
-        out_shape=(
-            jax.ShapeDtypeStruct((3, share, cols), jnp.float32),
-            jax.ShapeDtypeStruct((share, cols), jnp.float32),
-        ),
+        out_shape=jax.ShapeDtypeStruct(half_tiles, jnp.float32),
         in_specs=[pl.BlockSpec(memory_space=vmem)] * 6,
-        out_specs=(pl.BlockSpec(memory_space=vmem), pl.BlockSpec(memory_space=vmem)),
+        out_specs=pl.BlockSpec(memory_space=vmem),
         scratch_shapes=[
             pltpu.VMEM((4, rows, cols), jnp.float32),
             pltpu.VMEM(tiles, jnp.float32),
@@ -309,7 +324,9 @@
 
 def local(density, absorb):
     front, back, left, right = halos(density)
-    return march(density, front, back, left, right, absorb, lax.axis_size("gx"))
+    n = lax.axis_size("gx")
+    gathered = march(density, front, back, left, right, absorb, n)
+    return finish(gathered, density.shape[1] // n, density.shape[2])
 
 
 def solution(mesh):

time: 47.3 us -> 46.3 us (0.979)
  local copies, waits for them, and re-layouts: 2.48 us -> 0 us
  Pallas kernels: 43.9 us -> 45.4 us
    unnamed x2 -> x0, local copies, waits for them, and re-layouts: 2.48 us -> none
    pallas_call x1 -> x2, Pallas kernels: 29.2 us -> 30.7 us  [the longest x1 29 us: march(): pl.pallas_call(functools.partial(march_kernel, depth - 1, n), out_shape=j...]
where the time goes in v16:
time: 46.3 us; the launch traced here: 46 us
  Pallas kernels  45.4 us (98%)
  between operations  0.64 us (1%)
    pallas_call x1, Pallas kernels, march(): pl.pallas_call(functools.partial(march_kernel, depth - 1, n), out_shape=j...  29 us
    pallas_call x1, Pallas kernels, halos(): pl.pallas_call(halo_kernel, out_shape=(plane, plane, column, column), in_...  14.7 us
    pallas_call x1, Pallas kernels, finish(): pl.pallas_call(functools.partial(finish_kernel, share, cols // 128), out_...  1.61 us

profile of v16, /device:TPU:1, one launch (start us, length us, event | category | flops | bytes accessed | tf_op | source)
XLA Modules:
  0.0 46.0 jit_solution(10004131889460099302)
XLA Ops:
  0.6 14.7 %shard_map.41 = (f32[32,256]{1,0:T(8,128)}, f32[32,256]{1,0:T(8,128)}, f32[32,128]{1,0:T(8,128)}, f32[32,128]{1,0:T(8,128)}) custom-call(f32[128,32,256]{2,1,0:T(8,128)} %dens_ref.3), custom_call_target="tpu_custom_call" | custom-call | tf_op jit(solution)/shard_map/pallas_call | solution.py:304
  15.4 29.0 %shard_map.42.recv_ref = f32[16,8,128]{2,1,0:T(8,128)} custom-call(f32[128,32,256]{2,1,0:T(8,128)} %dens_ref.3, f32[32,256]{1,0:T(8,128)} %get-tuple-element.6.front_ref, f32[32,256]{1,0:T(8,128)} %get-tuple-element.7.back_ref, f32[32,128]{1,0:T(8,128)} %get-tuple-element.8.left_ref, f32[32,128]{1,0:T(8,128)} %get-tuple-element.9.right_ref, f32[32,256]{1,0:T(8,128)} %absorb_ref.1), custom_call_target="tpu_custom_call" | custom-call | tf_op jit(solution)/shard_map/pallas_call | solution.py:239
  44.4 1.6 %shard_map.43 = (f32[3,1,256]{2,1,0:T(1,128)}, f32[1,256]{1,0:T(1,128)}) custom-call(f32[16,8,128]{2,1,0:T(8,128)} %shard_map.42.recv_ref), custom_call_target="tpu_custom_call" | custom-call | tf_op jit(solution)/shard_map/pallas_call | solution.py:222

commit v17 on v16

--- a/solution.py
+++ b/solution.py
@@ -257,8 +257,8 @@
     )(density, front, back, left, right, absorb)
 
 
-def halo_kernel(dens_ref, front_ref, back_ref, left_ref, right_ref,
-                first_col, last_col, lands, send_sems, recv_sems):
+def halo_kernel(dens_hbm, front_ref, back_ref, left_ref, right_ref,
+                dens_ref, first_col, last_col, lands, send_sems, recv_sems, load_sem):
     depth, rows, cols = dens_ref.shape
     nx, ny = lax.axis_size("gx"), lax.axis_size("gy")
     gx, gy = lax.axis_index("gx"), lax.axis_index("gy")
@@ -267,6 +267,9 @@
     barrier = pltpu.get_barrier_semaphore()
     for peer in ((ahead_x, gy), (behind_x, gy), (gx, ahead_y), (gx, behind_y)):
         pl.semaphore_signal(barrier, inc=1, device_id=peer, device_id_type=MESH_ID)
+    load = pltpu.make_async_copy(dens_hbm, dens_ref, load_sem)
+    load.start()
+    load.wait()
     for z in range(rows):
         low = jnp.transpose(dens_ref[:, z, 0:128])
         high = jnp.transpose(dens_ref[:, z, cols - 128:cols])
@@ -275,8 +278,8 @@
     pl.semaphore_wait(barrier, 4)
     front_land, back_land, left_land, right_land = lands
     copies = [
-        (dens_ref.at[depth - 1], front_land, (ahead_x, gy)),
-        (dens_ref.at[0], back_land, (behind_x, gy)),
+        (dens_hbm.at[depth - 1], front_land, (ahead_x, gy)),
+        (dens_hbm.at[0], back_land, (behind_x, gy)),
         (last_col, left_land, (gx, ahead_y)),
         (first_col, right_land, (gx, behind_y)),
     ]
@@ -304,9 +307,10 @@
     return pl.pallas_call(
         halo_kernel,
         out_shape=(plane, plane, column, column),
-        in_specs=[pl.BlockSpec(memory_space=vmem)],
+        in_specs=[pl.BlockSpec(memory_space=pl.ANY)],
         out_specs=tuple(pl.BlockSpec(memory_space=vmem) for _ in range(4)),
         scratch_shapes=[
+            pltpu.VMEM((depth, rows, cols), jnp.float32),
             pltpu.VMEM((rows, depth), jnp.float32),
             pltpu.VMEM((rows, depth), jnp.float32),
             (
@@ -317,6 +321,7 @@
             ),
             pltpu.SemaphoreType.DMA((4,)),
             pltpu.SemaphoreType.DMA((4,)),
+            pltpu.SemaphoreType.DMA,
         ],
         compiler_params=pltpu.CompilerParams(collective_id=1, has_side_effects=True),
     )(density)

time: 46.3 us -> 46.2 us (level)
    pallas_call x1, Pallas kernels: 14.7 us -> 13.4 us  [halos(): pl.pallas_call(halo_kernel, out_shape=(plane, plane, column, column), in_...]
    pallas_call x1, Pallas kernels: 29 us -> 30.3 us  [march(): pl.pallas_call(functools.partial(march_kernel, depth - 1, n), out_shape=j...]
where the time goes in v17:
time: 46.2 us; the launch traced here: 46 us
  Pallas kernels  45.3 us (98%)
  between operations  0.64 us (1%)
    pallas_call x1, Pallas kernels, march(): pl.pallas_call(functools.partial(march_kernel, depth - 1, n), out_shape=j...  30.3 us
    pallas_call x1, Pallas kernels, halos(): pl.pallas_call(halo_kernel, out_shape=(plane, plane, column, column), in_...  13.4 us
    pallas_call x1, Pallas kernels, finish(): pl.pallas_call(functools.partial(finish_kernel, share, cols // 128), out_...  1.61 us

profile of v17, /device:TPU:1, one launch (start us, length us, event | category | flops | bytes accessed | tf_op | source)
XLA Modules:
  0.0 46.0 jit_solution(9707371022048121089)
XLA Ops:
  0.6 13.4 %shard_map.41 = (f32[32,256]{1,0:T(8,128)}, f32[32,256]{1,0:T(8,128)}, f32[32,128]{1,0:T(8,128)}, f32[32,128]{1,0:T(8,128)}) custom-call(f32[128,32,256]{2,1,0:T(8,128)} %dens_ref.1), custom_call_target="tpu_custom_call" | custom-call | tf_op jit(solution)/shard_map/pallas_call | solution.py:307
  14.1 30.3 %shard_map.42.recv_ref = f32[16,8,128]{2,1,0:T(8,128)} custom-call(f32[128,32,256]{2,1,0:T(8,128)} %dens_ref.1, f32[32,256]{1,0:T(8,128)} %get-tuple-element.6.front_ref, f32[32,256]{1,0:T(8,128)} %get-tuple-element.7.back_ref, f32[32,128]{1,0:T(8,128)} %get-tuple-element.8.left_ref, f32[32,128]{1,0:T(8,128)} %get-tuple-element.9.right_ref, f32[32,256]{1,0:T(8,128)} %absorb_ref.1), custom_call_target="tpu_custom_call" | custom-call | tf_op jit(solution)/shard_map/pallas_call | solution.py:239
  44.4 1.6 %shard_map.43 = (f32[3,1,256]{2,1,0:T(1,128)}, f32[1,256]{1,0:T(1,128)}) custom-call(f32[16,8,128]{2,1,0:T(8,128)} %shard_map.42.recv_ref), custom_call_target="tpu_custom_call" | custom-call | tf_op jit(solution)/shard_map/pallas_call | solution.py:222

commit v18 on v16

--- a/solution.py
+++ b/solution.py
@@ -15,9 +15,9 @@
 MESH_ID = pl.DeviceIdType.MESH
 
 
-def march_kernel(last, n, dens_ref, front_ref, back_ref, left_ref, right_ref, absorb_ref,
+def march_kernel(last, n, dens_hbm, front_ref, back_ref, left_ref, right_ref, absorb_ref,
                  colour_ref, out_ref, part, mixed, recv_pair, recv,
-                 send_pair, got_pair, send_sems, recv_sems, local_sem):
+                 send_pair, got_pair, send_sems, recv_sems, local_sem, dens_ref, load_sems):
     rows, cols = dens_ref.shape[1], dens_ref.shape[2]
     shape = (rows, 128)
     lane = lax.broadcasted_iota(jnp.int32, shape, 1)
@@ -41,6 +41,16 @@
 
     pl.semaphore_signal(barrier, inc=1, device_id=(me + 1 - 2 * parity, col), device_id_type=MESH_ID)
     lax.fori_loop(1, pairs, greet, 0)
+    pieces = load_sems.shape[0]
+    piece = (last + 1) // pieces
+    loads = [
+        pltpu.make_async_copy(
+            dens_hbm.at[pl.ds(c * piece, piece)], dens_ref.at[pl.ds(c * piece, piece)], load_sems.at[c]
+        )
+        for c in range(pieces)
+    ]
+    for load in loads:
+        load.start()
     for h in range(halves):
         lanes = slice(h * 128, (h + 1) * 128)
         left_lanes = slice((h - 1) * 128, h * 128) if h > 0 else None
@@ -95,9 +105,16 @@
 
         zero = jnp.zeros(shape, jnp.float32)
         one = jnp.ones(shape, jnp.float32)
-        _, total, t0, t1, t2, softsum = lax.fori_loop(
-            0, last + 1, step, (one, zero, zero, zero, zero, zero), unroll=16
-        )
+        carry = (one, zero, zero, zero, zero, zero)
+        if h == 0:
+            loads[0].wait()
+            for c in range(pieces):
+                if c + 1 < pieces:
+                    loads[c + 1].wait()
+                carry = lax.fori_loop(c * piece, (c + 1) * piece, step, carry, unroll=min(16, piece))
+        else:
+            carry = lax.fori_loop(0, last + 1, step, carry, unroll=16)
+        _, total, t0, t1, t2, softsum = carry
         for k, value in enumerate((t0, t1, t2)):
             out_ref[k, :, lanes] = 0.5 * (total + value)
         out_ref[3, :, lanes] = absorb * softsum
@@ -239,7 +256,7 @@
     return pl.pallas_call(
         functools.partial(march_kernel, depth - 1, n),
         out_shape=jax.ShapeDtypeStruct(half_tiles, jnp.float32),
-        in_specs=[pl.BlockSpec(memory_space=vmem)] * 6,
+        in_specs=[pl.BlockSpec(memory_space=pl.ANY)] + [pl.BlockSpec(memory_space=vmem)] * 5,
         out_specs=pl.BlockSpec(memory_space=vmem),
         scratch_shapes=[
             pltpu.VMEM((4, rows, cols), jnp.float32),
@@ -252,6 +269,8 @@
             pltpu.SemaphoreType.DMA((n // 2,)),
             pltpu.SemaphoreType.DMA((n // 2,)),
             pltpu.SemaphoreType.DMA,
+            pltpu.VMEM((depth, rows, cols), jnp.float32),
+            pltpu.SemaphoreType.DMA((8 if depth % 8 == 0 else 1,)),
         ],
         compiler_params=pltpu.CompilerParams(collective_id=0, has_side_effects=True),
     )(density, front, back, left, right, absorb)

time: 46.3 us -> 45.7 us (0.987)
  Pallas kernels: 45.4 us -> 44.7 us
    pallas_call x1, Pallas kernels: 29 us -> 28.4 us  [march(): pl.pallas_call(functools.partial(march_kernel, depth - 1, n), out_shape=j...]
where the time goes in v18:
time: 45.7 us; the launch traced here: 45.4 us
  Pallas kernels  44.7 us (98%)
  between operations  0.64 us (1%)
    pallas_call x1, Pallas kernels, march(): pl.pallas_call(functools.partial(march_kernel, depth - 1, n), out_shape=j...  28.4 us
    pallas_call x1, Pallas kernels, halos(): pl.pallas_call(halo_kernel, out_shape=(plane, plane, column, column), in_...  14.7 us
    pallas_call x1, Pallas kernels, finish(): pl.pallas_call(functools.partial(finish_kernel, share, cols // 128), out_...  1.61 us

profile of v18, /device:TPU:1, one launch (start us, length us, event | category | flops | bytes accessed | tf_op | source)
XLA Modules:
  0.0 45.4 jit_solution(17930179278326276315)
XLA Ops:
  0.6 14.7 %shard_map.41 = (f32[32,256]{1,0:T(8,128)}, f32[32,256]{1,0:T(8,128)}, f32[32,128]{1,0:T(8,128)}, f32[32,128]{1,0:T(8,128)}) custom-call(f32[128,32,256]{2,1,0:T(8,128)} %dens_hbm.1), custom_call_target="tpu_custom_call" | custom-call | tf_op jit(solution)/shard_map/pallas_call | solution.py:323
  15.4 28.4 %shard_map.42.recv_ref = f32[16,8,128]{2,1,0:T(8,128)} custom-call(f32[128,32,256]{2,1,0:T(8,128)} %dens_hbm.1, f32[32,256]{1,0:T(8,128)} %get-tuple-element.6.front_ref, f32[32,256]{1,0:T(8,128)} %get-tuple-element.7.back_ref, f32[32,128]{1,0:T(8,128)} %get-tuple-element.8.left_ref, f32[32,128]{1,0:T(8,128)} %get-tuple-element.9.right_ref, f32[32,256]{1,0:T(8,128)} %absorb_ref.1), custom_call_target="tpu_custom_call" | custom-call | tf_op jit(solution)/shard_map/pallas_call | solution.py:256
  43.8 1.6 %shard_map.43 = (f32[3,1,256]{2,1,0:T(1,128)}, f32[1,256]{1,0:T(1,128)}) custom-call(f32[16,8,128]{2,1,0:T(8,128)} %shard_map.42.recv_ref), custom_call_target="tpu_custom_call" | custom-call | tf_op jit(solution)/shard_map/pallas_call | solution.py:239

commit v19 on v18

--- a/solution.py
+++ b/solution.py
@@ -276,8 +276,8 @@
     )(density, front, back, left, right, absorb)
 
 
-def halo_kernel(dens_ref, front_ref, back_ref, left_ref, right_ref,
-                first_col, last_col, lands, send_sems, recv_sems):
+def halo_kernel(dens_hbm, front_ref, back_ref, left_ref, right_ref,
+                dens_ref, first_col, last_col, lands, send_sems, recv_sems, load_sems):
     depth, rows, cols = dens_ref.shape
     nx, ny = lax.axis_size("gx"), lax.axis_size("gy")
     gx, gy = lax.axis_index("gx"), lax.axis_index("gy")
@@ -286,7 +286,18 @@
     barrier = pltpu.get_barrier_semaphore()
     for peer in ((ahead_x, gy), (behind_x, gy), (gx, ahead_y), (gx, behind_y)):
         pl.semaphore_signal(barrier, inc=1, device_id=peer, device_id_type=MESH_ID)
+    group = rows // load_sems.shape[0]
+    loads = [
+        pltpu.make_async_copy(
+            dens_hbm.at[:, pl.ds(g * group, group)], dens_ref.at[:, pl.ds(g * group, group)], load_sems.at[g]
+        )
+        for g in range(load_sems.shape[0])
+    ]
+    for load in loads:
+        load.start()
     for z in range(rows):
+        if z % group == 0:
+            loads[z // group].wait()
         low = jnp.transpose(dens_ref[:, z, 0:128])
         high = jnp.transpose(dens_ref[:, z, cols - 128:cols])
         first_col[z:z + 1, :] = low[0:1, :]
@@ -294,8 +305,8 @@
     pl.semaphore_wait(barrier, 4)
     front_land, back_land, left_land, right_land = lands
     copies = [
-        (dens_ref.at[depth - 1], front_land, (ahead_x, gy)),
-        (dens_ref.at[0], back_land, (behind_x, gy)),
+        (dens_hbm.at[depth - 1], front_land, (ahead_x, gy)),
+        (dens_hbm.at[0], back_land, (behind_x, gy)),
         (last_col, left_land, (gx, ahead_y)),
         (first_col, right_land, (gx, behind_y)),
     ]
@@ -323,9 +334,10 @@
     return pl.pallas_call(
         halo_kernel,
         out_shape=(plane, plane, column, column),
-        in_specs=[pl.BlockSpec(memory_space=vmem)],
+        in_specs=[pl.BlockSpec(memory_space=pl.ANY)],
         out_specs=tuple(pl.BlockSpec(memory_space=vmem) for _ in range(4)),
         scratch_shapes=[
+            pltpu.VMEM((depth, rows, cols), jnp.float32),
             pltpu.VMEM((rows, depth), jnp.float32),
             pltpu.VMEM((rows, depth), jnp.float32),
             (
@@ -336,6 +348,7 @@
             ),
             pltpu.SemaphoreType.DMA((4,)),
             pltpu.SemaphoreType.DMA((4,)),
+            pltpu.SemaphoreType.DMA((rows // 8 if rows % 8 == 0 else 1,)),
         ],
         compiler_params=pltpu.CompilerParams(collective_id=1, has_side_effects=True),
     )(density)

time: 45.7 us -> 45.1 us (0.987)
  Pallas kernels: 44.7 us -> 44.2 us
    pallas_call x1, Pallas kernels: 14.7 us -> 12.8 us  [halos(): pl.pallas_call(halo_kernel, out_shape=(plane, plane, column, column), in_...]
    pallas_call x1, Pallas kernels: 28.4 us -> 29.7 us  [march(): pl.pallas_call(functools.partial(march_kernel, depth - 1, n), out_shape=j...]
where the time goes in v19:
time: 45.1 us; the launch traced here: 44.8 us
  Pallas kernels  44.2 us (98%)
  between operations  0.64 us (1%)
    pallas_call x1, Pallas kernels, march(): pl.pallas_call(functools.partial(march_kernel, depth - 1, n), out_shape=j...  29.7 us
    pallas_call x1, Pallas kernels, halos(): pl.pallas_call(halo_kernel, out_shape=(plane, plane, column, column), in_...  12.8 us
    pallas_call x1, Pallas kernels, finish(): pl.pallas_call(functools.partial(finish_kernel, share, cols // 128), out_...  1.61 us

profile of v19, /device:TPU:1, one launch (start us, length us, event | category | flops | bytes accessed | tf_op | source)
XLA Modules:
  0.0 44.8 jit_solution(14617591466105162636)
XLA Ops:
  0.6 12.8 %shard_map.41 = (f32[32,256]{1,0:T(8,128)}, f32[32,256]{1,0:T(8,128)}, f32[32,128]{1,0:T(8,128)}, f32[32,128]{1,0:T(8,128)}) custom-call(f32[128,32,256]{2,1,0:T(8,128)} %dens_hbm.3), custom_call_target="tpu_custom_call" | custom-call | tf_op jit(solution)/shard_map/pallas_call | solution.py:334
  13.4 29.7 %shard_map.42.recv_ref = f32[16,8,128]{2,1,0:T(8,128)} custom-call(f32[128,32,256]{2,1,0:T(8,128)} %dens_hbm.3, f32[32,256]{1,0:T(8,128)} %get-tuple-element.6.front_ref, f32[32,256]{1,0:T(8,128)} %get-tuple-element.7.back_ref, f32[32,128]{1,0:T(8,128)} %get-tuple-element.8.left_ref, f32[32,128]{1,0:T(8,128)} %get-tuple-element.9.right_ref, f32[32,256]{1,0:T(8,128)} %absorb_ref.1), custom_call_target="tpu_custom_call" | custom-call | tf_op jit(solution)/shard_map/pallas_call | solution.py:256
  43.2 1.6 %shard_map.43 = (f32[3,1,256]{2,1,0:T(1,128)}, f32[1,256]{1,0:T(1,128)}) custom-call(f32[16,8,128]{2,1,0:T(8,128)} %shard_map.42.recv_ref), custom_call_target="tpu_custom_call" | custom-call | tf_op jit(solution)/shard_map/pallas_call | solution.py:239

commit v20 on v19

--- a/solution.py
+++ b/solution.py
@@ -111,9 +111,9 @@
             for c in range(pieces):
                 if c + 1 < pieces:
                     loads[c + 1].wait()
-                carry = lax.fori_loop(c * piece, (c + 1) * piece, step, carry, unroll=min(16, piece))
+                carry = lax.fori_loop(c * piece, (c + 1) * piece, step, carry, unroll=piece)
         else:
-            carry = lax.fori_loop(0, last + 1, step, carry, unroll=16)
+            carry = lax.fori_loop(0, last + 1, step, carry, unroll=32)
         _, total, t0, t1, t2, softsum = carry
         for k, value in enumerate((t0, t1, t2)):
             out_ref[k, :, lanes] = 0.5 * (total + value)

time: 45.1 us -> 45 us (level)
  no operation moved by 1% of the time
where the time goes in v20:
time: 45 us; the launch traced here: 44.8 us
  Pallas kernels  44.1 us (98%)
  between operations  0.64 us (1%)
    pallas_call x1, Pallas kernels, march(): pl.pallas_call(functools.partial(march_kernel, depth - 1, n), out_shape=j...  29.7 us
    pallas_call x1, Pallas kernels, halos(): pl.pallas_call(halo_kernel, out_shape=(plane, plane, column, column), in_...  12.8 us
    pallas_call x1, Pallas kernels, finish(): pl.pallas_call(functools.partial(finish_kernel, share, cols // 128), out_...  1.61 us

profile of v20, /device:TPU:1, one launch (start us, length us, event | category | flops | bytes accessed | tf_op | source)
XLA Modules:
  0.0 44.8 jit_solution(13247571595456808668)
XLA Ops:
  0.6 12.8 %shard_map.41 = (f32[32,256]{1,0:T(8,128)}, f32[32,256]{1,0:T(8,128)}, f32[32,128]{1,0:T(8,128)}, f32[32,128]{1,0:T(8,128)}) custom-call(f32[128,32,256]{2,1,0:T(8,128)} %dens_hbm.3), custom_call_target="tpu_custom_call" | custom-call | tf_op jit(solution)/shard_map/pallas_call | solution.py:334
  13.4 29.7 %shard_map.42.recv_ref = f32[16,8,128]{2,1,0:T(8,128)} custom-call(f32[128,32,256]{2,1,0:T(8,128)} %dens_hbm.3, f32[32,256]{1,0:T(8,128)} %get-tuple-element.6.front_ref, f32[32,256]{1,0:T(8,128)} %get-tuple-element.7.back_ref, f32[32,128]{1,0:T(8,128)} %get-tuple-element.8.left_ref, f32[32,128]{1,0:T(8,128)} %get-tuple-element.9.right_ref, f32[32,256]{1,0:T(8,128)} %absorb_ref.1), custom_call_target="tpu_custom_call" | custom-call | tf_op jit(solution)/shard_map/pallas_call | solution.py:256
  43.1 1.6 %shard_map.43 = (f32[3,1,256]{2,1,0:T(1,128)}, f32[1,256]{1,0:T(1,128)}) custom-call(f32[16,8,128]{2,1,0:T(8,128)} %shard_map.42.recv_ref), custom_call_target="tpu_custom_call" | custom-call | tf_op jit(solution)/shard_map/pallas_call | solution.py:239

commit v21 on v19

--- a/solution.py
+++ b/solution.py
@@ -177,7 +177,7 @@
         mixed[j] = merge(front, back, share, halves)
         return carry
 
-    lax.fori_loop(0, pairs, combine_pair, 0)
+    lax.fori_loop(0, pairs, combine_pair, 0, unroll=True)
 
     def link(j, slot):
         return pltpu.make_async_remote_copy(
@@ -228,7 +228,7 @@
             c2 + value(block, 2) * seen,
         )
 
-    front, c0, c1, c2 = lax.fori_loop(0, pairs, accumulate, (zero, zero, zero, zero))
+    front, c0, c1, c2 = lax.fori_loop(0, pairs, accumulate, (zero, zero, zero, zero), unroll=True)
     for k, c in enumerate((c0, c1, c2)):
         colour_ref[k] = c.reshape(share, cols)
     transmit_ref[...] = jnp.exp(-front).reshape(share, cols)

time: 45.1 us -> 44.7 us (level)
  no operation moved by 1% of the time
where the time goes in v21:
time: 44.7 us; the launch traced here: 44.4 us
  Pallas kernels  43.8 us (98%)
  between operations  0.64 us (1%)
    pallas_call x1, Pallas kernels, march(): pl.pallas_call(functools.partial(march_kernel, depth - 1, n), out_shape=j...  29.5 us
    pallas_call x1, Pallas kernels, halos(): pl.pallas_call(halo_kernel, out_shape=(plane, plane, column, column), in_...  12.8 us
    pallas_call x1, Pallas kernels, finish(): pl.pallas_call(functools.partial(finish_kernel, share, cols // 128), out_...  1.46 us

profile of v21, /device:TPU:1, one launch (start us, length us, event | category | flops | bytes accessed | tf_op | source)
XLA Modules:
  0.0 44.4 jit_solution(15259485790456414846)
XLA Ops:
  0.6 12.8 %shard_map.41 = (f32[32,256]{1,0:T(8,128)}, f32[32,256]{1,0:T(8,128)}, f32[32,128]{1,0:T(8,128)}, f32[32,128]{1,0:T(8,128)}) custom-call(f32[128,32,256]{2,1,0:T(8,128)} %dens_hbm.3), custom_call_target="tpu_custom_call" | custom-call | tf_op jit(solution)/shard_map/pallas_call | solution.py:334
  13.4 29.5 %shard_map.42.recv_ref = f32[16,8,128]{2,1,0:T(8,128)} custom-call(f32[128,32,256]{2,1,0:T(8,128)} %dens_hbm.3, f32[32,256]{1,0:T(8,128)} %get-tuple-element.6.front_ref, f32[32,256]{1,0:T(8,128)} %get-tuple-element.7.back_ref, f32[32,128]{1,0:T(8,128)} %get-tuple-element.8.left_ref, f32[32,128]{1,0:T(8,128)} %get-tuple-element.9.right_ref, f32[32,256]{1,0:T(8,128)} %absorb_ref.1), custom_call_target="tpu_custom_call" | custom-call | tf_op jit(solution)/shard_map/pallas_call | solution.py:256
  43.0 1.5 %shard_map.43 = (f32[3,1,256]{2,1,0:T(1,128)}, f32[1,256]{1,0:T(1,128)}) custom-call(f32[16,8,128]{2,1,0:T(8,128)} %shard_map.42.recv_ref), custom_call_target="tpu_custom_call" | custom-call | tf_op jit(solution)/shard_map/pallas_call | solution.py:239
